TPU v7x, 1024 devices: a whole 4x8x16 slice. The times are simulated.
1024 devices in a mesh: row: 64 (over y_lo, z, core), col: 16 (over y_hi, x).
Axes of the slice: x: 4, y: 8 (y_hi: 4, y_lo: 2; y = y_hi * 2 + y_lo), z: 16, core: 2. Of those that a mesh axis runs over, the one named last changes fastest.
Arguments:
- covariance: float32 [8192, 8192], P('row', 'col')
- lon_speed: float32 [8192], replicated, may hold values from 0.05 to 0.45
- lat_speed: float32 [8192], replicated, may hold values from 0.05 to 0.45
- lon_sign: int32 [8192], replicated, may hold values from 0 to 1
- lat_sign: int32 [8192], replicated, may hold values from 0 to 1
- measurement_site_position: int32 [256], replicated, may hold values from 0 to 8191, as said below
- obs_var: float32 [256], replicated, may hold values from 0.5 to 2
Outputs:
- analysis: float32 [8192, 8192], P('row', 'col')
Inputs may be any that keep to these rules, and one draw needn't show every extreme that they name: `measurement_site_position`: distinct cells.
All inputs are finite; a program needn't handle non-finite values.
Results may differ from a plain program's by a relative error of at most 0.00012.
Values sent between devices are 32-bit elements; how exact they have to be, the bound alone decides.
No kernel may reach another device: no remote copies, remote signals or barrier semaphores. Data moves between devices by JAX's collectives and lax.ppermute only.
A program may use at most 32 MiB of HBM per device.

v0:
```python
import jax
import jax.numpy as jnp
from jax import lax
from jax.sharding import PartitionSpec as P

PARALLEL_STRIPS = 64
MERIDIAN_TOTAL = 128
STEPS = 3


def padded_2(cells, sides, width):
    for axis, dim in sides:
        count = lax.axis_size(axis)
        ends = count - 1
        head = lax.slice_in_dim(cells, 0, width, axis=dim)
        tail = lax.slice_in_dim(cells, cells.shape[dim] - width, cells.shape[dim], axis=dim)
        cells = jnp.concatenate(
            [
                lax.ppermute(tail, axis, [(i, (i + 1) % count) for i in range(ends)]),
                cells,
                lax.ppermute(head, axis, [((i + 1) % count, i) for i in range(ends)]),
            ],
            axis=dim,
        )
    return cells


def from_everyone(shard, axis):
    copies = jnp.broadcast_to(shard, (lax.axis_size(axis), *shard.shape))
    return lax.all_to_all(copies, axis, split_axis=0, concat_axis=0, tiled=True)


def over_copies(shard, axis):
    everything = from_everyone(shard, axis)
    return jnp.sum(everything, axis=0)


def together(arrays, axis):
    line, at, done = (jnp.concatenate([a.reshape(-1) for a in arrays]), 0, [])
    running = lax.psum(line, axis)
    for a in arrays:
        done.append(running[at : at + a.size].reshape(a.shape))
        at += a.size
    return tuple(done)


def advect(q, minus, plus, cu, cv, su, sv, lat_axis):
    lon_up = jnp.where(su > 0, jnp.roll(q, 1, lat_axis + 1), jnp.roll(q, -1, lat_axis + 1))
    lat_up = jnp.where(sv > 0, minus, plus)
    return q - cu * (q - lon_up) - cv * (q - lat_up)


def shards(
    covariance, lon_speed, lat_speed, lon_sign, lat_sign, measurement_site_position, obs_var
):
    rows_dev, cols_dev = covariance.shape
    row_bands = rows_dev // MERIDIAN_TOTAL
    col_bands = cols_dev // MERIDIAN_TOTAL
    row_start = lax.axis_index("row") * rows_dev
    col_start = lax.axis_index("col") * cols_dev

    def row_coeff(field):
        return lax.dynamic_slice_in_dim(field, row_start, rows_dev).reshape(
            row_bands, MERIDIAN_TOTAL, 1
        )

    row_cu, row_cv = (row_coeff(lon_speed), row_coeff(lat_speed))
    row_su, row_sv = (row_coeff(lon_sign), row_coeff(lat_sign))
    segment_patch = covariance
    for step in range(STEPS):
        padded = padded_2(segment_patch, (("row", 0),), MERIDIAN_TOTAL)
        shaped = padded.reshape(row_bands + 2, MERIDIAN_TOTAL, cols_dev)
        segment_patch = advect(
            shaped[1:-1], shaped[:-2], shaped[2:], row_cu, row_cv, row_su, row_sv, 0
        )
        segment_patch = segment_patch.reshape(rows_dev, cols_dev)
    margin = STEPS * MERIDIAN_TOTAL
    total_bands = col_bands + 2 * STEPS

    def wide_coeff(field):
        extended = jnp.pad(field, (margin, margin))
        return lax.dynamic_slice_in_dim(extended, col_start, cols_dev + 2 * margin).reshape(
            1, total_bands, MERIDIAN_TOTAL
        )

    col_cu, col_cv = (wide_coeff(lon_speed), wide_coeff(lat_speed))
    col_su, col_sv = (wide_coeff(lon_sign), wide_coeff(lat_sign))
    band_ids = col_start // MERIDIAN_TOTAL - STEPS + jnp.arange(total_bands, dtype=jnp.int32)
    inside = (
        ((band_ids >= 0) & (band_ids < PARALLEL_STRIPS))
        .astype(jnp.float32)
        .reshape(1, total_bands, 1)
    )
    padded = padded_2(segment_patch, (("col", 1),), margin)
    current = padded.reshape(rows_dev, total_bands, MERIDIAN_TOTAL)
    offset = 0
    for step in range(STEPS):
        count = current.shape[1]
        low, high = (offset + 1, offset + count - 1)
        current = (
            advect(
                current[:, 1:-1],
                current[:, :-2],
                current[:, 2:],
                col_cu[:, low:high],
                col_cv[:, low:high],
                col_su[:, low:high],
                col_sv[:, low:high],
                1,
            )
            * inside[:, low:high]
        )
        offset = offset + 1
    segment_patch = current.reshape(rows_dev, cols_dev)
    col_local = measurement_site_position - col_start
    row_local = measurement_site_position - row_start
    col_valid = (col_local >= 0) & (col_local < cols_dev)
    row_valid = (row_local >= 0) & (row_local < rows_dev)
    col_clip = jnp.clip(col_local, 0, cols_dev - 1)
    row_clip = jnp.clip(row_local, 0, rows_dev - 1)
    highest = lax.Precision.HIGHEST
    pht_local = jnp.where(col_valid[None, :], jnp.take(segment_patch, col_clip, axis=1), 0.0)
    hp_local = jnp.where(row_valid[:, None], jnp.take(segment_patch, row_clip, axis=0), 0.0)
    background_product_gain = over_copies(pht_local, "col")
    inner_local = jnp.where(
        row_valid[:, None], jnp.take(background_product_gain, row_clip, axis=0), 0.0
    )
    measured_background_lines, hpht = together((hp_local, inner_local), "row")
    innovation = hpht + jnp.diag(obs_var)
    factor = jnp.linalg.cholesky(innovation)
    weights = jax.scipy.linalg.cho_solve((factor, True), measured_background_lines)
    measurement_correction = jnp.dot(
        background_product_gain, weights, precision=highest, preferred_element_type=jnp.float32
    )
    return segment_patch - measurement_correction


def solution(mesh):
    return jax.shard_map(
        shards,
        mesh=mesh,
        in_specs=(P("row", "col"), P(), P(), P(), P(), P(), P()),
        out_specs=P("row", "col"),
        check_vma=False,
    )
```

profile of v0, /device:TPU:1, one launch (start us, length us, event | category | flops | bytes accessed | tf_op | source)
XLA Modules:
  0.0 630.9 jit_solution(3264469337388955791)
XLA Ops:
  6.5 1.1 copy.35
  7.6 5.4 collective-permute-start
  13.0 11.9 %collective-permute-start.1 = (f32[128,512]{0,1:T(8,128)S(1)}, f32[128,512]{0,1:T(8,128)S(1)}, u32[]{:S(2)}, u32[]{:S(2)}) collective-permute-start(f32[128,512]{0,1:T(8,128)S(1)} %copy.35), channel_id=1, source_target_pairs={{16,0},{32,16},{48,32},{64,48},{80,64},{96,80},{112,96},{128,112},... | collective-permute-start | bytes 786440 | tf_op jit(solution)/shard_map/ppermute | solution.py:21
  25.1 0.8 fusion.46
  26.0 0.8 fusion.47
  27.7 0.8 dynamic-slice_compare_fusion
  30.4 1.9 collective-permute-start.2
  32.3 2.4 collective-permute-start.3
  35.6 4.4 collective-permute-done.3
  40.2 1.9 collective-permute-start.4
  42.2 2.4 collective-permute-start.5
  45.5 4.4 collective-permute-done.5
  50.1 1.3 collective-permute-start.6
  51.4 1.3 collective-permute-start.7
  52.8 1.2 collective-permute-done.6
  54.0 3.8 collective-permute-done.7
  60.9 1.5 broadcast_in_dim.189
  62.4 6.6 %all-to-all-start = ((f32[16,128,256]{2,1,0:T(8,128)}), f32[16,128,256]{2,1,0:T(8,128)S(1)}, u32[]{:S(2)}, u32[]{:S(2)}) async-start(f32[16,128,256]{2,1,0:T(8,128)} %broadcast_in_dim.189), calls=%async_computation | async-start | bytes 4194304 | tf_op jit(solution)/shard_map/all_to_all | solution.py:30
  69.4 1.0 gather_fusion.1
  70.7 37.0 %all-to-all-done = f32[16,128,256]{2,1,0:T(8,128)S(1)} async-done(((f32[16,128,256]{2,1,0:T(8,128)}), f32[16,128,256]{2,1,0:T(8,128)S(1)}, u32[]{:S(2)}, u32[]{:S(2)}) %all-to-all-start) | async-done | bytes 2097184 | tf_op jit(solution)/shard_map/all_to_all | solution.py:30
  107.8 1.0 gather_fusion.2
  109.2 1.0 pad_maximum_fusion
  110.2 447.8 %all-reduce.7.cloned.1.call-done = f32[196608]{0:T(1024)} async-done(((f32[196608]{0:T(1024)}), f32[196608]{0:T(1024)}) %all-reduce.7.cloned.1.call-update) | async-done | bytes 786448 | tf_op jit(solution)/shard_map/psum | solution.py:40
  558.0 1.2 fusion.58
  559.7 11.7 %cholesky.48 = f32[128,128]{1,0:T(8,128)S(1)} custom-call(f32[128,128]{1,0:T(8,128)S(1)} %cholesky.112), custom_call_target="Cholesky" | custom-call | tf_op jit(solution)/shard_map/jit(cholesky)/cholesky | solution.py:130
  571.4 9.8 %custom-call.18 = f32[1,128,128]{1,2,0:T(8,128)S(1)} custom-call(f32[1,128,128]{2,1,0:T(8,128)S(1)} %get-tuple-element.69), custom_call_target="InvertDiagBlocksLowerTriangular" | custom-call | tf_op jit(solution)/shard_map/jit(cholesky)/cholesky | solution.py:130
  581.7 11.9 %cholesky.101 = f32[128,128]{1,0:T(8,128)S(1)} custom-call(f32[128,128]{1,0:T(8,128)S(1)} %convolution_subtract_fusion.3), custom_call_target="Cholesky" | custom-call | tf_op jit(solution)/shard_map/jit(cholesky)/cholesky | solution.py:130
  596.6 4.1 while.1
  597.2 1.3 dynamic-slice.7
  599.3 1.3 dynamic-slice.7
  600.8 19.7 %custom-call.19 = f32[2,128,128]{1,2,0:T(8,128)S(1)} custom-call(f32[2,128,128]{2,1,0:T(8,128)S(1)} %get-tuple-element.12), custom_call_target="InvertDiagBlocksLowerTriangular" | custom-call | tf_op jit(solution)/shard_map/jit(_cho_solve)/triangular_solve | solution.py:131
  622.9 1.1 convolution_subtract_fusion
  (98 shorter events, 15.8 us)
Async XLA Ops:
  7.6 22.6 %collective-permute-start = (f32[128,512]{0,1:T(8,128)S(1)}, f32[128,512]{0,1:T(8,128)S(1)}, u32[]{:S(2)}, u32[]{:S(2)}) collective-permute-start(f32[128,512]{0,1:T(8,128)S(1)} %copy.35), channel_id=1, source_target_pairs={{0,16},{16,32},{32,48},{48,64},{64,80},{80,96},{96,112},{112,128},... | collective-permute-start | bytes 786440 | tf_op jit(solution)/shard_map/ppermute | solution.py:19
  13.0 17.2 %collective-permute-start.1 = (f32[128,512]{0,1:T(8,128)S(1)}, f32[128,512]{0,1:T(8,128)S(1)}, u32[]{:S(2)}, u32[]{:S(2)}) collective-permute-start(f32[128,512]{0,1:T(8,128)S(1)} %copy.35), channel_id=1, source_target_pairs={{16,0},{32,16},{48,32},{64,48},{80,64},{96,80},{112,96},{128,112},... | collective-permute-start | bytes 786440 | tf_op jit(solution)/shard_map/ppermute | solution.py:21
  30.4 5.2 collective-permute-start.2
  32.3 7.7 %collective-permute-start.3 = (f32[128,512]{0,1:T(8,128)S(1)}, f32[128,512]{0,1:T(8,128)S(1)}, u32[]{:S(2)}, u32[]{:S(2)}) collective-permute-start(f32[128,512]{0,1:T(8,128)S(1)} %fusion.24), channel_id=1, source_target_pairs={{16,0},{32,16},{48,32},{64,48},{80,64},{96,80},{112,96},{128,112},... | collective-permute-start | bytes 786440 | tf_op jit(solution)/shard_map/ppermute | solution.py:21
  40.2 5.2 collective-permute-start.4
  42.2 7.7 %collective-permute-start.5 = (f32[128,512]{0,1:T(8,128)S(1)}, f32[128,512]{0,1:T(8,128)S(1)}, u32[]{:S(2)}, u32[]{:S(2)}) collective-permute-start(f32[128,512]{0,1:T(8,128)S(1)} %fusion.28), channel_id=1, source_target_pairs={{16,0},{32,16},{48,32},{64,48},{80,64},{96,80},{112,96},{128,112},... | collective-permute-start | bytes 786440 | tf_op jit(solution)/shard_map/ppermute | solution.py:21
  50.1 3.9 collective-permute-start.6
  51.4 6.4 %collective-permute-start.7 = (f32[128,384]{0,1:T(8,128)S(1)}, f32[128,384]{0,1:T(8,128)S(1)}, u32[]{:S(2)}, u32[]{:S(2)}) collective-permute-start(f32[128,384]{0,1:T(8,128)S(1)} %get-tuple-element.55), channel_id=1, source_target_pairs={{1,0},{2,1},{3,2},{4,3},{5,4},{6,5},{7,6},{8,7},{9,8},{10,9},{11,1... | collective-permute-start | bytes 589832 | tf_op jit(solution)/shard_map/ppermute | solution.py:21
  62.4 45.2 %all-to-all-start = ((f32[16,128,256]{2,1,0:T(8,128)}), f32[16,128,256]{2,1,0:T(8,128)S(1)}, u32[]{:S(2)}, u32[]{:S(2)}) async-start(f32[16,128,256]{2,1,0:T(8,128)} %broadcast_in_dim.189), calls=%async_computation | async-start | bytes 4194304 | tf_op jit(solution)/shard_map/all_to_all | solution.py:30
  69.0 489.0 %all-reduce.7.cloned.1.call-start = ((), (), s32[]{:S(2)}) async-start(), calls=%async_computation.1 | async-start | bytes 1572864 | tf_op jit(solution)/shard_map/psum | solution.py:40
  110.2 449.3 %copy-start = (f32[256]{0:T(256)S(1)}, f32[256]{0:T(256)}, u32[]{:S(2)}) copy-start(f32[256]{0:T(256)} %param.13) | copy-start | bytes 3076
Sparse Core Ops, SparseCore 0:
  110.3 447.6 all-reduce.6
where the time goes:
time: 632 us; the launch traced here: 631 us
  waiting for transfers between devices  500 us (79%)
  other arithmetic  59.9 us (9%)
  starting transfers between devices  35.4 us (6%)
  local copies, waits for them, and re-layouts  16.4 us (3%)
  between operations  15.3 us (2%)
    psum x1, waiting for transfers between devices, together(): running = lax.psum(line, axis)  448 us
    all_to_all x1, waiting for transfers between devices, from_everyone(): return lax.all_to_all(copies, axis, split_axis=0, concat_axis=0, tiled=True)  37 us
    another operation x7, other arithmetic, shards(): factor = jnp.linalg.cholesky(innovation)  34.8 us
    another operation x3, other arithmetic, shards(): jax.scipy.linalg.cho_solve((factor, True), measured_background_lines)  19.7 us
    ppermute x4, starting transfers between devices, padded_2(): lax.ppermute(head, axis, [((i + 1) % count, i) for i in range(ends)])  18.1 us
  transfers between devices with their start and end apart: 10, of which 8 were waited for; matrix products, arithmetic and copies ran while one was open for 1% of the time, Pallas kernels for 0%

commit v1 on v0

v1 whole, which is shorter than its diff:
```python
import functools

import jax
import jax.numpy as jnp
from jax import lax
from jax.experimental import pallas as pl
from jax.experimental.pallas import tpu as pltpu
from jax.sharding import Mesh
from jax.sharding import PartitionSpec as P

PARALLEL_STRIPS = 64
MERIDIAN_TOTAL = 128
STEPS = 3
HIGHEST = lax.Precision.HIGHEST
PANEL = 32
GROUP = 8
ROW = ("yl", "z", "co")
COL = ("yh", "x")


def padded_2(cells, sides, width):
    for axis, dim in sides:
        count = lax.axis_size(axis)
        ends = count - 1
        head = lax.slice_in_dim(cells, 0, width, axis=dim)
        tail = lax.slice_in_dim(cells, cells.shape[dim] - width, cells.shape[dim], axis=dim)
        cells = jnp.concatenate(
            [
                lax.ppermute(tail, axis, [(i, (i + 1) % count) for i in range(ends)]),
                cells,
                lax.ppermute(head, axis, [((i + 1) % count, i) for i in range(ends)]),
            ],
            axis=dim,
        )
    return cells


def advect(q, minus, plus, cu, cv, su, sv, lat_axis):
    lon_up = jnp.where(su > 0, jnp.roll(q, 1, lat_axis + 1), jnp.roll(q, -1, lat_axis + 1))
    lat_up = jnp.where(sv > 0, minus, plus)
    return q - cu * (q - lon_up) - cv * (q - lat_up)


def inverse_kernel(s_ref, var_ref, out_ref):
    n = s_ref.shape[0]
    s = s_ref[...]
    row_id = lax.broadcasted_iota(jnp.int32, (n, n), 0)
    col_id = lax.broadcasted_iota(jnp.int32, (n, n), 1)
    out_ref[...] = 0.5 * (s + s.T) + jnp.where(row_id == col_id, var_ref[...], 0.0)
    sub_wide = lax.broadcasted_iota(jnp.int32, (PANEL, n), 0)
    lane_wide = lax.broadcasted_iota(jnp.int32, (PANEL, n), 1)
    sub = lax.broadcasted_iota(jnp.int32, (PANEL, 128), 0)
    lane = lax.broadcasted_iota(jnp.int32, (PANEL, 128), 1)
    for at in range(0, n, PANEL):
        tile = at // 128 * 128
        rows = out_ref[at : at + PANEL, :]
        own = jnp.where(lane - (at - tile) == sub, 1.0, 0.0)
        for first in range(0, PANEL, GROUP):
            spread = [
                jnp.broadcast_to(rows[:, at + first + m : at + first + m + 1], (PANEL, 128))
                for m in range(GROUP)
            ]
            for m in range(GROUP):
                j = first + m
                factor = spread[m]
                pivot = factor[j : j + 1, :]
                inv = jnp.where(pivot > 0.0, 1.0 / pivot, jnp.nan)
                here = sub == j
                for k in range(m + 1, GROUP):
                    line = spread[k][j : j + 1, :] * inv
                    spread[k] = jnp.where(here, line, spread[k] - factor * line)
                line = own[j : j + 1, :] * inv
                own = jnp.where(here, line, own - factor * line)
                inv2 = jnp.concatenate([inv] * (n // 128), axis=1)
                factor2 = jnp.concatenate([factor] * (n // 128), axis=1)
                line = rows[j : j + 1, :] * inv2
                rows = jnp.where(sub_wide == j, line, rows - factor2 * line)
        placed = jnp.concatenate([own if t == tile else jnp.zeros_like(own) for t in range(0, n, 128)], axis=1)
        inside = (lane_wide >= at) & (lane_wide < at + PANEL)
        rows = jnp.where(inside, placed, rows)
        update = jnp.dot(out_ref[:, at : at + PANEL], rows, precision=HIGHEST, preferred_element_type=jnp.float32)
        keep = jnp.where((col_id >= at) & (col_id < at + PANEL), 0.0, out_ref[...])
        out_ref[...] = keep - update
        out_ref[at : at + PANEL, :] = rows


def spd_inverse(s, var):
    n = s.shape[0]
    return pl.pallas_call(
        inverse_kernel,
        out_shape=jax.ShapeDtypeStruct((n, n), jnp.float32),
        in_specs=[pl.BlockSpec(memory_space=pltpu.VMEM)] * 2,
        out_specs=pl.BlockSpec(memory_space=pltpu.VMEM),
        cost_estimate=pl.CostEstimate(flops=4 * n * n * n, bytes_accessed=8 * n * n, transcendentals=0),
        name="spd_inverse",
    )(s, var.reshape(1, n))


def everyone(chunk, axis):
    copies = jnp.broadcast_to(chunk, (lax.axis_size(axis), *chunk.shape))
    return lax.all_to_all(copies, axis, split_axis=0, concat_axis=0, tiled=True)


def scattered_sum(parts, axis):
    return jnp.sum(lax.all_to_all(parts, axis, split_axis=0, concat_axis=0, tiled=True), axis=0)


SWAP = [(0, 1), (1, 0)]


def halves(cells, dim, mine):
    width = cells.shape[dim] // 2
    low = lax.slice_in_dim(cells, 0, width, axis=dim)
    high = lax.slice_in_dim(cells, width, 2 * width, axis=dim)
    return jnp.where(mine == 0, low, high), jnp.where(mine == 0, high, low)


def joined(own, other, dim, mine):
    return jnp.concatenate(
        [jnp.where(mine == 0, own, other), jnp.where(mine == 0, other, own)], axis=dim
    )


def transported(covariance, lon_speed, lat_speed, lon_sign, lat_sign, row_start, col_start):
    rows_dev, cols_dev = covariance.shape
    row_bands = rows_dev // MERIDIAN_TOTAL
    col_bands = cols_dev // MERIDIAN_TOTAL

    def row_coeff(field):
        return lax.dynamic_slice_in_dim(field, row_start, rows_dev).reshape(
            row_bands, MERIDIAN_TOTAL, 1
        )

    row_cu, row_cv = (row_coeff(lon_speed), row_coeff(lat_speed))
    row_su, row_sv = (row_coeff(lon_sign), row_coeff(lat_sign))
    segment_patch = covariance
    for step in range(STEPS):
        padded = padded_2(segment_patch, ((ROW, 0),), MERIDIAN_TOTAL)
        shaped = padded.reshape(row_bands + 2, MERIDIAN_TOTAL, cols_dev)
        segment_patch = advect(
            shaped[1:-1], shaped[:-2], shaped[2:], row_cu, row_cv, row_su, row_sv, 0
        )
        segment_patch = segment_patch.reshape(rows_dev, cols_dev)
    margin = STEPS * MERIDIAN_TOTAL
    total_bands = col_bands + 2 * STEPS

    def wide_coeff(field):
        extended = jnp.pad(field, (margin, margin))
        return lax.dynamic_slice_in_dim(extended, col_start, cols_dev + 2 * margin).reshape(
            1, total_bands, MERIDIAN_TOTAL
        )

    col_cu, col_cv = (wide_coeff(lon_speed), wide_coeff(lat_speed))
    col_su, col_sv = (wide_coeff(lon_sign), wide_coeff(lat_sign))
    band_ids = col_start // MERIDIAN_TOTAL - STEPS + jnp.arange(total_bands, dtype=jnp.int32)
    inside = (
        ((band_ids >= 0) & (band_ids < PARALLEL_STRIPS))
        .astype(jnp.float32)
        .reshape(1, total_bands, 1)
    )
    padded = padded_2(segment_patch, ((COL, 1),), margin)
    current = padded.reshape(rows_dev, total_bands, MERIDIAN_TOTAL)
    offset = 0
    for step in range(STEPS):
        count = current.shape[1]
        low, high = (offset + 1, offset + count - 1)
        current = (
            advect(
                current[:, 1:-1],
                current[:, :-2],
                current[:, 2:],
                col_cu[:, low:high],
                col_cv[:, low:high],
                col_su[:, low:high],
                col_sv[:, low:high],
                1,
            )
            * inside[:, low:high]
        )
        offset = offset + 1
    return current.reshape(rows_dev, cols_dev)


def shards(
    covariance, lon_speed, lat_speed, lon_sign, lat_sign, measurement_site_position, obs_var
):
    rows_dev, cols_dev = covariance.shape
    nobs = measurement_site_position.shape[0]
    lat_half, core = lax.axis_index("yl"), lax.axis_index("co")
    row_start = lax.axis_index(ROW) * rows_dev
    col_start = lax.axis_index(COL) * cols_dev
    dot = functools.partial(
        lax.dot_general, precision=HIGHEST, preferred_element_type=jnp.float32
    )
    forecast = transported(
        covariance, lon_speed, lat_speed, lon_sign, lat_sign, row_start, col_start
    )
    site = measurement_site_position[:, None]

    def picks(start, size):
        cell = start + lax.broadcasted_iota(jnp.int32, (nobs, size), 1)
        return (cell == site).astype(jnp.float32)

    pht = dot(picks(col_start, cols_dev), forecast, (((1,), (1,)), ((), ())))
    sides = lax.axis_size(COL)
    pht = scattered_sum(pht.reshape(sides, nobs // sides, rows_dev), COL)

    half = cols_dev // 2
    own, other = halves(forecast, 1, core)
    both = joined(own, lax.ppermute(other, "co", SWAP), 0, core)
    hp = dot(picks(row_start - core * rows_dev, 2 * rows_dev), both, (((1,), (0,)), ((), ())))
    own, other = halves(hp, 0, lat_half)
    hp = own + lax.ppermute(other, "yl", SWAP)
    deep = lax.axis_size("z")
    hp = scattered_sum(hp.reshape(deep, nobs // 2 // deep, half), "z")

    hpht = dot(hp, picks(col_start + core * half, half), (((1,), (1,)), ((), ())))
    hpht = jnp.sum(everyone(hpht, COL), axis=0)
    block = jnp.concatenate([hp, hpht], axis=1)
    block = everyone(block, "z").reshape(nobs // 2, half + nobs)
    block = joined(block, lax.ppermute(block, "yl", SWAP), 0, lat_half)
    block = lax.all_gather(block, "co", axis=0)
    hp = jnp.concatenate([block[0, :, :half], block[1, :, :half]], axis=1)
    hpht = block[0, :, half:] + block[1, :, half:]

    inverse = spd_inverse(hpht, obs_var)
    pht = everyone(pht, COL).reshape(nobs, rows_dev)
    gain = dot(inverse, pht, (((1,), (0,)), ((), ())))
    return forecast - dot(gain, hp, (((0,), (0,)), ((), ())))


def solution(mesh):
    fine = Mesh(mesh.devices.reshape(2, 16, 2, 4, 4), ROW + COL)
    return jax.shard_map(
        shards,
        mesh=fine,
        in_specs=(P(ROW, COL), P(), P(), P(), P(), P(), P()),
        out_specs=P(ROW, COL),
        check_vma=False,
    )
```

time: 632 us -> 199 us (0.31)
  waiting for transfers between devices: 500 us -> 41.8 us
  blocking collectives: 0 us -> 55 us
  other arithmetic: 59.9 us -> 6.22 us
  starting transfers between devices: 35.4 us -> 58 us
  Pallas kernels: 0 us -> 12 us
  local copies, waits for them, and re-layouts: 16.4 us -> 4.99 us
    psum x1 -> x0, waiting for transfers between devices: 448 us -> none  [together(): running = lax.psum(line, axis)]
    all_to_all x0 -> x3, blocking collectives: none -> 55 us  [the longest x2 42.8 us: everyone(): return lax.all_to_all(copies, axis, split_axis=0, concat_axis=0, tiled=True)]
    another operation x10 -> x0, other arithmetic: 54.5 us -> none  [the longest x7 34.8 us: shards(): factor = jnp.linalg.cholesky(innovation)]
    all_to_all x1 -> x2, waiting for transfers between devices: 37 us -> 11.9 us  [the longest x1 11.9 us: scattered_sum(): lax.all_to_all(parts, axis, split_axis=0, concat_axis=0, tiled=True)]
    ppermute x0 -> x3, starting transfers between devices: none -> 21.1 us  [the longest x1 16.1 us: shards(): hp = own + lax.ppermute(other, 'yl', SWAP)]
    pallas_call x0 -> x1, Pallas kernels: none -> 12 us  [spd_inverse(): pl.pallas_call(inverse_kernel, out_shape=jax.ShapeDtypeStruct((n, n), jnp...]
    ppermute x0 -> x3, waiting for transfers between devices: none -> 8.78 us  [the longest x1 3.99 us: shards(): block = joined(block, lax.ppermute(block, 'yl', SWAP), 0, lat_half)]
  transfers between devices with their start and end apart: 10 -> 14, of which waited for: 8 -> 11; matrix products, arithmetic and copies ran while one was open for 1% -> 2% of each run, Pallas kernels for 0% -> 6%
where the time goes in v1:
time: 199 us; the launch traced here: 196 us
  starting transfers between devices  58 us (29%)
  blocking collectives  55 us (28%)
  waiting for transfers between devices  41.8 us (21%)
  between operations  13.9 us (7%)
  Pallas kernels  12 us (6%)
  other arithmetic  6.22 us (3%)
  local copies, waits for them, and re-layouts  4.99 us (3%)
  matrix products  3.47 us (2%)
    all_to_all x2, blocking collectives, everyone(): return lax.all_to_all(copies, axis, split_axis=0, concat_axis=0, tiled=True)  42.8 us
    ppermute x4, starting transfers between devices, padded_2(): lax.ppermute(head, axis, [((i + 1) % count, i) for i in range(ends)])  18.1 us
    ppermute x1, starting transfers between devices, shards(): hp = own + lax.ppermute(other, 'yl', SWAP)  16.1 us
    ppermute x4, waiting for transfers between devices, padded_2(): lax.ppermute(head, axis, [((i + 1) % count, i) for i in range(ends)])  12.6 us
    all_to_all x1, blocking collectives, scattered_sum(): lax.all_to_all(parts, axis, split_axis=0, concat_axis=0, tiled=True)  12.2 us
    pallas_call x1, Pallas kernels, spd_inverse(): pl.pallas_call(inverse_kernel, out_shape=jax.ShapeDtypeStruct((n, n), jnp...  12 us
    all_to_all x1, waiting for transfers between devices, scattered_sum(): lax.all_to_all(parts, axis, split_axis=0, concat_axis=0, tiled=True)  11.9 us
    ppermute x4, starting transfers between devices, padded_2(): lax.ppermute(tail, axis, [(i, (i + 1) % count) for i in range(ends)])  10.5 us
  transfers between devices with their start and end apart: 14, of which 11 were waited for; matrix products, arithmetic and copies ran while one was open for 2% of the time, Pallas kernels for 6%

profile of v1, /device:TPU:1, one launch (start us, length us, event | category | flops | bytes accessed | tf_op | source)
XLA Modules:
  0.0 195.5 jit_solution(18254978089595288124)
XLA Ops:
  6.5 1.1 copy.17
  7.6 5.4 %collective-permute-start = (f32[128,512]{0,1:T(8,128)S(1)}, f32[128,512]{0,1:T(8,128)S(1)}, u32[]{:S(2)}, u32[]{:S(2)}) collective-permute-start(f32[128,512]{0,1:T(8,128)S(1)} %copy.17), channel_id=1, source_target_pairs={{0,16},{16,32},{32,48},{48,64},{64,80},{80,96},{96,112},{112,128},... | collective-permute-start | bytes 786440 | tf_op jit(solution)/shard_map/ppermute | solution.py:29
  13.0 11.9 %collective-permute-start.1 = (f32[128,512]{0,1:T(8,128)S(1)}, f32[128,512]{0,1:T(8,128)S(1)}, u32[]{:S(2)}, u32[]{:S(2)}) collective-permute-start(f32[128,512]{0,1:T(8,128)S(1)} %copy.17), channel_id=1, source_target_pairs={{16,0},{32,16},{48,32},{64,48},{80,64},{96,80},{112,96},{128,112},... | collective-permute-start | bytes 786440 | tf_op jit(solution)/shard_map/ppermute | solution.py:31
  26.9 1.9 collective-permute-start.2
  28.9 2.4 %collective-permute-start.3 = (f32[128,512]{0,1:T(8,128)S(1)}, f32[128,512]{0,1:T(8,128)S(1)}, u32[]{:S(2)}, u32[]{:S(2)}) collective-permute-start(f32[128,512]{0,1:T(8,128)S(1)} %fusion.27), channel_id=1, source_target_pairs={{16,0},{32,16},{48,32},{64,48},{80,64},{96,80},{112,96},{128,112},... | collective-permute-start | bytes 786440 | tf_op jit(solution)/shard_map/ppermute | solution.py:31
  32.1 4.4 %collective-permute-done.3 = f32[128,512]{0,1:T(8,128)S(1)} collective-permute-done((f32[128,512]{0,1:T(8,128)S(1)}, f32[128,512]{0,1:T(8,128)S(1)}, u32[]{:S(2)}, u32[]{:S(2)}) %collective-permute-start.3) | collective-permute-done | bytes 262176 | tf_op jit(solution)/shard_map/ppermute | solution.py:31
  36.8 1.9 collective-permute-start.4
  38.7 2.4 %collective-permute-start.5 = (f32[128,512]{0,1:T(8,128)S(1)}, f32[128,512]{0,1:T(8,128)S(1)}, u32[]{:S(2)}, u32[]{:S(2)}) collective-permute-start(f32[128,512]{0,1:T(8,128)S(1)} %fusion.31), channel_id=1, source_target_pairs={{16,0},{32,16},{48,32},{64,48},{80,64},{96,80},{112,96},{128,112},... | collective-permute-start | bytes 786440 | tf_op jit(solution)/shard_map/ppermute | solution.py:31
  42.0 4.4 %collective-permute-done.5 = f32[128,512]{0,1:T(8,128)S(1)} collective-permute-done((f32[128,512]{0,1:T(8,128)S(1)}, f32[128,512]{0,1:T(8,128)S(1)}, u32[]{:S(2)}, u32[]{:S(2)}) %collective-permute-start.5) | collective-permute-done | bytes 262176 | tf_op jit(solution)/shard_map/ppermute | solution.py:31
  46.6 1.3 collective-permute-start.6
  47.9 1.3 collective-permute-start.7
  49.3 1.2 collective-permute-done.6
  50.5 3.8 %collective-permute-done.7 = f32[128,384]{0,1:T(8,128)S(1)} collective-permute-done((f32[128,384]{0,1:T(8,128)S(1)}, f32[128,384]{0,1:T(8,128)S(1)}, u32[]{:S(2)}, u32[]{:S(2)}) %collective-permute-start.7) | collective-permute-done | bytes 196640 | tf_op jit(solution)/shard_map/ppermute | solution.py:31
  54.5 0.8 fusion.3
  56.6 1.9 collective-permute-start.8
  58.5 1.3 collective-permute-done.8
  60.9 16.1 %collective-permute-start.9 = (f32[128,256]{1,0:T(8,128)S(1)}, f32[128,256]{1,0:T(8,128)S(1)}, u32[]{:S(2)}, u32[]{:S(2)}) collective-permute-start(f32[128,256]{1,0:T(8,128)S(1)} %slice_select_fusion.3), channel_id=1, source_target_pairs={{0,512},{512,0},{1,513},{513,1},{2,514},{514,2},{3,515},{515,3},{4... | collective-permute-start | bytes 393224 | tf_op jit(solution)/shard_map/ppermute | solution.py:213
  77.0 3.5 %collective-permute-done.9 = f32[128,256]{1,0:T(8,128)S(1)} collective-permute-done((f32[128,256]{1,0:T(8,128)S(1)}, f32[128,256]{1,0:T(8,128)S(1)}, u32[]{:S(2)}, u32[]{:S(2)}) %collective-permute-start.9) | collective-permute-done | bytes 131104 | tf_op jit(solution)/shard_map/ppermute | solution.py:213
  81.2 4.6 %all-to-all-start = ((f32[16,8,256]{2,1,0:T(8,128)}), f32[16,8,256]{2,1,0:T(8,128)S(1)}, u32[]{:S(2)}, u32[]{:S(2)}) async-start(f32[16,8,256]{2,1,0:T(8,128)} %add_bitcast_fusion), calls=%async_computation | async-start | bytes 262144 | tf_op jit(solution)/shard_map/all_to_all | solution.py:105
  85.8 11.9 %all-to-all-done = f32[16,8,256]{2,1,0:T(8,128)S(1)} async-done(((f32[16,8,256]{2,1,0:T(8,128)}), f32[16,8,256]{2,1,0:T(8,128)S(1)}, u32[]{:S(2)}, u32[]{:S(2)}) %all-to-all-start) | async-done | bytes 131104 | tf_op jit(solution)/shard_map/all_to_all | solution.py:105
  98.1 24.7 %all_to_all.25 = f32[16,8,256]{2,1,0:T(8,128)S(1)} all-to-all(f32[16,8,256]{2,1,0:T(8,128)S(1)} %broadcast_in_dim.100), channel_id=1, replica_groups=mesh['yl'=2,'z'=16,'co'=2,'yh'=4,'x'=4] {'yh','x'}, dimensions={0} | all-to-all | bytes 262144 | tf_op jit(solution)/shard_map/all_to_all | solution.py:101
  122.9 18.1 %all_to_all.26 = f32[16,8,512]{2,1,0:T(8,128)S(1)} all-to-all(f32[16,8,512]{2,1,0:T(8,128)S(1)} %broadcast_in_dim.101), channel_id=1, replica_groups=mesh['yl'=2,'z'=16,'co'=2,'yh'=4,'x'=4] {'z'}, dimensions={0} | all-to-all | bytes 524288 | tf_op jit(solution)/shard_map/all_to_all | solution.py:101
  140.9 3.1 %collective-permute-start.10 = (f32[128,512]{1,0:T(8,128)S(1)}, f32[128,512]{1,0:T(8,128)S(1)}, u32[]{:S(2)}, u32[]{:S(2)}) collective-permute-start(f32[128,512]{1,0:T(8,128)S(1)} %bitcast.101), channel_id=1, source_target_pairs={{0,512},{512,0},{1,513},{513,1},{2,514},{514,2},{3,515},{515,3},{4... | collective-permute-start | bytes 786440 | tf_op jit(solution)/shard_map/ppermute | solution.py:221
  144.0 4.0 %collective-permute-done.10 = f32[128,512]{1,0:T(8,128)S(1)} collective-permute-done((f32[128,512]{1,0:T(8,128)S(1)}, f32[128,512]{1,0:T(8,128)S(1)}, u32[]{:S(2)}, u32[]{:S(2)}) %collective-permute-start.10) | collective-permute-done | bytes 262176 | tf_op jit(solution)/shard_map/ppermute | solution.py:221
  148.1 0.8 pad_maximum_fusion.1
  149.4 12.2 %all_to_all.27 = f32[16,16,128]{2,1,0:T(8,128)S(1)} all-to-all(f32[16,16,128]{2,1,0:T(8,128)S(1)} %fusion.10), channel_id=1, replica_groups=mesh['yl'=2,'z'=16,'co'=2,'yh'=4,'x'=4] {'yh','x'}, dimensions={0} | all-to-all | bytes 262144 | tf_op jit(solution)/shard_map/all_to_all | solution.py:105
  162.4 3.7 %all-to-all-start.4 = ((f32[16,16,128]{2,1,0:T(8,128)}), f32[16,16,128]{2,1,0:T(8,128)S(1)}, u32[]{:S(2)}, u32[]{:S(2)}) async-start(f32[16,16,128]{2,1,0:T(8,128)} %broadcast_in_dim.102), calls=%async_computation.4 | async-start | bytes 262144 | tf_op jit(solution)/shard_map/all_to_all | solution.py:101
  166.1 6.1 %all-gather.3.cloned.1.call-done = f32[512,512]{1,0:T(8,128)} async-done(((f32[256,512]{1,0:T(8,128)}), f32[512,512]{1,0:T(8,128)}) %all-gather.3.cloned.1.call-update) | async-done | bytes 1048592 | tf_op jit(solution)/shard_map/all_gather | solution.py:222
  172.2 2.0 %slice_bitcast_fusion.1 = (f32[256,256]{1,0:T(8,128)S(1)}, f32[256,256]{1,0:T(8,128)}, f32[256,256]{1,0:T(8,128)S(1)}) fusion(f32[2,256,512]{2,1,0:T(8,128)} %bitcast.100), kind=kLoop, calls=%fused_computation.27 | loop fusion | flops 65536 | bytes 1835008 | tf_op jit(solution)/shard_map/squeeze | solution.py:223
  174.1 12.0 %spd_inverse.1 = f32[256,256]{1,0:T(8,128)} custom-call(f32[256,256]{1,0:T(8,128)} %get-tuple-element.6.s_ref, f32[1,256]{1,0:T(1,128)} %bitcast.103), custom_call_target="tpu_custom_call" | custom-call | flops 67108864 | bytes 524288 | tf_op jit(solution)/shard_map/spd_inverse/pallas_call | solution.py:89
  186.2 1.3 fusion.71
  187.5 1.2 convolution_subtract_fusion
  (77 shorter events, 8.8 us)
Async XLA Ops:
  6.5 18.6 %copy-start.3 = (f32[8192]{0:T(1024)S(1)}, f32[8192]{0:T(1024)}, u32[]{:S(2)}) copy-start(f32[8192]{0:T(1024)} %param.9) | copy-start | bytes 98308
  7.6 17.5 %copy-start.2 = (f32[8192]{0:T(1024)S(1)}, f32[8192]{0:T(1024)}, u32[]{:S(2)}) copy-start(f32[8192]{0:T(1024)} %param.8) | copy-start | bytes 98308
  7.6 19.1 %collective-permute-start = (f32[128,512]{0,1:T(8,128)S(1)}, f32[128,512]{0,1:T(8,128)S(1)}, u32[]{:S(2)}, u32[]{:S(2)}) collective-permute-start(f32[128,512]{0,1:T(8,128)S(1)} %copy.17), channel_id=1, source_target_pairs={{0,16},{16,32},{32,48},{48,64},{64,80},{80,96},{96,112},{112,128},... | collective-permute-start | bytes 786440 | tf_op jit(solution)/shard_map/ppermute | solution.py:29
  13.0 13.7 %collective-permute-start.1 = (f32[128,512]{0,1:T(8,128)S(1)}, f32[128,512]{0,1:T(8,128)S(1)}, u32[]{:S(2)}, u32[]{:S(2)}) collective-permute-start(f32[128,512]{0,1:T(8,128)S(1)} %copy.17), channel_id=1, source_target_pairs={{16,0},{32,16},{48,32},{64,48},{80,64},{96,80},{112,96},{128,112},... | collective-permute-start | bytes 786440 | tf_op jit(solution)/shard_map/ppermute | solution.py:31
  25.2 0.8 copy-start.1
  25.2 0.8 copy-start
  26.9 5.2 %collective-permute-start.2 = (f32[128,512]{0,1:T(8,128)S(1)}, f32[128,512]{0,1:T(8,128)S(1)}, u32[]{:S(2)}, u32[]{:S(2)}) collective-permute-start(f32[128,512]{0,1:T(8,128)S(1)} %fusion.27), channel_id=1, source_target_pairs={{0,16},{16,32},{32,48},{48,64},{64,80},{80,96},{96,112},{112,128},... | collective-permute-start | bytes 786440 | tf_op jit(solution)/shard_map/ppermute | solution.py:29
  28.9 7.7 %collective-permute-start.3 = (f32[128,512]{0,1:T(8,128)S(1)}, f32[128,512]{0,1:T(8,128)S(1)}, u32[]{:S(2)}, u32[]{:S(2)}) collective-permute-start(f32[128,512]{0,1:T(8,128)S(1)} %fusion.27), channel_id=1, source_target_pairs={{16,0},{32,16},{48,32},{64,48},{80,64},{96,80},{112,96},{128,112},... | collective-permute-start | bytes 786440 | tf_op jit(solution)/shard_map/ppermute | solution.py:31
  36.8 5.2 %collective-permute-start.4 = (f32[128,512]{0,1:T(8,128)S(1)}, f32[128,512]{0,1:T(8,128)S(1)}, u32[]{:S(2)}, u32[]{:S(2)}) collective-permute-start(f32[128,512]{0,1:T(8,128)S(1)} %fusion.31), channel_id=1, source_target_pairs={{0,16},{16,32},{32,48},{48,64},{64,80},{80,96},{96,112},{112,128},... | collective-permute-start | bytes 786440 | tf_op jit(solution)/shard_map/ppermute | solution.py:29
  38.7 7.7 %collective-permute-start.5 = (f32[128,512]{0,1:T(8,128)S(1)}, f32[128,512]{0,1:T(8,128)S(1)}, u32[]{:S(2)}, u32[]{:S(2)}) collective-permute-start(f32[128,512]{0,1:T(8,128)S(1)} %fusion.31), channel_id=1, source_target_pairs={{16,0},{32,16},{48,32},{64,48},{80,64},{96,80},{112,96},{128,112},... | collective-permute-start | bytes 786440 | tf_op jit(solution)/shard_map/ppermute | solution.py:31
  46.6 3.9 %collective-permute-start.6 = (f32[128,384]{0,1:T(8,128)S(1)}, f32[128,384]{0,1:T(8,128)S(1)}, u32[]{:S(2)}, u32[]{:S(2)}) collective-permute-start(f32[128,384]{0,1:T(8,128)S(1)} %get-tuple-element.24), channel_id=1, source_target_pairs={{0,1},{1,2},{2,3},{3,4},{4,5},{5,6},{6,7},{7,8},{8,9},{9,10},{10,1... | collective-permute-start | bytes 589832 | tf_op jit(solution)/shard_map/ppermute | solution.py:29
  47.9 6.4 %collective-permute-start.7 = (f32[128,384]{0,1:T(8,128)S(1)}, f32[128,384]{0,1:T(8,128)S(1)}, u32[]{:S(2)}, u32[]{:S(2)}) collective-permute-start(f32[128,384]{0,1:T(8,128)S(1)} %get-tuple-element.25), channel_id=1, source_target_pairs={{1,0},{2,1},{3,2},{4,3},{5,4},{6,5},{7,6},{8,7},{9,8},{10,9},{11,1... | collective-permute-start | bytes 589832 | tf_op jit(solution)/shard_map/ppermute | solution.py:31
  56.6 3.2 %collective-permute-start.8 = (f32[128,256]{1,0:T(8,128)S(1)}, f32[128,256]{1,0:T(8,128)S(1)}, u32[]{:S(2)}, u32[]{:S(2)}) collective-permute-start(f32[128,256]{1,0:T(8,128)S(1)} %slice_select_fusion.4), channel_id=1, source_target_pairs={{0,16},{16,0},{1,17},{17,1},{2,18},{18,2},{3,19},{19,3},{4,20},{20... | collective-permute-start | bytes 393224 | tf_op jit(solution)/shard_map/ppermute | solution.py:210
  59.9 0.7 copy-start.4
  60.9 19.6 %collective-permute-start.9 = (f32[128,256]{1,0:T(8,128)S(1)}, f32[128,256]{1,0:T(8,128)S(1)}, u32[]{:S(2)}, u32[]{:S(2)}) collective-permute-start(f32[128,256]{1,0:T(8,128)S(1)} %slice_select_fusion.3), channel_id=1, source_target_pairs={{0,512},{512,0},{1,513},{513,1},{2,514},{514,2},{3,515},{515,3},{4... | collective-permute-start | bytes 393224 | tf_op jit(solution)/shard_map/ppermute | solution.py:213
  81.2 16.6 %all-to-all-start = ((f32[16,8,256]{2,1,0:T(8,128)}), f32[16,8,256]{2,1,0:T(8,128)S(1)}, u32[]{:S(2)}, u32[]{:S(2)}) async-start(f32[16,8,256]{2,1,0:T(8,128)} %add_bitcast_fusion), calls=%async_computation | async-start | bytes 262144 | tf_op jit(solution)/shard_map/all_to_all | solution.py:105
  85.8 86.4 %all-gather.3.cloned.1.call-start = ((), (), s32[]{:S(2)}) async-start(), calls=%async_computation.5 | async-start | bytes 1572864 | tf_op jit(solution)/shard_map/all_gather | solution.py:222
  140.9 7.1 %collective-permute-start.10 = (f32[128,512]{1,0:T(8,128)S(1)}, f32[128,512]{1,0:T(8,128)S(1)}, u32[]{:S(2)}, u32[]{:S(2)}) collective-permute-start(f32[128,512]{1,0:T(8,128)S(1)} %bitcast.101), channel_id=1, source_target_pairs={{0,512},{512,0},{1,513},{513,1},{2,514},{514,2},{3,515},{515,3},{4... | collective-permute-start | bytes 786440 | tf_op jit(solution)/shard_map/ppermute | solution.py:221
  162.4 23.8 %all-to-all-start.4 = ((f32[16,16,128]{2,1,0:T(8,128)}), f32[16,16,128]{2,1,0:T(8,128)S(1)}, u32[]{:S(2)}, u32[]{:S(2)}) async-start(f32[16,16,128]{2,1,0:T(8,128)} %broadcast_in_dim.102), calls=%async_computation.4 | async-start | bytes 262144 | tf_op jit(solution)/shard_map/all_to_all | solution.py:101
Sparse Core Ops, SparseCore 0:
  149.1 23.0 all-gather.2

commit v2 on v1

--- a/solution.py
+++ b/solution.py
@@ -215,16 +215,19 @@
     hp = scattered_sum(hp.reshape(deep, nobs // 2 // deep, half), "z")
 
     hpht = dot(hp, picks(col_start + core * half, half), (((1,), (1,)), ((), ())))
-    hpht = jnp.sum(everyone(hpht, COL), axis=0)
+    flat = pht.shape[1]
+    mine = pht.shape[0]
+    found = everyone(jnp.concatenate([pht, hpht.reshape(-1, flat)], axis=0), COL)
+    pht = found[:, :mine].reshape(nobs, rows_dev)
+    hpht = jnp.sum(found[:, mine:], axis=0).reshape(hpht.shape)
     block = jnp.concatenate([hp, hpht], axis=1)
     block = everyone(block, "z").reshape(nobs // 2, half + nobs)
     block = joined(block, lax.ppermute(block, "yl", SWAP), 0, lat_half)
-    block = lax.all_gather(block, "co", axis=0)
-    hp = jnp.concatenate([block[0, :, :half], block[1, :, :half]], axis=1)
-    hpht = block[0, :, half:] + block[1, :, half:]
+    fellow = lax.ppermute(block, "co", SWAP)
+    hp = joined(block[:, :half], fellow[:, :half], 1, core)
+    hpht = block[:, half:] + fellow[:, half:]
 
     inverse = spd_inverse(hpht, obs_var)
-    pht = everyone(pht, COL).reshape(nobs, rows_dev)
     gain = dot(inverse, pht, (((1,), (0,)), ((), ())))
     return forecast - dot(gain, hp, (((0,), (0,)), ((), ())))
 

time: 199 us -> 180 us (0.905); the launches traced: 196 us -> 179 us
  blocking collectives: 55 us -> 32.1 us
  starting transfers between devices: 58 us -> 79.4 us
  between operations: 13.9 us -> 0.56 us
    all_to_all x1 -> x2, starting transfers between devices: 4.59 us -> 19.9 us  [scattered_sum(): lax.all_to_all(parts, axis, split_axis=0, concat_axis=0, tiled=True)]
    all_to_all x1 -> x0, blocking collectives: 12.2 us -> none  [scattered_sum(): lax.all_to_all(parts, axis, split_axis=0, concat_axis=0, tiled=True)]
    all_to_all x2, blocking collectives: 42.8 us -> 32.1 us  [everyone(): return lax.all_to_all(copies, axis, split_axis=0, concat_axis=0, tiled=True)]
    ppermute x0 -> x1, starting transfers between devices: none -> 10.6 us  [shards(): fellow = lax.ppermute(block, 'co', SWAP)]
    all_to_all x1 -> x2, waiting for transfers between devices: 11.9 us -> 20.6 us  [scattered_sum(): lax.all_to_all(parts, axis, split_axis=0, concat_axis=0, tiled=True)]
    all_gather x1 -> x0, waiting for transfers between devices: 6.11 us -> none  [shards(): block = lax.all_gather(block, 'co', axis=0)]
    all_to_all x1 -> x0, starting transfers between devices: 3.69 us -> none  [everyone(): return lax.all_to_all(copies, axis, split_axis=0, concat_axis=0, tiled=True)]
    ppermute x1, waiting for transfers between devices: 3.5 us -> 0.01 us  [shards(): hp = own + lax.ppermute(other, 'yl', SWAP)]
  transfers between devices with their start and end apart: 14 -> 14, of which waited for: 11 -> 11; matrix products, arithmetic and copies ran while one was open for 2% -> 2% of each run, Pallas kernels for 6% -> 0%
where the time goes in v2:
time: 180 us; the launch traced here: 179 us
  starting transfers between devices  79.4 us (44%)
  waiting for transfers between devices  42.3 us (24%)
  blocking collectives  32.1 us (18%)
  Pallas kernels  12 us (7%)
  local copies, waits for them, and re-layouts  4.34 us (2%)
  other arithmetic  4.26 us (2%)
  matrix products  4.14 us (2%)
    all_to_all x2, blocking collectives, everyone(): return lax.all_to_all(copies, axis, split_axis=0, concat_axis=0, tiled=True)  32.1 us
    all_to_all x2, waiting for transfers between devices, scattered_sum(): lax.all_to_all(parts, axis, split_axis=0, concat_axis=0, tiled=True)  20.6 us
    all_to_all x2, starting transfers between devices, scattered_sum(): lax.all_to_all(parts, axis, split_axis=0, concat_axis=0, tiled=True)  19.9 us
    ppermute x4, starting transfers between devices, padded_2(): lax.ppermute(head, axis, [((i + 1) % count, i) for i in range(ends)])  18.1 us
    ppermute x1, starting transfers between devices, shards(): hp = own + lax.ppermute(other, 'yl', SWAP)  16.1 us
    ppermute x4, waiting for transfers between devices, padded_2(): lax.ppermute(head, axis, [((i + 1) % count, i) for i in range(ends)])  12.6 us
    pallas_call x1, Pallas kernels, spd_inverse(): pl.pallas_call(inverse_kernel, out_shape=jax.ShapeDtypeStruct((n, n), jnp...  12 us
    ppermute x1, starting transfers between devices, shards(): fellow = lax.ppermute(block, 'co', SWAP)  10.6 us
  transfers between devices with their start and end apart: 14, of which 11 were waited for; matrix products, arithmetic and copies ran while one was open for 2% of the time, Pallas kernels for 0%

profile of v2, /device:TPU:1, one launch (start us, length us, event | category | flops | bytes accessed | tf_op | source)
XLA Modules:
  0.0 179.1 jit_solution(15758640803088557064)
XLA Ops:
  0.0 1.1 copy.17
  1.1 5.4 %collective-permute-start = (f32[128,512]{0,1:T(8,128)S(1)}, f32[128,512]{0,1:T(8,128)S(1)}, u32[]{:S(2)}, u32[]{:S(2)}) collective-permute-start(f32[128,512]{0,1:T(8,128)S(1)} %copy.17), channel_id=1, source_target_pairs={{0,16},{16,32},{32,48},{48,64},{64,80},{80,96},{96,112},{112,128},... | collective-permute-start | bytes 786440 | tf_op jit(solution)/shard_map/ppermute | solution.py:29
  6.5 11.9 %collective-permute-start.1 = (f32[128,512]{0,1:T(8,128)S(1)}, f32[128,512]{0,1:T(8,128)S(1)}, u32[]{:S(2)}, u32[]{:S(2)}) collective-permute-start(f32[128,512]{0,1:T(8,128)S(1)} %copy.17), channel_id=1, source_target_pairs={{16,0},{32,16},{48,32},{64,48},{80,64},{96,80},{112,96},{128,112},... | collective-permute-start | bytes 786440 | tf_op jit(solution)/shard_map/ppermute | solution.py:31
  20.4 1.9 %collective-permute-start.2 = (f32[128,512]{0,1:T(8,128)S(1)}, f32[128,512]{0,1:T(8,128)S(1)}, u32[]{:S(2)}, u32[]{:S(2)}) collective-permute-start(f32[128,512]{0,1:T(8,128)S(1)} %fusion.29), channel_id=1, source_target_pairs={{0,16},{16,32},{32,48},{48,64},{64,80},{80,96},{96,112},{112,128},... | collective-permute-start | bytes 786440 | tf_op jit(solution)/shard_map/ppermute | solution.py:29
  22.3 2.4 %collective-permute-start.3 = (f32[128,512]{0,1:T(8,128)S(1)}, f32[128,512]{0,1:T(8,128)S(1)}, u32[]{:S(2)}, u32[]{:S(2)}) collective-permute-start(f32[128,512]{0,1:T(8,128)S(1)} %fusion.29), channel_id=1, source_target_pairs={{16,0},{32,16},{48,32},{64,48},{80,64},{96,80},{112,96},{128,112},... | collective-permute-start | bytes 786440 | tf_op jit(solution)/shard_map/ppermute | solution.py:31
  25.6 4.4 %collective-permute-done.3 = f32[128,512]{0,1:T(8,128)S(1)} collective-permute-done((f32[128,512]{0,1:T(8,128)S(1)}, f32[128,512]{0,1:T(8,128)S(1)}, u32[]{:S(2)}, u32[]{:S(2)}) %collective-permute-start.3) | collective-permute-done | bytes 262176 | tf_op jit(solution)/shard_map/ppermute | solution.py:31
  30.2 1.9 %collective-permute-start.4 = (f32[128,512]{0,1:T(8,128)S(1)}, f32[128,512]{0,1:T(8,128)S(1)}, u32[]{:S(2)}, u32[]{:S(2)}) collective-permute-start(f32[128,512]{0,1:T(8,128)S(1)} %fusion.33), channel_id=1, source_target_pairs={{0,16},{16,32},{32,48},{48,64},{64,80},{80,96},{96,112},{112,128},... | collective-permute-start | bytes 786440 | tf_op jit(solution)/shard_map/ppermute | solution.py:29
  32.2 2.4 %collective-permute-start.5 = (f32[128,512]{0,1:T(8,128)S(1)}, f32[128,512]{0,1:T(8,128)S(1)}, u32[]{:S(2)}, u32[]{:S(2)}) collective-permute-start(f32[128,512]{0,1:T(8,128)S(1)} %fusion.33), channel_id=1, source_target_pairs={{16,0},{32,16},{48,32},{64,48},{80,64},{96,80},{112,96},{128,112},... | collective-permute-start | bytes 786440 | tf_op jit(solution)/shard_map/ppermute | solution.py:31
  35.4 4.4 %collective-permute-done.5 = f32[128,512]{0,1:T(8,128)S(1)} collective-permute-done((f32[128,512]{0,1:T(8,128)S(1)}, f32[128,512]{0,1:T(8,128)S(1)}, u32[]{:S(2)}, u32[]{:S(2)}) %collective-permute-start.5) | collective-permute-done | bytes 262176 | tf_op jit(solution)/shard_map/ppermute | solution.py:31
  40.1 1.3 collective-permute-start.6
  41.4 1.3 collective-permute-start.7
  42.8 1.2 collective-permute-done.6
  44.0 3.8 %collective-permute-done.7 = f32[128,384]{0,1:T(8,128)S(1)} collective-permute-done((f32[128,384]{0,1:T(8,128)S(1)}, f32[128,384]{0,1:T(8,128)S(1)}, u32[]{:S(2)}, u32[]{:S(2)}) %collective-permute-start.7) | collective-permute-done | bytes 196640 | tf_op jit(solution)/shard_map/ppermute | solution.py:31
  48.0 0.8 fusion.3
  50.1 1.9 %collective-permute-start.8 = (f32[128,256]{1,0:T(8,128)S(1)}, f32[128,256]{1,0:T(8,128)S(1)}, u32[]{:S(2)}, u32[]{:S(2)}) collective-permute-start(f32[128,256]{1,0:T(8,128)S(1)} %slice_select_fusion.6), channel_id=1, source_target_pairs={{0,16},{16,0},{1,17},{17,1},{2,18},{18,2},{3,19},{19,3},{4,20},{20... | collective-permute-start | bytes 393224 | tf_op jit(solution)/shard_map/ppermute | solution.py:210
  53.7 16.1 %collective-permute-start.9 = (f32[128,256]{1,0:T(8,128)S(1)}, f32[128,256]{1,0:T(8,128)S(1)}, u32[]{:S(2)}, u32[]{:S(2)}) collective-permute-start(f32[128,256]{1,0:T(8,128)S(1)} %slice_select_fusion.5), channel_id=1, source_target_pairs={{0,512},{512,0},{1,513},{513,1},{2,514},{514,2},{3,515},{515,3},{4... | collective-permute-start | bytes 393224 | tf_op jit(solution)/shard_map/ppermute | solution.py:213
  69.8 1.1 fusion.10
  70.9 12.3 %all-to-all-start.1 = ((f32[16,16,128]{2,1,0:T(8,128)}), f32[16,16,128]{2,1,0:T(8,128)S(1)}, u32[]{:S(2)}, u32[]{:S(2)}) async-start(f32[16,16,128]{2,1,0:T(8,128)} %fusion.10), calls=%async_computation.1 | async-start | bytes 262144 | tf_op jit(solution)/shard_map/all_to_all | solution.py:105
  83.2 0.7 add_bitcast_fusion
  83.9 8.7 %all-to-all-done.1 = f32[16,16,128]{2,1,0:T(8,128)S(1)} async-done(((f32[16,16,128]{2,1,0:T(8,128)}), f32[16,16,128]{2,1,0:T(8,128)S(1)}, u32[]{:S(2)}, u32[]{:S(2)}) %all-to-all-start.1) | async-done | bytes 131104 | tf_op jit(solution)/shard_map/all_to_all | solution.py:105
  92.5 7.6 %all-to-all-start = ((f32[16,8,256]{2,1,0:T(8,128)}), f32[16,8,256]{2,1,0:T(8,128)S(1)}, u32[]{:S(2)}, u32[]{:S(2)}) async-start(f32[16,8,256]{2,1,0:T(8,128)} %add_bitcast_fusion), calls=%async_computation | async-start | bytes 262144 | tf_op jit(solution)/shard_map/all_to_all | solution.py:105
  100.2 11.9 %all-to-all-done = f32[16,8,256]{2,1,0:T(8,128)S(1)} async-done(((f32[16,8,256]{2,1,0:T(8,128)}), f32[16,8,256]{2,1,0:T(8,128)S(1)}, u32[]{:S(2)}, u32[]{:S(2)}) %all-to-all-start) | async-done | bytes 131104 | tf_op jit(solution)/shard_map/all_to_all | solution.py:105
  112.5 13.8 %all_to_all.20 = f32[16,32,128]{2,1,0:T(8,128)S(1)} all-to-all(f32[16,32,128]{2,1,0:T(8,128)S(1)} %broadcast_in_dim.97), channel_id=1, replica_groups=mesh['yl'=2,'z'=16,'co'=2,'yh'=4,'x'=4] {'yh','x'}, dimensions={0} | all-to-all | bytes 524288 | tf_op jit(solution)/shard_map/all_to_all | solution.py:101
  126.4 18.2 %all_to_all.21 = f32[16,8,512]{2,1,0:T(8,128)S(1)} all-to-all(f32[16,8,512]{2,1,0:T(8,128)S(1)} %broadcast_in_dim.98), channel_id=1, replica_groups=mesh['yl'=2,'z'=16,'co'=2,'yh'=4,'x'=4] {'z'}, dimensions={0} | all-to-all | bytes 524288 | tf_op jit(solution)/shard_map/all_to_all | solution.py:101
  144.6 2.3 %collective-permute-start.10 = (f32[128,512]{1,0:T(8,128)S(1)}, f32[128,512]{1,0:T(8,128)S(1)}, u32[]{:S(2)}, u32[]{:S(2)}) collective-permute-start(f32[128,512]{1,0:T(8,128)S(1)} %bitcast.93), channel_id=1, source_target_pairs={{0,512},{512,0},{1,513},{513,1},{2,514},{514,2},{3,515},{515,3},{4... | collective-permute-start | bytes 786440 | tf_op jit(solution)/shard_map/ppermute | solution.py:225
  146.9 4.8 %collective-permute-done.10 = f32[128,512]{1,0:T(8,128)S(1)} collective-permute-done((f32[128,512]{1,0:T(8,128)S(1)}, f32[128,512]{1,0:T(8,128)S(1)}, u32[]{:S(2)}, u32[]{:S(2)}) %collective-permute-start.10) | collective-permute-done | bytes 262176 | tf_op jit(solution)/shard_map/ppermute | solution.py:225
  151.8 10.6 %collective-permute-start.11 = (f32[256,512]{1,0:T(8,128)S(1)}, f32[256,512]{1,0:T(8,128)S(1)}, u32[]{:S(2)}, u32[]{:S(2)}) collective-permute-start(f32[256,512]{1,0:T(8,128)S(1)} %pad_maximum_fusion), channel_id=1, source_target_pairs={{0,16},{16,0},{1,17},{17,1},{2,18},{18,2},{3,19},{19,3},{4,20},{20... | collective-permute-start | bytes 1572872 | tf_op jit(solution)/shard_map/ppermute | solution.py:226
  162.4 1.3 collective-permute-done.11
  163.8 0.8 slice_select_fusion.4
  164.6 12.0 %spd_inverse.1 = f32[256,256]{1,0:T(8,128)} custom-call(f32[256,256]{1,0:T(8,128)} %get-tuple-element.7.s_ref, f32[1,256]{1,0:T(1,128)} %bitcast.95), custom_call_target="tpu_custom_call" | custom-call | flops 67108864 | bytes 524288 | tf_op jit(solution)/shard_map/spd_inverse/pallas_call | solution.py:89
  176.6 1.3 fusion.74
  177.9 1.2 convolution_subtract_fusion
  (77 shorter events, 7.6 us)
Async XLA Ops:
  0.0 18.6 %copy-start.3 = (f32[8192]{0:T(1024)S(1)}, f32[8192]{0:T(1024)}, u32[]{:S(2)}) copy-start(f32[8192]{0:T(1024)} %param.9) | copy-start | bytes 98308
  1.1 17.5 %copy-start.2 = (f32[8192]{0:T(1024)S(1)}, f32[8192]{0:T(1024)}, u32[]{:S(2)}) copy-start(f32[8192]{0:T(1024)} %param.8) | copy-start | bytes 98308
  1.1 19.1 %collective-permute-start = (f32[128,512]{0,1:T(8,128)S(1)}, f32[128,512]{0,1:T(8,128)S(1)}, u32[]{:S(2)}, u32[]{:S(2)}) collective-permute-start(f32[128,512]{0,1:T(8,128)S(1)} %copy.17), channel_id=1, source_target_pairs={{0,16},{16,32},{32,48},{48,64},{64,80},{80,96},{96,112},{112,128},... | collective-permute-start | bytes 786440 | tf_op jit(solution)/shard_map/ppermute | solution.py:29
  6.5 13.7 %collective-permute-start.1 = (f32[128,512]{0,1:T(8,128)S(1)}, f32[128,512]{0,1:T(8,128)S(1)}, u32[]{:S(2)}, u32[]{:S(2)}) collective-permute-start(f32[128,512]{0,1:T(8,128)S(1)} %copy.17), channel_id=1, source_target_pairs={{16,0},{32,16},{48,32},{64,48},{80,64},{96,80},{112,96},{128,112},... | collective-permute-start | bytes 786440 | tf_op jit(solution)/shard_map/ppermute | solution.py:31
  18.6 0.8 copy-start.1
  18.7 0.8 copy-start
  20.4 5.2 %collective-permute-start.2 = (f32[128,512]{0,1:T(8,128)S(1)}, f32[128,512]{0,1:T(8,128)S(1)}, u32[]{:S(2)}, u32[]{:S(2)}) collective-permute-start(f32[128,512]{0,1:T(8,128)S(1)} %fusion.29), channel_id=1, source_target_pairs={{0,16},{16,32},{32,48},{48,64},{64,80},{80,96},{96,112},{112,128},... | collective-permute-start | bytes 786440 | tf_op jit(solution)/shard_map/ppermute | solution.py:29
  22.3 7.7 %collective-permute-start.3 = (f32[128,512]{0,1:T(8,128)S(1)}, f32[128,512]{0,1:T(8,128)S(1)}, u32[]{:S(2)}, u32[]{:S(2)}) collective-permute-start(f32[128,512]{0,1:T(8,128)S(1)} %fusion.29), channel_id=1, source_target_pairs={{16,0},{32,16},{48,32},{64,48},{80,64},{96,80},{112,96},{128,112},... | collective-permute-start | bytes 786440 | tf_op jit(solution)/shard_map/ppermute | solution.py:31
  30.2 5.2 %collective-permute-start.4 = (f32[128,512]{0,1:T(8,128)S(1)}, f32[128,512]{0,1:T(8,128)S(1)}, u32[]{:S(2)}, u32[]{:S(2)}) collective-permute-start(f32[128,512]{0,1:T(8,128)S(1)} %fusion.33), channel_id=1, source_target_pairs={{0,16},{16,32},{32,48},{48,64},{64,80},{80,96},{96,112},{112,128},... | collective-permute-start | bytes 786440 | tf_op jit(solution)/shard_map/ppermute | solution.py:29
  32.2 7.7 %collective-permute-start.5 = (f32[128,512]{0,1:T(8,128)S(1)}, f32[128,512]{0,1:T(8,128)S(1)}, u32[]{:S(2)}, u32[]{:S(2)}) collective-permute-start(f32[128,512]{0,1:T(8,128)S(1)} %fusion.33), channel_id=1, source_target_pairs={{16,0},{32,16},{48,32},{64,48},{80,64},{96,80},{112,96},{128,112},... | collective-permute-start | bytes 786440 | tf_op jit(solution)/shard_map/ppermute | solution.py:31
  40.1 3.9 %collective-permute-start.6 = (f32[128,384]{0,1:T(8,128)S(1)}, f32[128,384]{0,1:T(8,128)S(1)}, u32[]{:S(2)}, u32[]{:S(2)}) collective-permute-start(f32[128,384]{0,1:T(8,128)S(1)} %get-tuple-element.26), channel_id=1, source_target_pairs={{0,1},{1,2},{2,3},{3,4},{4,5},{5,6},{6,7},{7,8},{8,9},{9,10},{10,1... | collective-permute-start | bytes 589832 | tf_op jit(solution)/shard_map/ppermute | solution.py:29
  41.4 6.4 %collective-permute-start.7 = (f32[128,384]{0,1:T(8,128)S(1)}, f32[128,384]{0,1:T(8,128)S(1)}, u32[]{:S(2)}, u32[]{:S(2)}) collective-permute-start(f32[128,384]{0,1:T(8,128)S(1)} %get-tuple-element.27), channel_id=1, source_target_pairs={{1,0},{2,1},{3,2},{4,3},{5,4},{6,5},{7,6},{8,7},{9,8},{10,9},{11,1... | collective-permute-start | bytes 589832 | tf_op jit(solution)/shard_map/ppermute | solution.py:31
  50.1 3.2 %collective-permute-start.8 = (f32[128,256]{1,0:T(8,128)S(1)}, f32[128,256]{1,0:T(8,128)S(1)}, u32[]{:S(2)}, u32[]{:S(2)}) collective-permute-start(f32[128,256]{1,0:T(8,128)S(1)} %slice_select_fusion.6), channel_id=1, source_target_pairs={{0,16},{16,0},{1,17},{17,1},{2,18},{18,2},{3,19},{19,3},{4,20},{20... | collective-permute-start | bytes 393224 | tf_op jit(solution)/shard_map/ppermute | solution.py:210
  52.0 0.7 copy-start.4
  53.7 29.5 %collective-permute-start.9 = (f32[128,256]{1,0:T(8,128)S(1)}, f32[128,256]{1,0:T(8,128)S(1)}, u32[]{:S(2)}, u32[]{:S(2)}) collective-permute-start(f32[128,256]{1,0:T(8,128)S(1)} %slice_select_fusion.5), channel_id=1, source_target_pairs={{0,512},{512,0},{1,513},{513,1},{2,514},{514,2},{3,515},{515,3},{4... | collective-permute-start | bytes 393224 | tf_op jit(solution)/shard_map/ppermute | solution.py:213
  70.9 21.7 %all-to-all-start.1 = ((f32[16,16,128]{2,1,0:T(8,128)}), f32[16,16,128]{2,1,0:T(8,128)S(1)}, u32[]{:S(2)}, u32[]{:S(2)}) async-start(f32[16,16,128]{2,1,0:T(8,128)} %fusion.10), calls=%async_computation.1 | async-start | bytes 262144 | tf_op jit(solution)/shard_map/all_to_all | solution.py:105
  92.5 19.6 %all-to-all-start = ((f32[16,8,256]{2,1,0:T(8,128)}), f32[16,8,256]{2,1,0:T(8,128)S(1)}, u32[]{:S(2)}, u32[]{:S(2)}) async-start(f32[16,8,256]{2,1,0:T(8,128)} %add_bitcast_fusion), calls=%async_computation | async-start | bytes 262144 | tf_op jit(solution)/shard_map/all_to_all | solution.py:105
  144.6 7.1 %collective-permute-start.10 = (f32[128,512]{1,0:T(8,128)S(1)}, f32[128,512]{1,0:T(8,128)S(1)}, u32[]{:S(2)}, u32[]{:S(2)}) collective-permute-start(f32[128,512]{1,0:T(8,128)S(1)} %bitcast.93), channel_id=1, source_target_pairs={{0,512},{512,0},{1,513},{513,1},{2,514},{514,2},{3,515},{515,3},{4... | collective-permute-start | bytes 786440 | tf_op jit(solution)/shard_map/ppermute | solution.py:225
  151.8 12.0 %collective-permute-start.11 = (f32[256,512]{1,0:T(8,128)S(1)}, f32[256,512]{1,0:T(8,128)S(1)}, u32[]{:S(2)}, u32[]{:S(2)}) collective-permute-start(f32[256,512]{1,0:T(8,128)S(1)} %pad_maximum_fusion), channel_id=1, source_target_pairs={{0,16},{16,0},{1,17},{17,1},{2,18},{18,2},{3,19},{19,3},{4,20},{20... | collective-permute-start | bytes 1572872 | tf_op jit(solution)/shard_map/ppermute | solution.py:226

commit v3 on v1

--- a/solution.py
+++ b/solution.py
@@ -96,6 +96,90 @@
     )(s, var.reshape(1, n))
 
 
+def footprint_kernel(start_ref, site_ref, keep_ref, west_ref, east_ref, south_ref, north_ref, cov_ref,
+                     spread_ref, rows_ref, cols_ref):
+    nobs = site_ref.shape[0]
+    bands = keep_ref.shape[0]
+    chunk = 32
+    lane = lax.broadcasted_iota(jnp.int32, (chunk, MERIDIAN_TOTAL), 1)
+
+    def footprint(first, count, store):
+        total = count + 2 * STEPS
+
+        def coeff(ref, t):
+            band = first + (t - STEPS)
+            inside = (band >= 0) & (band < bands)
+            line = ref[pl.ds(jnp.clip(band, 0, bands - 1), 1), :]
+            return jnp.where(inside, line, 0.0)
+
+        def body(i, carry):
+            at = pl.multiple_of(i * chunk, chunk)
+            site = site_ref[pl.ds(at, chunk), :]
+            v = [
+                (site == (first + (t - STEPS)) * MERIDIAN_TOTAL + lane).astype(jnp.float32)
+                for t in range(total)
+            ]
+            for step in range(STEPS):
+                low, high = (step + 1, total - step - 1)
+                new = []
+                for t in range(low, high):
+                    w = coeff(keep_ref, t) * v[t]
+                    w = w + pltpu.roll(coeff(west_ref, t) * v[t], MERIDIAN_TOTAL - 1, 1)
+                    w = w + pltpu.roll(coeff(east_ref, t) * v[t], 1, 1)
+                    w = w + coeff(south_ref, t + 1) * v[t + 1]
+                    w = w + coeff(north_ref, t - 1) * v[t - 1]
+                    new.append(w)
+                v = [None] * low + new + [None] * (total - high)
+            store(at, v[STEPS : STEPS + count])
+            return carry
+
+        lax.fori_loop(0, nobs // chunk, body, 0)
+
+    def store_rows(at, v):
+        rows_ref[pl.ds(at, chunk), 0:MERIDIAN_TOTAL] = v[0]
+
+    def store_cols(at, v):
+        for b, w in enumerate(v):
+            spread_ref[pl.ds(at, chunk), b * MERIDIAN_TOTAL : (b + 1) * MERIDIAN_TOTAL] = w
+
+    footprint(start_ref[0], cov_ref.shape[0] // MERIDIAN_TOTAL, store_rows)
+    footprint(start_ref[1], cov_ref.shape[1] // MERIDIAN_TOTAL, store_cols)
+    cov = cov_ref[...]
+    near = rows_ref[:, 0:MERIDIAN_TOTAL]
+    rows_ref[...] = jnp.dot(near, cov, precision=HIGHEST, preferred_element_type=jnp.float32)
+    cols_ref[...] = lax.dot_general(
+        spread_ref[...], cov, (((1,), (1,)), ((), ())), precision=HIGHEST, preferred_element_type=jnp.float32
+    )
+
+
+def footprints(covariance, starts, site, lon_speed, lat_speed, lon_sign, lat_sign):
+    rows_dev, cols_dev = covariance.shape
+    nobs = site.shape[0]
+    bands = lon_speed.shape[0] // MERIDIAN_TOTAL
+
+    def grid_of(field):
+        return field.reshape(bands, MERIDIAN_TOTAL)
+
+    cu, cv = grid_of(lon_speed), grid_of(lat_speed)
+    su, sv = grid_of(lon_sign) > 0, grid_of(lat_sign) > 0
+    fields = [
+        1.0 - cu - cv,
+        jnp.where(su, cu, 0.0),
+        jnp.where(su, 0.0, cu),
+        jnp.where(sv, cv, 0.0),
+        jnp.where(sv, 0.0, cv),
+    ]
+    shapes = [(nobs, cols_dev), (nobs, cols_dev), (nobs, rows_dev)]
+    return pl.pallas_call(
+        footprint_kernel,
+        out_shape=[jax.ShapeDtypeStruct(shape, jnp.float32) for shape in shapes],
+        in_specs=[pl.BlockSpec(memory_space=pltpu.SMEM)] + [pl.BlockSpec(memory_space=pltpu.VMEM)] * 7,
+        out_specs=[pl.BlockSpec(memory_space=pltpu.VMEM)] * 3,
+        cost_estimate=pl.CostEstimate(flops=400 * 1000 * 1000, bytes_accessed=2000000, transcendentals=0),
+        name="footprints",
+    )(starts, site, *fields, covariance)
+
+
 def everyone(chunk, axis):
     copies = jnp.broadcast_to(chunk, (lax.axis_size(axis), *chunk.shape))
     return lax.all_to_all(copies, axis, split_axis=0, concat_axis=0, tiled=True)
@@ -121,10 +205,9 @@
     )
 
 
-def transported(covariance, lon_speed, lat_speed, lon_sign, lat_sign, row_start, col_start):
-    rows_dev, cols_dev = covariance.shape
+def row_transported(cells, lon_speed, lat_speed, lon_sign, lat_sign, row_start):
+    rows_dev, width = cells.shape
     row_bands = rows_dev // MERIDIAN_TOTAL
-    col_bands = cols_dev // MERIDIAN_TOTAL
 
     def row_coeff(field):
         return lax.dynamic_slice_in_dim(field, row_start, rows_dev).reshape(
@@ -133,16 +216,19 @@
 
     row_cu, row_cv = (row_coeff(lon_speed), row_coeff(lat_speed))
     row_su, row_sv = (row_coeff(lon_sign), row_coeff(lat_sign))
-    segment_patch = covariance
     for step in range(STEPS):
-        padded = padded_2(segment_patch, ((ROW, 0),), MERIDIAN_TOTAL)
-        shaped = padded.reshape(row_bands + 2, MERIDIAN_TOTAL, cols_dev)
-        segment_patch = advect(
+        padded = padded_2(cells, ((ROW, 0),), MERIDIAN_TOTAL)
+        shaped = padded.reshape(row_bands + 2, MERIDIAN_TOTAL, width)
+        cells = advect(
             shaped[1:-1], shaped[:-2], shaped[2:], row_cu, row_cv, row_su, row_sv, 0
         )
-        segment_patch = segment_patch.reshape(rows_dev, cols_dev)
+        cells = cells.reshape(rows_dev, width)
+    return cells
+
+
+def col_fields(lon_speed, lat_speed, lon_sign, lat_sign, col_start, cols_dev):
     margin = STEPS * MERIDIAN_TOTAL
-    total_bands = col_bands + 2 * STEPS
+    total_bands = cols_dev // MERIDIAN_TOTAL + 2 * STEPS
 
     def wide_coeff(field):
         extended = jnp.pad(field, (margin, margin))
@@ -150,35 +236,26 @@
             1, total_bands, MERIDIAN_TOTAL
         )
 
-    col_cu, col_cv = (wide_coeff(lon_speed), wide_coeff(lat_speed))
-    col_su, col_sv = (wide_coeff(lon_sign), wide_coeff(lat_sign))
     band_ids = col_start // MERIDIAN_TOTAL - STEPS + jnp.arange(total_bands, dtype=jnp.int32)
     inside = (
         ((band_ids >= 0) & (band_ids < PARALLEL_STRIPS))
         .astype(jnp.float32)
         .reshape(1, total_bands, 1)
     )
-    padded = padded_2(segment_patch, ((COL, 1),), margin)
-    current = padded.reshape(rows_dev, total_bands, MERIDIAN_TOTAL)
-    offset = 0
+    return [wide_coeff(field) for field in (lon_speed, lat_speed, lon_sign, lat_sign)] + [inside]
+
+
+def col_transported(padded, fields):
+    rows, width = padded.shape
+    current = padded.reshape(rows, width // MERIDIAN_TOTAL, MERIDIAN_TOTAL)
     for step in range(STEPS):
         count = current.shape[1]
-        low, high = (offset + 1, offset + count - 1)
+        low, high = (step + 1, step + count - 1)
+        cu, cv, su, sv, inside = (field[:, low:high] for field in fields)
         current = (
-            advect(
-                current[:, 1:-1],
-                current[:, :-2],
-                current[:, 2:],
-                col_cu[:, low:high],
-                col_cv[:, low:high],
-                col_su[:, low:high],
-                col_sv[:, low:high],
-                1,
-            )
-            * inside[:, low:high]
-        )
-        offset = offset + 1
-    return current.reshape(rows_dev, cols_dev)
+            advect(current[:, 1:-1], current[:, :-2], current[:, 2:], cu, cv, su, sv, 1) * inside
+        )
+    return current.reshape(rows, -1)
 
 
 def shards(
@@ -187,41 +264,47 @@
     rows_dev, cols_dev = covariance.shape
     nobs = measurement_site_position.shape[0]
     lat_half, core = lax.axis_index("yl"), lax.axis_index("co")
-    row_start = lax.axis_index(ROW) * rows_dev
-    col_start = lax.axis_index(COL) * cols_dev
+    row, col = lax.axis_index(ROW), lax.axis_index(COL)
+    row_start, col_start = row * rows_dev, col * cols_dev
+    margin = STEPS * MERIDIAN_TOTAL
     dot = functools.partial(
         lax.dot_general, precision=HIGHEST, preferred_element_type=jnp.float32
     )
-    forecast = transported(
-        covariance, lon_speed, lat_speed, lon_sign, lat_sign, row_start, col_start
-    )
+    winds = (lon_speed, lat_speed, lon_sign, lat_sign)
     site = measurement_site_position[:, None]
-
-    def picks(start, size):
-        cell = start + lax.broadcasted_iota(jnp.int32, (nobs, size), 1)
-        return (cell == site).astype(jnp.float32)
-
-    pht = dot(picks(col_start, cols_dev), forecast, (((1,), (1,)), ((), ())))
+    starts = jnp.stack([row_start, col_start]) // MERIDIAN_TOTAL
+    spread, hp, pht = footprints(covariance, starts, site, *winds)
+
+    own, other = halves(hp, 0, core)
+    fellow = lax.ppermute(other, "co", SWAP)
     sides = lax.axis_size(COL)
     pht = scattered_sum(pht.reshape(sides, nobs // sides, rows_dev), COL)
-
-    half = cols_dev // 2
-    own, other = halves(forecast, 1, core)
-    both = joined(own, lax.ppermute(other, "co", SWAP), 0, core)
-    hp = dot(picks(row_start - core * rows_dev, 2 * rows_dev), both, (((1,), (0,)), ((), ())))
-    own, other = halves(hp, 0, lat_half)
+    own, other = halves(own + fellow, 0, lat_half)
     hp = own + lax.ppermute(other, "yl", SWAP)
     deep = lax.axis_size("z")
-    hp = scattered_sum(hp.reshape(deep, nobs // 2 // deep, half), "z")
-
-    hpht = dot(hp, picks(col_start + core * half, half), (((1,), (1,)), ((), ())))
-    hpht = jnp.sum(everyone(hpht, COL), axis=0)
+    hp = scattered_sum(hp.reshape(deep, nobs // 4 // deep, cols_dev), "z")
+
+    forecast = row_transported(
+        jnp.concatenate([covariance, pht.T], axis=1), *winds, row_start
+    )
+    pht = forecast[:, cols_dev:].T
+    fields = col_fields(*winds, col_start, cols_dev)
+    forecast = col_transported(padded_2(forecast[:, :cols_dev], ((COL, 1),), margin), fields)
+
+    hpht = dot(hp, spread, (((1,), (1,)), ((), ())))
+    found = everyone(jnp.concatenate([hp, hpht], axis=1), COL)
+    hpht = jnp.sum(found[:, :, cols_dev:], axis=0)
+    near = lax.dynamic_slice_in_dim(
+        jnp.pad(found[:, :, :cols_dev], ((1, 1), (0, 0), (0, 0))), col, 3
+    )
+    hp = jnp.concatenate([near[0, :, cols_dev - margin :], near[1], near[2, :, :margin]], axis=1)
+    hp = col_transported(hp, fields)
+
     block = jnp.concatenate([hp, hpht], axis=1)
-    block = everyone(block, "z").reshape(nobs // 2, half + nobs)
+    block = everyone(block, "z").reshape(nobs // 4, cols_dev + nobs)
     block = joined(block, lax.ppermute(block, "yl", SWAP), 0, lat_half)
-    block = lax.all_gather(block, "co", axis=0)
-    hp = jnp.concatenate([block[0, :, :half], block[1, :, :half]], axis=1)
-    hpht = block[0, :, half:] + block[1, :, half:]
+    block = joined(block, lax.ppermute(block, "co", SWAP), 0, core)
+    hp, hpht = block[:, :cols_dev], block[:, cols_dev:]
 
     inverse = spd_inverse(hpht, obs_var)
     pht = everyone(pht, COL).reshape(nobs, rows_dev)

time: 199 us -> 174 us (0.87); the launches traced: 196 us -> 173 us
  blocking collectives: 55 us -> 0 us
  starting transfers between devices: 58 us -> 99.7 us
  between operations: 13.9 us -> 0.65 us
  Pallas kernels: 12 us -> 20.3 us
  waiting for transfers between devices: 41.8 us -> 33.6 us
  local copies, waits for them, and re-layouts: 4.99 us -> 8.39 us
    all_to_all x3 -> x0, blocking collectives: 55 us -> none  [the longest x2 42.8 us: everyone(): return lax.all_to_all(copies, axis, split_axis=0, concat_axis=0, tiled=True)]
    all_to_all x1 -> x3, starting transfers between devices: 3.69 us -> 28 us  [everyone(): return lax.all_to_all(copies, axis, split_axis=0, concat_axis=0, tiled=True)]
    all_to_all x1 -> x2, starting transfers between devices: 4.59 us -> 24.9 us  [scattered_sum(): lax.all_to_all(parts, axis, split_axis=0, concat_axis=0, tiled=True)]
    all_to_all x1 -> x3, waiting for transfers between devices: 0.01 us -> 17 us  [everyone(): return lax.all_to_all(copies, axis, split_axis=0, concat_axis=0, tiled=True)]
    ppermute x1 -> x2, starting transfers between devices: 1.92 us -> 18 us  [the longest x1 9.46 us: shards(): fellow = lax.ppermute(other, 'co', SWAP)]
    ppermute x1, starting transfers between devices: 16.1 us -> 1.92 us  [shards(): hp = own + lax.ppermute(other, 'yl', SWAP)]
    all_to_all x1 -> x2, waiting for transfers between devices: 11.9 us -> 0.01 us  [scattered_sum(): lax.all_to_all(parts, axis, split_axis=0, concat_axis=0, tiled=True)]
    ppermute x4, waiting for transfers between devices: 12.6 us -> 3.4 us  [padded_2(): lax.ppermute(head, axis, [((i + 1) % count, i) for i in range(ends)])]
  transfers between devices with their start and end apart: 14 -> 17, of which waited for: 11 -> 8; matrix products, arithmetic and copies ran while one was open for 2% -> 5% of each run, Pallas kernels for 6% -> 7%
where the time goes in v3:
time: 174 us; the launch traced here: 173 us
  starting transfers between devices  99.7 us (57%)
  waiting for transfers between devices  33.6 us (19%)
  Pallas kernels  20.3 us (12%)
  local copies, waits for them, and re-layouts  8.39 us (5%)
  other arithmetic  6.97 us (4%)
  matrix products  2.99 us (2%)
    all_to_all x3, starting transfers between devices, everyone(): return lax.all_to_all(copies, axis, split_axis=0, concat_axis=0, tiled=True)  28 us
    all_to_all x2, starting transfers between devices, scattered_sum(): lax.all_to_all(parts, axis, split_axis=0, concat_axis=0, tiled=True)  24.9 us
    all_to_all x3, waiting for transfers between devices, everyone(): return lax.all_to_all(copies, axis, split_axis=0, concat_axis=0, tiled=True)  17 us
    ppermute x4, starting transfers between devices, padded_2(): lax.ppermute(head, axis, [((i + 1) % count, i) for i in range(ends)])  13.8 us
    pallas_call x1, Pallas kernels, spd_inverse(): pl.pallas_call(inverse_kernel, out_shape=jax.ShapeDtypeStruct((n, n), jnp...  12.1 us
    ppermute x4, starting transfers between devices, padded_2(): lax.ppermute(tail, axis, [(i, (i + 1) % count) for i in range(ends)])  11.1 us
    ppermute x1, starting transfers between devices, shards(): fellow = lax.ppermute(other, 'co', SWAP)  9.46 us
    ppermute x1, starting transfers between devices, shards(): block = joined(block, lax.ppermute(block, 'co', SWAP), 0, core)  8.57 us
  transfers between devices with their start and end apart: 17, of which 8 were waited for; matrix products, arithmetic and copies ran while one was open for 5% of the time, Pallas kernels for 7%

profile of v3, /device:TPU:1, one launch (start us, length us, event | category | flops | bytes accessed | tf_op | source)
XLA Modules:
  0.0 172.7 jit_solution(4715419435582590638)
XLA Ops:
  0.7 0.8 copy.9.site_ref
  3.4 8.3 %footprints.1 = (f32[256,512]{1,0:T(8,128)}, f32[256,512]{1,0:T(8,128)}, f32[256,128]{1,0:T(8,128)}) custom-call(s32[2]{0:T(128)} %and_select_fusion.start_ref, s32[256,1]{1,0:T(8,128)} %copy.9.site_ref, f32[64,128]{1,0:T(8,128)} %get-tuple-element.54.keep_ref, f32[64,128]{1,0:T(8,128)} %get-tuple-element.55.west_ref, f32[64,128]{1,0:T(8,128)} %get-tuple-element.66.east_ref, ...), custom_call_target="tpu_custom_call" | custom-call | flops 400000000 | bytes 2000000 | tf_op jit(solution)/shard_map/footprints/pallas_call | solution.py:173
  11.7 10.2 %all-to-all-start = ((f32[16,16,128]{2,1,0:T(8,128)}), f32[16,16,128]{2,1,0:T(8,128)S(1)}, u32[]{:S(2)}, u32[]{:S(2)}) async-start(f32[16,16,128]{2,1,0:T(8,128)} %bitcast.112), calls=%async_computation | async-start | bytes 262144 | tf_op jit(solution)/shard_map/all_to_all | solution.py:189
  21.9 1.1 slice_select_fusion.3
  23.0 9.5 %collective-permute-start.8 = (f32[128,512]{1,0:T(8,128)S(1)}, f32[128,512]{1,0:T(8,128)S(1)}, u32[]{:S(2)}, u32[]{:S(2)}) collective-permute-start(f32[128,512]{1,0:T(8,128)S(1)} %slice_select_fusion.3), channel_id=1, source_target_pairs={{0,16},{16,0},{1,17},{17,1},{2,18},{18,2},{3,19},{19,3},{4,20},{20... | collective-permute-start | bytes 786440 | tf_op jit(solution)/shard_map/ppermute | solution.py:279
  33.5 8.2 %collective-permute-start.1 = (f32[128,528]{0,1:T(8,128)S(1)}, f32[128,528]{0,1:T(8,128)S(1)}, u32[]{:S(2)}, u32[]{:S(2)}) collective-permute-start(f32[128,528]{0,1:T(8,128)S(1)} %get-tuple-element.41), channel_id=1, source_target_pairs={{16,0},{32,16},{48,32},{64,48},{80,64},{96,80},{112,96},{128,112},... | collective-permute-start | bytes 811016 | tf_op jit(solution)/shard_map/ppermute | solution.py:31
  41.6 1.9 %collective-permute-start = (f32[128,528]{0,1:T(8,128)S(1)}, f32[128,528]{0,1:T(8,128)S(1)}, u32[]{:S(2)}, u32[]{:S(2)}) collective-permute-start(f32[128,528]{0,1:T(8,128)S(1)} %get-tuple-element.41), channel_id=1, source_target_pairs={{0,16},{16,32},{32,48},{48,64},{64,80},{80,96},{96,112},{112,128},... | collective-permute-start | bytes 811016 | tf_op jit(solution)/shard_map/ppermute | solution.py:29
  43.7 0.9 copy-done.1
  44.7 1.9 %collective-permute-start.9 = (f32[64,512]{1,0:T(8,128)S(1)}, f32[64,512]{1,0:T(8,128)S(1)}, u32[]{:S(2)}, u32[]{:S(2)}) collective-permute-start(f32[64,512]{1,0:T(8,128)S(1)} %slice_select_fusion.4), channel_id=1, source_target_pairs={{0,512},{512,0},{1,513},{513,1},{2,514},{514,2},{3,515},{515,3},{4... | collective-permute-start | bytes 393224 | tf_op jit(solution)/shard_map/ppermute | solution.py:283
  46.8 3.6 %collective-permute-done.9 = f32[64,512]{1,0:T(8,128)S(1)} collective-permute-done((f32[64,512]{1,0:T(8,128)S(1)}, f32[64,512]{1,0:T(8,128)S(1)}, u32[]{:S(2)}, u32[]{:S(2)}) %collective-permute-start.9) | collective-permute-done | bytes 131104 | tf_op jit(solution)/shard_map/ppermute | solution.py:283
  51.1 14.7 %all-to-all-start.1 = ((f32[16,4,512]{2,1,0:T(4,128)}), f32[16,4,512]{2,1,0:T(4,128)S(1)}, u32[]{:S(2)}, u32[]{:S(2)}) async-start(f32[16,4,512]{2,1,0:T(4,128)} %reshape.159), calls=%async_computation.1 | async-start | bytes 262144 | tf_op jit(solution)/shard_map/all_to_all | solution.py:189
  66.1 4.1 %collective-permute-start.2 = (f32[128,528]{0,1:T(8,128)S(1)}, f32[128,528]{0,1:T(8,128)S(1)}, u32[]{:S(2)}, u32[]{:S(2)}) collective-permute-start(f32[128,528]{0,1:T(8,128)S(1)} %fusion.18), channel_id=1, source_target_pairs={{0,16},{16,32},{32,48},{48,64},{64,80},{80,96},{96,112},{112,128},... | collective-permute-start | bytes 811016 | tf_op jit(solution)/shard_map/ppermute | solution.py:29
  70.2 1.9 %collective-permute-start.3 = (f32[128,528]{0,1:T(8,128)S(1)}, f32[128,528]{0,1:T(8,128)S(1)}, u32[]{:S(2)}, u32[]{:S(2)}) collective-permute-start(f32[128,528]{0,1:T(8,128)S(1)} %fusion.18), channel_id=1, source_target_pairs={{16,0},{32,16},{48,32},{64,48},{80,64},{96,80},{112,96},{128,112},... | collective-permute-start | bytes 811016 | tf_op jit(solution)/shard_map/ppermute | solution.py:31
  72.5 3.8 %collective-permute-done.2 = f32[128,528]{0,1:T(8,128)S(1)} collective-permute-done((f32[128,528]{0,1:T(8,128)S(1)}, f32[128,528]{0,1:T(8,128)S(1)}, u32[]{:S(2)}, u32[]{:S(2)}) %collective-permute-start.2) | collective-permute-done | bytes 270368 | tf_op jit(solution)/shard_map/ppermute | solution.py:29
  76.3 2.7 %collective-permute-done.3 = f32[128,528]{0,1:T(8,128)S(1)} collective-permute-done((f32[128,528]{0,1:T(8,128)S(1)}, f32[128,528]{0,1:T(8,128)S(1)}, u32[]{:S(2)}, u32[]{:S(2)}) %collective-permute-start.3) | collective-permute-done | bytes 270368 | tf_op jit(solution)/shard_map/ppermute | solution.py:31
  79.2 1.9 %collective-permute-start.4 = (f32[128,528]{0,1:T(8,128)S(1)}, f32[128,528]{0,1:T(8,128)S(1)}, u32[]{:S(2)}, u32[]{:S(2)}) collective-permute-start(f32[128,528]{0,1:T(8,128)S(1)} %fusion.22), channel_id=1, source_target_pairs={{0,16},{16,32},{32,48},{48,64},{64,80},{80,96},{96,112},{112,128},... | collective-permute-start | bytes 811016 | tf_op jit(solution)/shard_map/ppermute | solution.py:29
  81.1 2.4 %collective-permute-start.5 = (f32[128,528]{0,1:T(8,128)S(1)}, f32[128,528]{0,1:T(8,128)S(1)}, u32[]{:S(2)}, u32[]{:S(2)}) collective-permute-start(f32[128,528]{0,1:T(8,128)S(1)} %fusion.22), channel_id=1, source_target_pairs={{16,0},{32,16},{48,32},{64,48},{80,64},{96,80},{112,96},{128,112},... | collective-permute-start | bytes 811016 | tf_op jit(solution)/shard_map/ppermute | solution.py:31
  83.9 0.9 copy-done.2
  86.0 3.5 %all-to-all-start.2 = ((f32[16,4,768]{2,1,0:T(4,128)}), f32[16,4,768]{2,1,0:T(4,128)S(1)}, u32[]{:S(2)}, u32[]{:S(2)}) async-start(f32[16,4,768]{2,1,0:T(4,128)} %broadcast_in_dim.151), calls=%async_computation.2 | async-start | bytes 393216 | tf_op jit(solution)/shard_map/all_to_all | solution.py:185
  89.8 3.2 %collective-permute-start.6 = (f32[128,384]{0,1:T(8,128)S(1)}, f32[128,384]{0,1:T(8,128)S(1)}, u32[]{:S(2)}, u32[]{:S(2)}) collective-permute-start(f32[128,384]{0,1:T(8,128)S(1)} %get-tuple-element.31), channel_id=1, source_target_pairs={{0,1},{1,2},{2,3},{3,4},{4,5},{5,6},{6,7},{7,8},{8,9},{9,10},{10,1... | collective-permute-start | bytes 589832 | tf_op jit(solution)/shard_map/ppermute | solution.py:29
  93.0 1.3 collective-permute-start.7
  94.3 6.2 %all-to-all-done.2 = f32[16,4,768]{2,1,0:T(4,128)S(1)} async-done(((f32[16,4,768]{2,1,0:T(4,128)}), f32[16,4,768]{2,1,0:T(4,128)S(1)}, u32[]{:S(2)}, u32[]{:S(2)}) %all-to-all-start.2) | async-done | bytes 196640 | tf_op jit(solution)/shard_map/all_to_all | solution.py:185
  103.0 10.0 %all-to-all-start.3 = ((f32[16,4,768]{2,1,0:T(4,128)}), f32[16,4,768]{2,1,0:T(4,128)S(1)}, u32[]{:S(2)}, u32[]{:S(2)}) async-start(f32[16,4,768]{2,1,0:T(4,128)} %broadcast_in_dim.158), calls=%async_computation.3 | async-start | bytes 393216 | tf_op jit(solution)/shard_map/all_to_all | solution.py:185
  113.0 0.8 fusion.4
  114.5 10.8 %all-to-all-done.3 = f32[16,4,768]{2,1,0:T(4,128)S(1)} async-done(((f32[16,4,768]{2,1,0:T(4,128)}), f32[16,4,768]{2,1,0:T(4,128)S(1)}, u32[]{:S(2)}, u32[]{:S(2)}) %all-to-all-start.3) | async-done | bytes 196640 | tf_op jit(solution)/shard_map/all_to_all | solution.py:185
  125.9 14.5 %all-to-all-start.4 = ((f32[16,16,128]{2,1,0:T(8,128)}), f32[16,16,128]{2,1,0:T(8,128)S(1)}, u32[]{:S(2)}, u32[]{:S(2)}) async-start(f32[16,16,128]{2,1,0:T(8,128)} %broadcast_in_dim.159), calls=%async_computation.4 | async-start | bytes 262144 | tf_op jit(solution)/shard_map/all_to_all | solution.py:185
  140.5 1.9 %collective-permute-start.10 = (f32[64,768]{1,0:T(8,128)S(1)}, f32[64,768]{1,0:T(8,128)S(1)}, u32[]{:S(2)}, u32[]{:S(2)}) collective-permute-start(f32[64,768]{1,0:T(8,128)S(1)} %reshape.162), channel_id=1, source_target_pairs={{0,512},{512,0},{1,513},{513,1},{2,514},{514,2},{3,515},{515,3},{4... | collective-permute-start | bytes 589832 | tf_op jit(solution)/shard_map/ppermute | solution.py:305
  142.5 5.1 %collective-permute-done.10 = f32[64,768]{1,0:T(8,128)S(1)} collective-permute-done((f32[64,768]{1,0:T(8,128)S(1)}, f32[64,768]{1,0:T(8,128)S(1)}, u32[]{:S(2)}, u32[]{:S(2)}) %collective-permute-start.10) | collective-permute-done | bytes 196640 | tf_op jit(solution)/shard_map/ppermute | solution.py:305
  147.6 8.6 %collective-permute-start.11 = (f32[128,768]{1,0:T(8,128)S(1)}, f32[128,768]{1,0:T(8,128)S(1)}, u32[]{:S(2)}, u32[]{:S(2)}) collective-permute-start(f32[128,768]{1,0:T(8,128)S(1)} %pad_maximum_fusion.3), channel_id=1, source_target_pairs={{0,16},{16,0},{1,17},{17,1},{2,18},{18,2},{3,19},{19,3},{4,20},{20... | collective-permute-start | bytes 1179656 | tf_op jit(solution)/shard_map/ppermute | solution.py:306
  158.1 12.1 %spd_inverse.1 = f32[256,256]{1,0:T(8,128)} custom-call(f32[256,256]{1,0:T(8,128)} %pad_maximum_fusion.5.s_ref, f32[1,256]{1,0:T(1,128)} %bitcast.117), custom_call_target="tpu_custom_call" | custom-call | flops 67108864 | bytes 524288 | tf_op jit(solution)/shard_map/spd_inverse/pallas_call | solution.py:89
  170.2 1.3 fusion.85
  171.5 1.2 convolution_subtract_fusion
  (109 shorter events, 12.8 us)
Async XLA Ops:
  0.0 0.7 copy-start.8
  0.7 1.5 copy-start.3
  0.7 1.5 copy-start.4
  0.7 1.5 copy-start.6
  0.7 1.5 copy-start.7
  11.7 21.7 %all-to-all-start = ((f32[16,16,128]{2,1,0:T(8,128)}), f32[16,16,128]{2,1,0:T(8,128)S(1)}, u32[]{:S(2)}, u32[]{:S(2)}) async-start(f32[16,16,128]{2,1,0:T(8,128)} %bitcast.112), calls=%async_computation | async-start | bytes 262144 | tf_op jit(solution)/shard_map/all_to_all | solution.py:189
  23.0 10.3 %copy-start.5 = (f32[128,512]{1,0:T(8,128)S(1)}, f32[128,512]{1,0:T(8,128)}, u32[]{:S(2)}) copy-start(f32[128,512]{1,0:T(8,128)} %cov_ref.1) | copy-start | bytes 786436
  23.0 20.7 %collective-permute-start.8 = (f32[128,512]{1,0:T(8,128)S(1)}, f32[128,512]{1,0:T(8,128)S(1)}, u32[]{:S(2)}, u32[]{:S(2)}) collective-permute-start(f32[128,512]{1,0:T(8,128)S(1)} %slice_select_fusion.3), channel_id=1, source_target_pairs={{0,16},{16,0},{1,17},{17,1},{2,18},{18,2},{3,19},{19,3},{4,20},{20... | collective-permute-start | bytes 786440 | tf_op jit(solution)/shard_map/ppermute | solution.py:279
  33.5 32.4 %collective-permute-start.1 = (f32[128,528]{0,1:T(8,128)S(1)}, f32[128,528]{0,1:T(8,128)S(1)}, u32[]{:S(2)}, u32[]{:S(2)}) collective-permute-start(f32[128,528]{0,1:T(8,128)S(1)} %get-tuple-element.41), channel_id=1, source_target_pairs={{16,0},{32,16},{48,32},{64,48},{80,64},{96,80},{112,96},{128,112},... | collective-permute-start | bytes 811016 | tf_op jit(solution)/shard_map/ppermute | solution.py:31
  41.6 24.2 %collective-permute-start = (f32[128,528]{0,1:T(8,128)S(1)}, f32[128,528]{0,1:T(8,128)S(1)}, u32[]{:S(2)}, u32[]{:S(2)}) collective-permute-start(f32[128,528]{0,1:T(8,128)S(1)} %get-tuple-element.41), channel_id=1, source_target_pairs={{0,16},{16,32},{32,48},{48,64},{64,80},{80,96},{96,112},{112,128},... | collective-permute-start | bytes 811016 | tf_op jit(solution)/shard_map/ppermute | solution.py:29
  43.6 1.0 copy-start.1
  44.7 5.7 %collective-permute-start.9 = (f32[64,512]{1,0:T(8,128)S(1)}, f32[64,512]{1,0:T(8,128)S(1)}, u32[]{:S(2)}, u32[]{:S(2)}) collective-permute-start(f32[64,512]{1,0:T(8,128)S(1)} %slice_select_fusion.4), channel_id=1, source_target_pairs={{0,512},{512,0},{1,513},{513,1},{2,514},{514,2},{3,515},{515,3},{4... | collective-permute-start | bytes 393224 | tf_op jit(solution)/shard_map/ppermute | solution.py:283
  51.1 32.7 %all-to-all-start.1 = ((f32[16,4,512]{2,1,0:T(4,128)}), f32[16,4,512]{2,1,0:T(4,128)S(1)}, u32[]{:S(2)}, u32[]{:S(2)}) async-start(f32[16,4,512]{2,1,0:T(4,128)} %reshape.159), calls=%async_computation.1 | async-start | bytes 262144 | tf_op jit(solution)/shard_map/all_to_all | solution.py:189
  66.1 10.1 %collective-permute-start.2 = (f32[128,528]{0,1:T(8,128)S(1)}, f32[128,528]{0,1:T(8,128)S(1)}, u32[]{:S(2)}, u32[]{:S(2)}) collective-permute-start(f32[128,528]{0,1:T(8,128)S(1)} %fusion.18), channel_id=1, source_target_pairs={{0,16},{16,32},{32,48},{48,64},{64,80},{80,96},{96,112},{112,128},... | collective-permute-start | bytes 811016 | tf_op jit(solution)/shard_map/ppermute | solution.py:29
  70.2 8.7 %collective-permute-start.3 = (f32[128,528]{0,1:T(8,128)S(1)}, f32[128,528]{0,1:T(8,128)S(1)}, u32[]{:S(2)}, u32[]{:S(2)}) collective-permute-start(f32[128,528]{0,1:T(8,128)S(1)} %fusion.18), channel_id=1, source_target_pairs={{16,0},{32,16},{48,32},{64,48},{80,64},{96,80},{112,96},{128,112},... | collective-permute-start | bytes 811016 | tf_op jit(solution)/shard_map/ppermute | solution.py:31
  79.2 10.3 %collective-permute-start.4 = (f32[128,528]{0,1:T(8,128)S(1)}, f32[128,528]{0,1:T(8,128)S(1)}, u32[]{:S(2)}, u32[]{:S(2)}) collective-permute-start(f32[128,528]{0,1:T(8,128)S(1)} %fusion.22), channel_id=1, source_target_pairs={{0,16},{16,32},{32,48},{48,64},{64,80},{80,96},{96,112},{112,128},... | collective-permute-start | bytes 811016 | tf_op jit(solution)/shard_map/ppermute | solution.py:29
  81.1 8.4 %collective-permute-start.5 = (f32[128,528]{0,1:T(8,128)S(1)}, f32[128,528]{0,1:T(8,128)S(1)}, u32[]{:S(2)}, u32[]{:S(2)}) collective-permute-start(f32[128,528]{0,1:T(8,128)S(1)} %fusion.22), channel_id=1, source_target_pairs={{16,0},{32,16},{48,32},{64,48},{80,64},{96,80},{112,96},{128,112},... | collective-permute-start | bytes 811016 | tf_op jit(solution)/shard_map/ppermute | solution.py:31
  83.7 1.0 copy-start.2
  86.0 14.6 %all-to-all-start.2 = ((f32[16,4,768]{2,1,0:T(4,128)}), f32[16,4,768]{2,1,0:T(4,128)S(1)}, u32[]{:S(2)}, u32[]{:S(2)}) async-start(f32[16,4,768]{2,1,0:T(4,128)} %broadcast_in_dim.151), calls=%async_computation.2 | async-start | bytes 393216 | tf_op jit(solution)/shard_map/all_to_all | solution.py:185
  89.8 4.5 %copy-start = (f32[128,528]{0,1:T(8,128)}, f32[128,528]{0,1:T(8,128)S(1)}, u32[]{:S(2)}) copy-start(f32[128,528]{0,1:T(8,128)S(1)} %fusion.26) | copy-start | bytes 811012
  89.8 11.5 %collective-permute-start.6 = (f32[128,384]{0,1:T(8,128)S(1)}, f32[128,384]{0,1:T(8,128)S(1)}, u32[]{:S(2)}, u32[]{:S(2)}) collective-permute-start(f32[128,384]{0,1:T(8,128)S(1)} %get-tuple-element.31), channel_id=1, source_target_pairs={{0,1},{1,2},{2,3},{3,4},{4,5},{5,6},{6,7},{7,8},{8,9},{9,10},{10,1... | collective-permute-start | bytes 589832 | tf_op jit(solution)/shard_map/ppermute | solution.py:29
  93.0 9.0 %collective-permute-start.7 = (f32[128,384]{0,1:T(8,128)S(1)}, f32[128,384]{0,1:T(8,128)S(1)}, u32[]{:S(2)}, u32[]{:S(2)}) collective-permute-start(f32[128,384]{0,1:T(8,128)S(1)} %get-tuple-element.32), channel_id=1, source_target_pairs={{1,0},{2,1},{3,2},{4,3},{5,4},{6,5},{7,6},{8,7},{9,8},{10,9},{11,1... | collective-permute-start | bytes 589832 | tf_op jit(solution)/shard_map/ppermute | solution.py:31
  100.8 1.2 slice-start
  103.0 22.3 %all-to-all-start.3 = ((f32[16,4,768]{2,1,0:T(4,128)}), f32[16,4,768]{2,1,0:T(4,128)S(1)}, u32[]{:S(2)}, u32[]{:S(2)}) async-start(f32[16,4,768]{2,1,0:T(4,128)} %broadcast_in_dim.158), calls=%async_computation.3 | async-start | bytes 393216 | tf_op jit(solution)/shard_map/all_to_all | solution.py:185
  125.9 44.2 %all-to-all-start.4 = ((f32[16,16,128]{2,1,0:T(8,128)}), f32[16,16,128]{2,1,0:T(8,128)S(1)}, u32[]{:S(2)}, u32[]{:S(2)}) async-start(f32[16,16,128]{2,1,0:T(8,128)} %broadcast_in_dim.159), calls=%async_computation.4 | async-start | bytes 262144 | tf_op jit(solution)/shard_map/all_to_all | solution.py:185
  140.5 7.0 %collective-permute-start.10 = (f32[64,768]{1,0:T(8,128)S(1)}, f32[64,768]{1,0:T(8,128)S(1)}, u32[]{:S(2)}, u32[]{:S(2)}) collective-permute-start(f32[64,768]{1,0:T(8,128)S(1)} %reshape.162), channel_id=1, source_target_pairs={{0,512},{512,0},{1,513},{513,1},{2,514},{514,2},{3,515},{515,3},{4... | collective-permute-start | bytes 589832 | tf_op jit(solution)/shard_map/ppermute | solution.py:305
  147.6 9.7 %collective-permute-start.11 = (f32[128,768]{1,0:T(8,128)S(1)}, f32[128,768]{1,0:T(8,128)S(1)}, u32[]{:S(2)}, u32[]{:S(2)}) collective-permute-start(f32[128,768]{1,0:T(8,128)S(1)} %pad_maximum_fusion.3), channel_id=1, source_target_pairs={{0,16},{16,0},{1,17},{17,1},{2,18},{18,2},{3,19},{19,3},{4,20},{20... | collective-permute-start | bytes 1179656 | tf_op jit(solution)/shard_map/ppermute | solution.py:306

commit v4 on v3

--- a/solution.py
+++ b/solution.py
@@ -96,38 +96,42 @@
     )(s, var.reshape(1, n))
 
 
-def footprint_kernel(start_ref, site_ref, keep_ref, west_ref, east_ref, south_ref, north_ref, cov_ref,
-                     spread_ref, rows_ref, cols_ref):
-    nobs = site_ref.shape[0]
-    bands = keep_ref.shape[0]
+def footprint_kernel(start_ref, site_ref, cu_ref, cv_ref, su_ref, sv_ref, cov_ref, spread_ref, rows_ref, coef_ref, near_ref, site_col_ref):
+    nobs = site_ref.shape[1]
+    bands = cu_ref.shape[0]
     chunk = 32
     lane = lax.broadcasted_iota(jnp.int32, (chunk, MERIDIAN_TOTAL), 1)
+    site_col_ref[...] = jnp.broadcast_to(site_ref[...], (8, nobs)).T
 
     def footprint(first, count, store):
         total = count + 2 * STEPS
-
-        def coeff(ref, t):
+        for t in range(total):
             band = first + (t - STEPS)
             inside = (band >= 0) & (band < bands)
-            line = ref[pl.ds(jnp.clip(band, 0, bands - 1), 1), :]
-            return jnp.where(inside, line, 0.0)
+            at = pl.ds(jnp.clip(band, 0, bands - 1), 1)
+            cu = jnp.where(inside, cu_ref[at, :], 0.0)
+            cv = jnp.where(inside, cv_ref[at, :], 0.0)
+            west = jnp.where(su_ref[at, :] > 0, cu, 0.0)
+            south = jnp.where(sv_ref[at, :] > 0, cv, 0.0)
+            for k, line in enumerate((1.0 - cu - cv, west, cu - west, south, cv - south)):
+                coef_ref[5 * t + k : 5 * t + k + 1, :] = line
+
+        def coeff(t, k):
+            return coef_ref[5 * t + k : 5 * t + k + 1, :]
 
         def body(i, carry):
             at = pl.multiple_of(i * chunk, chunk)
-            site = site_ref[pl.ds(at, chunk), :]
-            v = [
-                (site == (first + (t - STEPS)) * MERIDIAN_TOTAL + lane).astype(jnp.float32)
-                for t in range(total)
-            ]
+            site = site_col_ref[pl.ds(at, chunk), 0:1] - (first - STEPS) * MERIDIAN_TOTAL - lane
+            v = [(site == t * MERIDIAN_TOTAL).astype(jnp.float32) for t in range(total)]
             for step in range(STEPS):
                 low, high = (step + 1, total - step - 1)
                 new = []
                 for t in range(low, high):
-                    w = coeff(keep_ref, t) * v[t]
-                    w = w + pltpu.roll(coeff(west_ref, t) * v[t], MERIDIAN_TOTAL - 1, 1)
-                    w = w + pltpu.roll(coeff(east_ref, t) * v[t], 1, 1)
-                    w = w + coeff(south_ref, t + 1) * v[t + 1]
-                    w = w + coeff(north_ref, t - 1) * v[t - 1]
+                    w = coeff(t, 0) * v[t]
+                    w = w + pltpu.roll(coeff(t, 1) * v[t], MERIDIAN_TOTAL - 1, 1)
+                    w = w + pltpu.roll(coeff(t, 2) * v[t], 1, 1)
+                    w = w + coeff(t + 1, 3) * v[t + 1]
+                    w = w + coeff(t - 1, 4) * v[t - 1]
                     new.append(w)
                 v = [None] * low + new + [None] * (total - high)
             store(at, v[STEPS : STEPS + count])
@@ -135,49 +139,38 @@
 
         lax.fori_loop(0, nobs // chunk, body, 0)
 
-    def store_rows(at, v):
-        rows_ref[pl.ds(at, chunk), 0:MERIDIAN_TOTAL] = v[0]
-
-    def store_cols(at, v):
+    def store_near(at, v):
+        near_ref[pl.ds(at, chunk), :] = v[0]
+
+    def store_spread(at, v):
         for b, w in enumerate(v):
             spread_ref[pl.ds(at, chunk), b * MERIDIAN_TOTAL : (b + 1) * MERIDIAN_TOTAL] = w
 
-    footprint(start_ref[0], cov_ref.shape[0] // MERIDIAN_TOTAL, store_rows)
-    footprint(start_ref[1], cov_ref.shape[1] // MERIDIAN_TOTAL, store_cols)
-    cov = cov_ref[...]
-    near = rows_ref[:, 0:MERIDIAN_TOTAL]
-    rows_ref[...] = jnp.dot(near, cov, precision=HIGHEST, preferred_element_type=jnp.float32)
-    cols_ref[...] = lax.dot_general(
-        spread_ref[...], cov, (((1,), (1,)), ((), ())), precision=HIGHEST, preferred_element_type=jnp.float32
-    )
-
-
-def footprints(covariance, starts, site, lon_speed, lat_speed, lon_sign, lat_sign):
+    footprint(start_ref[0], 1, store_near)
+    rows_ref[...] = jnp.dot(near_ref[...], cov_ref[...], precision=HIGHEST, preferred_element_type=jnp.float32)
+    footprint(start_ref[1], cov_ref.shape[1] // MERIDIAN_TOTAL, store_spread)
+
+
+def footprints(covariance, starts, site, *winds):
     rows_dev, cols_dev = covariance.shape
+    assert rows_dev == MERIDIAN_TOTAL
     nobs = site.shape[0]
-    bands = lon_speed.shape[0] // MERIDIAN_TOTAL
-
-    def grid_of(field):
-        return field.reshape(bands, MERIDIAN_TOTAL)
-
-    cu, cv = grid_of(lon_speed), grid_of(lat_speed)
-    su, sv = grid_of(lon_sign) > 0, grid_of(lat_sign) > 0
-    fields = [
-        1.0 - cu - cv,
-        jnp.where(su, cu, 0.0),
-        jnp.where(su, 0.0, cu),
-        jnp.where(sv, cv, 0.0),
-        jnp.where(sv, 0.0, cv),
-    ]
-    shapes = [(nobs, cols_dev), (nobs, cols_dev), (nobs, rows_dev)]
+    bands = winds[0].shape[0] // MERIDIAN_TOTAL
+    total = cols_dev // MERIDIAN_TOTAL + 2 * STEPS
+    vmem = pl.BlockSpec(memory_space=pltpu.VMEM)
     return pl.pallas_call(
         footprint_kernel,
-        out_shape=[jax.ShapeDtypeStruct(shape, jnp.float32) for shape in shapes],
-        in_specs=[pl.BlockSpec(memory_space=pltpu.SMEM)] + [pl.BlockSpec(memory_space=pltpu.VMEM)] * 7,
-        out_specs=[pl.BlockSpec(memory_space=pltpu.VMEM)] * 3,
-        cost_estimate=pl.CostEstimate(flops=400 * 1000 * 1000, bytes_accessed=2000000, transcendentals=0),
+        out_shape=[jax.ShapeDtypeStruct((nobs, cols_dev), jnp.float32)] * 2,
+        in_specs=[pl.BlockSpec(memory_space=pltpu.SMEM)] + [vmem] * 6,
+        out_specs=[vmem] * 2,
+        scratch_shapes=[
+            pltpu.VMEM((5 * total + 6, MERIDIAN_TOTAL), jnp.float32),
+            pltpu.VMEM((nobs, MERIDIAN_TOTAL), jnp.float32),
+            pltpu.VMEM((nobs, 8), jnp.int32),
+        ],
+        cost_estimate=pl.CostEstimate(flops=400 * 1000 * 1000, bytes_accessed=1500000, transcendentals=0),
         name="footprints",
-    )(starts, site, *fields, covariance)
+    )(starts, site.reshape(1, nobs), *(field.reshape(bands, MERIDIAN_TOTAL) for field in winds), covariance)
 
 
 def everyone(chunk, axis):
@@ -271,28 +264,29 @@
         lax.dot_general, precision=HIGHEST, preferred_element_type=jnp.float32
     )
     winds = (lon_speed, lat_speed, lon_sign, lat_sign)
-    site = measurement_site_position[:, None]
     starts = jnp.stack([row_start, col_start]) // MERIDIAN_TOTAL
-    spread, hp, pht = footprints(covariance, starts, site, *winds)
+    spread, hp = footprints(covariance, starts, measurement_site_position, *winds)
 
     own, other = halves(hp, 0, core)
-    fellow = lax.ppermute(other, "co", SWAP)
-    sides = lax.axis_size(COL)
-    pht = scattered_sum(pht.reshape(sides, nobs // sides, rows_dev), COL)
-    own, other = halves(own + fellow, 0, lat_half)
+    own, other = halves(own + lax.ppermute(other, "co", SWAP), 0, lat_half)
     hp = own + lax.ppermute(other, "yl", SWAP)
     deep = lax.axis_size("z")
     hp = scattered_sum(hp.reshape(deep, nobs // 4 // deep, cols_dev), "z")
 
-    forecast = row_transported(
-        jnp.concatenate([covariance, pht.T], axis=1), *winds, row_start
-    )
-    pht = forecast[:, cols_dev:].T
+    forecast = row_transported(covariance, *winds, row_start)
+    pht = dot(spread, forecast, (((1,), (1,)), ((), ())))
     fields = col_fields(*winds, col_start, cols_dev)
-    forecast = col_transported(padded_2(forecast[:, :cols_dev], ((COL, 1),), margin), fields)
-
+
+    sides = lax.axis_size(COL)
     hpht = dot(hp, spread, (((1,), (1,)), ((), ())))
-    found = everyone(jnp.concatenate([hp, hpht], axis=1), COL)
+    mine = jnp.concatenate([hp, hpht], axis=1)
+    pht = pht.reshape(sides, nobs // sides, rows_dev)
+    packed = jnp.broadcast_to(mine.reshape(1, -1, rows_dev), (sides, mine.size // rows_dev, rows_dev))
+    packed = lax.all_to_all(
+        jnp.concatenate([packed, pht], axis=1), COL, split_axis=0, concat_axis=0, tiled=True
+    )
+    found = packed[:, : mine.size // rows_dev].reshape(sides, *mine.shape)
+    pht = jnp.sum(packed[:, mine.size // rows_dev :], axis=0)
     hpht = jnp.sum(found[:, :, cols_dev:], axis=0)
     near = lax.dynamic_slice_in_dim(
         jnp.pad(found[:, :, :cols_dev], ((1, 1), (0, 0), (0, 0))), col, 3
@@ -302,12 +296,14 @@
 
     block = jnp.concatenate([hp, hpht], axis=1)
     block = everyone(block, "z").reshape(nobs // 4, cols_dev + nobs)
+    forecast = col_transported(padded_2(forecast, ((COL, 1),), margin), fields)
     block = joined(block, lax.ppermute(block, "yl", SWAP), 0, lat_half)
     block = joined(block, lax.ppermute(block, "co", SWAP), 0, core)
     hp, hpht = block[:, :cols_dev], block[:, cols_dev:]
 
+    pht, hpht = lax.optimization_barrier((pht, hpht))
+    pht = everyone(pht, COL).reshape(nobs, rows_dev)
     inverse = spd_inverse(hpht, obs_var)
-    pht = everyone(pht, COL).reshape(nobs, rows_dev)
     gain = dot(inverse, pht, (((1,), (0,)), ((), ())))
     return forecast - dot(gain, hp, (((0,), (0,)), ((), ())))
 

time: 174 us -> 166 us (0.954)
  starting transfers between devices: 99.7 us -> 94.2 us
  waiting for transfers between devices: 33.6 us -> 31.8 us
    all_to_all x2 -> x1, starting transfers between devices: 24.9 us -> 8.69 us  [scattered_sum(): lax.all_to_all(parts, axis, split_axis=0, concat_axis=0, tiled=True)]
    all_to_all x0 -> x1, starting transfers between devices: none -> 9.38 us  [shards(): lax.all_to_all(jnp.concatenate([packed, pht], axis=1), COL, split_axis=0,...]
    ppermute x1, starting transfers between devices: 9.46 us -> 1.92 us  [shards(): own, other = halves(own + lax.ppermute(other, 'co', SWAP), 0, lat_half)]
    all_to_all x3 -> x2, waiting for transfers between devices: 17 us -> 11.3 us  [everyone(): return lax.all_to_all(copies, axis, split_axis=0, concat_axis=0, tiled=True)]
    all_to_all x3 -> x2, starting transfers between devices: 28 us -> 22.8 us  [everyone(): return lax.all_to_all(copies, axis, split_axis=0, concat_axis=0, tiled=True)]
    ppermute x1, starting transfers between devices: 1.92 us -> 6.81 us  [shards(): hp = own + lax.ppermute(other, 'yl', SWAP)]
    ppermute x4, starting transfers between devices: 11.1 us -> 15.9 us  [padded_2(): lax.ppermute(tail, axis, [(i, (i + 1) % count) for i in range(ends)])]
    ppermute x4, starting transfers between devices: 13.8 us -> 17.6 us  [padded_2(): lax.ppermute(head, axis, [((i + 1) % count, i) for i in range(ends)])]
  transfers between devices with their start and end apart: 17 -> 16, of which waited for: 8 -> 9; matrix products, arithmetic and copies ran while one was open for 5% -> 4% of each run, Pallas kernels for 7% -> 12%
where the time goes in v4:
time: 166 us; the launch traced here: 164 us
  starting transfers between devices  94.2 us (57%)
  waiting for transfers between devices  31.8 us (19%)
  Pallas kernels  20 us (12%)
  local copies, waits for them, and re-layouts  7.89 us (5%)
  other arithmetic  6.35 us (4%)
  matrix products  3.58 us (2%)
    all_to_all x2, starting transfers between devices, everyone(): return lax.all_to_all(copies, axis, split_axis=0, concat_axis=0, tiled=True)  22.8 us
    ppermute x4, starting transfers between devices, padded_2(): lax.ppermute(head, axis, [((i + 1) % count, i) for i in range(ends)])  17.6 us
    ppermute x4, starting transfers between devices, padded_2(): lax.ppermute(tail, axis, [(i, (i + 1) % count) for i in range(ends)])  15.9 us
    pallas_call x1, Pallas kernels, spd_inverse(): pl.pallas_call(inverse_kernel, out_shape=jax.ShapeDtypeStruct((n, n), jnp...  12.1 us
    all_to_all x2, waiting for transfers between devices, everyone(): return lax.all_to_all(copies, axis, split_axis=0, concat_axis=0, tiled=True)  11.3 us
    all_to_all x1, starting transfers between devices, shards(): lax.all_to_all(jnp.concatenate([packed, pht], axis=1), COL, split_axis=0,...  9.38 us
    all_to_all x1, starting transfers between devices, scattered_sum(): lax.all_to_all(parts, axis, split_axis=0, concat_axis=0, tiled=True)  8.69 us
    ppermute x1, starting transfers between devices, shards(): block = joined(block, lax.ppermute(block, 'co', SWAP), 0, core)  8.65 us
  transfers between devices with their start and end apart: 16, of which 9 were waited for; matrix products, arithmetic and copies ran while one was open for 4% of the time, Pallas kernels for 12%

profile of v4, /device:TPU:1, one launch (start us, length us, event | category | flops | bytes accessed | tf_op | source)
XLA Modules:
  0.0 164.5 jit_solution(6763920336082843956)
XLA Ops:
  0.0 1.1 copy.10
  1.1 5.4 %collective-permute-start = (f32[128,512]{0,1:T(8,128)S(1)}, f32[128,512]{0,1:T(8,128)S(1)}, u32[]{:S(2)}, u32[]{:S(2)}) collective-permute-start(f32[128,512]{0,1:T(8,128)S(1)} %copy.10), channel_id=1, source_target_pairs={{0,16},{16,32},{32,48},{48,64},{64,80},{80,96},{96,112},{112,128},... | collective-permute-start | bytes 786440 | tf_op jit(solution)/shard_map/ppermute | solution.py:29
  6.5 11.9 %collective-permute-start.1 = (f32[128,512]{0,1:T(8,128)S(1)}, f32[128,512]{0,1:T(8,128)S(1)}, u32[]{:S(2)}, u32[]{:S(2)}) collective-permute-start(f32[128,512]{0,1:T(8,128)S(1)} %copy.10), channel_id=1, source_target_pairs={{16,0},{32,16},{48,32},{64,48},{80,64},{96,80},{112,96},{128,112},... | collective-permute-start | bytes 786440 | tf_op jit(solution)/shard_map/ppermute | solution.py:31
  19.1 8.0 %footprints.1 = (f32[256,512]{1,0:T(8,128)}, f32[256,512]{1,0:T(8,128)}) custom-call(s32[2]{0:T(128)} %and_select_fusion.start_ref, s32[1,256]{1,0:T(1,128)} %bitcast.115, f32[64,128]{1,0:T(8,128)} %bitcast.113, f32[64,128]{1,0:T(8,128)} %bitcast.112, s32[64,128]{1,0:T(8,128)} %bitcast.110, s32[64,128]{1,0:T(8,128)} %bitcast.109, f32[128,512]{1,0:T(8,128)} %cov_ref.1), custom_call_target="tpu_custom_call" | custom-call | flops 400000000 | bytes 1500000 | tf_op jit(solution)/shard_map/footprints/pallas_call | solution.py:161
  27.0 1.1 slice_select_fusion.3
  28.1 1.9 %collective-permute-start.8 = (f32[128,512]{1,0:T(8,128)S(1)}, f32[128,512]{1,0:T(8,128)S(1)}, u32[]{:S(2)}, u32[]{:S(2)}) collective-permute-start(f32[128,512]{1,0:T(8,128)S(1)} %slice_select_fusion.3), channel_id=1, source_target_pairs={{0,16},{16,0},{1,17},{17,1},{2,18},{18,2},{3,19},{19,3},{4,20},{20... | collective-permute-start | bytes 786440 | tf_op jit(solution)/shard_map/ppermute | solution.py:271
  32.0 1.9 %collective-permute-start.2 = (f32[128,512]{0,1:T(8,128)S(1)}, f32[128,512]{0,1:T(8,128)S(1)}, u32[]{:S(2)}, u32[]{:S(2)}) collective-permute-start(f32[128,512]{0,1:T(8,128)S(1)} %fusion.22), channel_id=1, source_target_pairs={{0,16},{16,32},{32,48},{48,64},{64,80},{80,96},{96,112},{112,128},... | collective-permute-start | bytes 786440 | tf_op jit(solution)/shard_map/ppermute | solution.py:29
  33.9 2.4 %collective-permute-start.3 = (f32[128,512]{0,1:T(8,128)S(1)}, f32[128,512]{0,1:T(8,128)S(1)}, u32[]{:S(2)}, u32[]{:S(2)}) collective-permute-start(f32[128,512]{0,1:T(8,128)S(1)} %fusion.22), channel_id=1, source_target_pairs={{16,0},{32,16},{48,32},{64,48},{80,64},{96,80},{112,96},{128,112},... | collective-permute-start | bytes 786440 | tf_op jit(solution)/shard_map/ppermute | solution.py:31
  36.5 0.9 copy-done.1
  37.5 6.8 %collective-permute-start.9 = (f32[64,512]{1,0:T(8,128)S(1)}, f32[64,512]{1,0:T(8,128)S(1)}, u32[]{:S(2)}, u32[]{:S(2)}) collective-permute-start(f32[64,512]{1,0:T(8,128)S(1)} %slice_select_fusion.4), channel_id=1, source_target_pairs={{0,512},{512,0},{1,513},{513,1},{2,514},{514,2},{3,515},{515,3},{4... | collective-permute-start | bytes 393224 | tf_op jit(solution)/shard_map/ppermute | solution.py:272
  44.4 2.2 %collective-permute-done.9 = f32[64,512]{1,0:T(8,128)S(1)} collective-permute-done((f32[64,512]{1,0:T(8,128)S(1)}, f32[64,512]{1,0:T(8,128)S(1)}, u32[]{:S(2)}, u32[]{:S(2)}) %collective-permute-start.9) | collective-permute-done | bytes 131104 | tf_op jit(solution)/shard_map/ppermute | solution.py:272
  47.4 8.7 %all-to-all-start = ((f32[16,4,512]{2,1,0:T(4,128)}), f32[16,4,512]{2,1,0:T(4,128)S(1)}, u32[]{:S(2)}, u32[]{:S(2)}) async-start(f32[16,4,512]{2,1,0:T(4,128)} %reshape.163), calls=%async_computation | async-start | bytes 262144 | tf_op jit(solution)/shard_map/all_to_all | solution.py:182
  56.3 4.7 %collective-permute-start.4 = (f32[128,512]{0,1:T(8,128)S(1)}, f32[128,512]{0,1:T(8,128)S(1)}, u32[]{:S(2)}, u32[]{:S(2)}) collective-permute-start(f32[128,512]{0,1:T(8,128)S(1)} %fusion.26), channel_id=1, source_target_pairs={{0,16},{16,32},{32,48},{48,64},{64,80},{80,96},{96,112},{112,128},... | collective-permute-start | bytes 786440 | tf_op jit(solution)/shard_map/ppermute | solution.py:29
  60.9 1.9 %collective-permute-start.5 = (f32[128,512]{0,1:T(8,128)S(1)}, f32[128,512]{0,1:T(8,128)S(1)}, u32[]{:S(2)}, u32[]{:S(2)}) collective-permute-start(f32[128,512]{0,1:T(8,128)S(1)} %fusion.26), channel_id=1, source_target_pairs={{16,0},{32,16},{48,32},{64,48},{80,64},{96,80},{112,96},{128,112},... | collective-permute-start | bytes 786440 | tf_op jit(solution)/shard_map/ppermute | solution.py:31
  63.1 3.5 %collective-permute-done.4 = f32[128,512]{0,1:T(8,128)S(1)} collective-permute-done((f32[128,512]{0,1:T(8,128)S(1)}, f32[128,512]{0,1:T(8,128)S(1)}, u32[]{:S(2)}, u32[]{:S(2)}) %collective-permute-start.4) | collective-permute-done | bytes 262176 | tf_op jit(solution)/shard_map/ppermute | solution.py:29
  66.6 2.8 %collective-permute-done.5 = f32[128,512]{0,1:T(8,128)S(1)} collective-permute-done((f32[128,512]{0,1:T(8,128)S(1)}, f32[128,512]{0,1:T(8,128)S(1)}, u32[]{:S(2)}, u32[]{:S(2)}) %collective-permute-start.5) | collective-permute-done | bytes 262176 | tf_op jit(solution)/shard_map/ppermute | solution.py:31
  69.7 0.8 copy-done
  72.5 9.4 %all-to-all-start.1 = ((f32[16,40,128]{2,1,0:T(8,128)}), f32[16,40,128]{2,1,0:T(8,128)S(1)}, u32[]{:S(2)}, u32[]{:S(2)}) async-start(f32[16,40,128]{2,1,0:T(8,128)} %pad_maximum_fusion.4), calls=%async_computation.1 | async-start | bytes 655360 | tf_op jit(solution)/shard_map/all_to_all | solution.py:285
  81.9 1.3 collective-permute-start.7
  83.2 4.0 %collective-permute-start.6 = (f32[128,384]{0,1:T(8,128)S(1)}, f32[128,384]{0,1:T(8,128)S(1)}, u32[]{:S(2)}, u32[]{:S(2)}) collective-permute-start(f32[128,384]{0,1:T(8,128)S(1)} %get-tuple-element.29), channel_id=1, source_target_pairs={{0,1},{1,2},{2,3},{3,4},{4,5},{5,6},{6,7},{7,8},{8,9},{9,10},{10,1... | collective-permute-start | bytes 589832 | tf_op jit(solution)/shard_map/ppermute | solution.py:29
  87.3 2.7 %collective-permute-done.7 = f32[128,384]{0,1:T(8,128)S(1)} collective-permute-done((f32[128,384]{0,1:T(8,128)S(1)}, f32[128,384]{0,1:T(8,128)S(1)}, u32[]{:S(2)}, u32[]{:S(2)}) %collective-permute-start.7) | collective-permute-done | bytes 196640 | tf_op jit(solution)/shard_map/ppermute | solution.py:31
  89.9 1.4 collective-permute-done.6
  91.4 3.3 %all-to-all-done.1 = f32[16,40,128]{2,1,0:T(8,128)S(1)} async-done(((f32[16,40,128]{2,1,0:T(8,128)}), f32[16,40,128]{2,1,0:T(8,128)S(1)}, u32[]{:S(2)}, u32[]{:S(2)}) %all-to-all-start.1) | async-done | bytes 327712 | tf_op jit(solution)/shard_map/all_to_all | solution.py:285
  96.3 9.3 %all-to-all-start.2 = ((f32[16,4,768]{2,1,0:T(4,128)}), f32[16,4,768]{2,1,0:T(4,128)S(1)}, u32[]{:S(2)}, u32[]{:S(2)}) async-start(f32[16,4,768]{2,1,0:T(4,128)} %broadcast_in_dim.150), calls=%async_computation.2 | async-start | bytes 393216 | tf_op jit(solution)/shard_map/all_to_all | solution.py:178
  106.6 11.3 %all-to-all-done.2 = f32[16,4,768]{2,1,0:T(4,128)S(1)} async-done(((f32[16,4,768]{2,1,0:T(4,128)}), f32[16,4,768]{2,1,0:T(4,128)S(1)}, u32[]{:S(2)}, u32[]{:S(2)}) %all-to-all-start.2) | async-done | bytes 196640 | tf_op jit(solution)/shard_map/all_to_all | solution.py:178
  118.0 2.4 %collective-permute-start.10 = (f32[64,768]{1,0:T(8,128)S(1)}, f32[64,768]{1,0:T(8,128)S(1)}, u32[]{:S(2)}, u32[]{:S(2)}) collective-permute-start(f32[64,768]{1,0:T(8,128)S(1)} %reshape.167), channel_id=1, source_target_pairs={{0,512},{512,0},{1,513},{513,1},{2,514},{514,2},{3,515},{515,3},{4... | collective-permute-start | bytes 589832 | tf_op jit(solution)/shard_map/ppermute | solution.py:300
  120.4 4.0 %collective-permute-done.10 = f32[64,768]{1,0:T(8,128)S(1)} collective-permute-done((f32[64,768]{1,0:T(8,128)S(1)}, f32[64,768]{1,0:T(8,128)S(1)}, u32[]{:S(2)}, u32[]{:S(2)}) %collective-permute-start.10) | collective-permute-done | bytes 196640 | tf_op jit(solution)/shard_map/ppermute | solution.py:300
  124.5 8.7 %collective-permute-start.11 = (f32[128,768]{1,0:T(8,128)S(1)}, f32[128,768]{1,0:T(8,128)S(1)}, u32[]{:S(2)}, u32[]{:S(2)}) collective-permute-start(f32[128,768]{1,0:T(8,128)S(1)} %pad_maximum_fusion.3), channel_id=1, source_target_pairs={{0,16},{16,0},{1,17},{17,1},{2,18},{18,2},{3,19},{19,3},{4,20},{20... | collective-permute-start | bytes 1179656 | tf_op jit(solution)/shard_map/ppermute | solution.py:301
  135.9 13.5 %all-to-all-start.3 = ((f32[16,16,128]{2,1,0:T(8,128)}), f32[16,16,128]{2,1,0:T(8,128)S(1)}, u32[]{:S(2)}, u32[]{:S(2)}) async-start(f32[16,16,128]{2,1,0:T(8,128)} %broadcast_in_dim.151), calls=%async_computation.3 | async-start | bytes 262144 | tf_op jit(solution)/shard_map/all_to_all | solution.py:178
  149.9 12.1 %spd_inverse.1 = f32[256,256]{1,0:T(8,128)} custom-call(f32[256,256]{1,0:T(8,128)} %pad_maximum_fusion.5.s_ref, f32[1,256]{1,0:T(1,128)} %bitcast.114), custom_call_target="tpu_custom_call" | custom-call | flops 67108864 | bytes 524288 | tf_op jit(solution)/shard_map/spd_inverse/pallas_call | solution.py:89
  162.0 1.3 fusion.86
  163.3 1.2 convolution_subtract_fusion
  (99 shorter events, 12.1 us)
Async XLA Ops:
  1.1 30.7 %collective-permute-start = (f32[128,512]{0,1:T(8,128)S(1)}, f32[128,512]{0,1:T(8,128)S(1)}, u32[]{:S(2)}, u32[]{:S(2)}) collective-permute-start(f32[128,512]{0,1:T(8,128)S(1)} %copy.10), channel_id=1, source_target_pairs={{0,16},{16,32},{32,48},{48,64},{64,80},{80,96},{96,112},{112,128},... | collective-permute-start | bytes 786440 | tf_op jit(solution)/shard_map/ppermute | solution.py:29
  6.5 25.3 %collective-permute-start.1 = (f32[128,512]{0,1:T(8,128)S(1)}, f32[128,512]{0,1:T(8,128)S(1)}, u32[]{:S(2)}, u32[]{:S(2)}) collective-permute-start(f32[128,512]{0,1:T(8,128)S(1)} %copy.10), channel_id=1, source_target_pairs={{16,0},{32,16},{48,32},{64,48},{80,64},{96,80},{112,96},{128,112},... | collective-permute-start | bytes 786440 | tf_op jit(solution)/shard_map/ppermute | solution.py:31
  27.0 3.0 %copy-start.4 = (f32[8192]{0:T(1024)S(1)}, f32[8192]{0:T(1024)}, u32[]{:S(2)}) copy-start(f32[8192]{0:T(1024)} %param.9) | copy-start | bytes 98308
  27.0 3.0 %copy-start.5 = (f32[8192]{0:T(1024)S(1)}, f32[8192]{0:T(1024)}, u32[]{:S(2)}) copy-start(f32[8192]{0:T(1024)} %param.8) | copy-start | bytes 98308
  28.1 8.3 %collective-permute-start.8 = (f32[128,512]{1,0:T(8,128)S(1)}, f32[128,512]{1,0:T(8,128)S(1)}, u32[]{:S(2)}, u32[]{:S(2)}) collective-permute-start(f32[128,512]{1,0:T(8,128)S(1)} %slice_select_fusion.3), channel_id=1, source_target_pairs={{0,16},{16,0},{1,17},{17,1},{2,18},{18,2},{3,19},{19,3},{4,20},{20... | collective-permute-start | bytes 786440 | tf_op jit(solution)/shard_map/ppermute | solution.py:271
  30.1 0.8 copy-start.2
  30.1 0.8 copy-start.3
  32.0 24.1 %collective-permute-start.2 = (f32[128,512]{0,1:T(8,128)S(1)}, f32[128,512]{0,1:T(8,128)S(1)}, u32[]{:S(2)}, u32[]{:S(2)}) collective-permute-start(f32[128,512]{0,1:T(8,128)S(1)} %fusion.22), channel_id=1, source_target_pairs={{0,16},{16,32},{32,48},{48,64},{64,80},{80,96},{96,112},{112,128},... | collective-permute-start | bytes 786440 | tf_op jit(solution)/shard_map/ppermute | solution.py:29
  33.9 22.2 %collective-permute-start.3 = (f32[128,512]{0,1:T(8,128)S(1)}, f32[128,512]{0,1:T(8,128)S(1)}, u32[]{:S(2)}, u32[]{:S(2)}) collective-permute-start(f32[128,512]{0,1:T(8,128)S(1)} %fusion.22), channel_id=1, source_target_pairs={{16,0},{32,16},{48,32},{64,48},{80,64},{96,80},{112,96},{128,112},... | collective-permute-start | bytes 786440 | tf_op jit(solution)/shard_map/ppermute | solution.py:31
  36.3 1.0 copy-start.1
  37.5 9.2 %collective-permute-start.9 = (f32[64,512]{1,0:T(8,128)S(1)}, f32[64,512]{1,0:T(8,128)S(1)}, u32[]{:S(2)}, u32[]{:S(2)}) collective-permute-start(f32[64,512]{1,0:T(8,128)S(1)} %slice_select_fusion.4), channel_id=1, source_target_pairs={{0,512},{512,0},{1,513},{513,1},{2,514},{514,2},{3,515},{515,3},{4... | collective-permute-start | bytes 393224 | tf_op jit(solution)/shard_map/ppermute | solution.py:272
  47.4 23.7 %all-to-all-start = ((f32[16,4,512]{2,1,0:T(4,128)}), f32[16,4,512]{2,1,0:T(4,128)S(1)}, u32[]{:S(2)}, u32[]{:S(2)}) async-start(f32[16,4,512]{2,1,0:T(4,128)} %reshape.163), calls=%async_computation | async-start | bytes 262144 | tf_op jit(solution)/shard_map/all_to_all | solution.py:182
  56.3 10.3 %collective-permute-start.4 = (f32[128,512]{0,1:T(8,128)S(1)}, f32[128,512]{0,1:T(8,128)S(1)}, u32[]{:S(2)}, u32[]{:S(2)}) collective-permute-start(f32[128,512]{0,1:T(8,128)S(1)} %fusion.26), channel_id=1, source_target_pairs={{0,16},{16,32},{32,48},{48,64},{64,80},{80,96},{96,112},{112,128},... | collective-permute-start | bytes 786440 | tf_op jit(solution)/shard_map/ppermute | solution.py:29
  60.9 8.5 %collective-permute-start.5 = (f32[128,512]{0,1:T(8,128)S(1)}, f32[128,512]{0,1:T(8,128)S(1)}, u32[]{:S(2)}, u32[]{:S(2)}) collective-permute-start(f32[128,512]{0,1:T(8,128)S(1)} %fusion.26), channel_id=1, source_target_pairs={{16,0},{32,16},{48,32},{64,48},{80,64},{96,80},{112,96},{128,112},... | collective-permute-start | bytes 786440 | tf_op jit(solution)/shard_map/ppermute | solution.py:31
  69.5 1.0 copy-start
  72.5 22.2 %all-to-all-start.1 = ((f32[16,40,128]{2,1,0:T(8,128)}), f32[16,40,128]{2,1,0:T(8,128)S(1)}, u32[]{:S(2)}, u32[]{:S(2)}) async-start(f32[16,40,128]{2,1,0:T(8,128)} %pad_maximum_fusion.4), calls=%async_computation.1 | async-start | bytes 655360 | tf_op jit(solution)/shard_map/all_to_all | solution.py:285
  81.9 8.0 %collective-permute-start.7 = (f32[128,384]{0,1:T(8,128)S(1)}, f32[128,384]{0,1:T(8,128)S(1)}, u32[]{:S(2)}, u32[]{:S(2)}) collective-permute-start(f32[128,384]{0,1:T(8,128)S(1)} %get-tuple-element.30), channel_id=1, source_target_pairs={{1,0},{2,1},{3,2},{4,3},{5,4},{6,5},{7,6},{8,7},{9,8},{10,9},{11,1... | collective-permute-start | bytes 589832 | tf_op jit(solution)/shard_map/ppermute | solution.py:31
  83.2 8.1 %collective-permute-start.6 = (f32[128,384]{0,1:T(8,128)S(1)}, f32[128,384]{0,1:T(8,128)S(1)}, u32[]{:S(2)}, u32[]{:S(2)}) collective-permute-start(f32[128,384]{0,1:T(8,128)S(1)} %get-tuple-element.29), channel_id=1, source_target_pairs={{0,1},{1,2},{2,3},{3,4},{4,5},{5,6},{6,7},{7,8},{8,9},{9,10},{10,1... | collective-permute-start | bytes 589832 | tf_op jit(solution)/shard_map/ppermute | solution.py:29
  96.3 21.6 %all-to-all-start.2 = ((f32[16,4,768]{2,1,0:T(4,128)}), f32[16,4,768]{2,1,0:T(4,128)S(1)}, u32[]{:S(2)}, u32[]{:S(2)}) async-start(f32[16,4,768]{2,1,0:T(4,128)} %broadcast_in_dim.150), calls=%async_computation.2 | async-start | bytes 393216 | tf_op jit(solution)/shard_map/all_to_all | solution.py:178
  118.0 6.4 %collective-permute-start.10 = (f32[64,768]{1,0:T(8,128)S(1)}, f32[64,768]{1,0:T(8,128)S(1)}, u32[]{:S(2)}, u32[]{:S(2)}) collective-permute-start(f32[64,768]{1,0:T(8,128)S(1)} %reshape.167), channel_id=1, source_target_pairs={{0,512},{512,0},{1,513},{513,1},{2,514},{514,2},{3,515},{515,3},{4... | collective-permute-start | bytes 589832 | tf_op jit(solution)/shard_map/ppermute | solution.py:300
  124.5 10.0 %collective-permute-start.11 = (f32[128,768]{1,0:T(8,128)S(1)}, f32[128,768]{1,0:T(8,128)S(1)}, u32[]{:S(2)}, u32[]{:S(2)}) collective-permute-start(f32[128,768]{1,0:T(8,128)S(1)} %pad_maximum_fusion.3), channel_id=1, source_target_pairs={{0,16},{16,0},{1,17},{17,1},{2,18},{18,2},{3,19},{19,3},{4,20},{20... | collective-permute-start | bytes 1179656 | tf_op jit(solution)/shard_map/ppermute | solution.py:301
  135.9 26.1 %all-to-all-start.3 = ((f32[16,16,128]{2,1,0:T(8,128)}), f32[16,16,128]{2,1,0:T(8,128)S(1)}, u32[]{:S(2)}, u32[]{:S(2)}) async-start(f32[16,16,128]{2,1,0:T(8,128)} %broadcast_in_dim.151), calls=%async_computation.3 | async-start | bytes 262144 | tf_op jit(solution)/shard_map/all_to_all | solution.py:178

commit v5 on v4

--- a/solution.py
+++ b/solution.py
@@ -209,7 +209,7 @@
 
     row_cu, row_cv = (row_coeff(lon_speed), row_coeff(lat_speed))
     row_su, row_sv = (row_coeff(lon_sign), row_coeff(lat_sign))
-    for step in range(STEPS):
+    for _ in range(STEPS):
         padded = padded_2(cells, ((ROW, 0),), MERIDIAN_TOTAL)
         shaped = padded.reshape(row_bands + 2, MERIDIAN_TOTAL, width)
         cells = advect(
@@ -285,6 +285,7 @@
     packed = lax.all_to_all(
         jnp.concatenate([packed, pht], axis=1), COL, split_axis=0, concat_axis=0, tiled=True
     )
+    packed, forecast = lax.optimization_barrier((packed, forecast))
     found = packed[:, : mine.size // rows_dev].reshape(sides, *mine.shape)
     pht = jnp.sum(packed[:, mine.size // rows_dev :], axis=0)
     hpht = jnp.sum(found[:, :, cols_dev:], axis=0)
@@ -296,7 +297,8 @@
 
     block = jnp.concatenate([hp, hpht], axis=1)
     block = everyone(block, "z").reshape(nobs // 4, cols_dev + nobs)
-    forecast = col_transported(padded_2(forecast, ((COL, 1),), margin), fields)
+    forecast = padded_2(forecast, ((COL, 1),), margin)
+    forecast = col_transported(forecast, fields)
     block = joined(block, lax.ppermute(block, "yl", SWAP), 0, lat_half)
     block = joined(block, lax.ppermute(block, "co", SWAP), 0, core)
     hp, hpht = block[:, :cols_dev], block[:, cols_dev:]

time: 166 us -> 166 us (level)
  waiting for transfers between devices: 31.8 us -> 37 us
  starting transfers between devices: 94.2 us -> 89.6 us
    all_to_all x1, waiting for transfers between devices: 3.27 us -> 12.6 us  [shards(): lax.all_to_all(jnp.concatenate([packed, pht], axis=1), COL, split_axis=0,...]
    all_to_all x2, starting transfers between devices: 22.8 us -> 18.2 us  [everyone(): return lax.all_to_all(copies, axis, split_axis=0, concat_axis=0, tiled=True)]
    ppermute x4, waiting for transfers between devices: 5.52 us -> 2.86 us  [padded_2(): lax.ppermute(head, axis, [((i + 1) % count, i) for i in range(ends)])]
  transfers between devices with their start and end apart: 16 -> 16, of which waited for: 9 -> 7; matrix products, arithmetic and copies ran while one was open for 4% -> 5% of each run, Pallas kernels for 12% -> 12%
where the time goes in v5:
time: 166 us; the launch traced here: 165 us
  starting transfers between devices  89.6 us (54%)
  waiting for transfers between devices  37 us (22%)
  Pallas kernels  20 us (12%)
  local copies, waits for them, and re-layouts  7.9 us (5%)
  other arithmetic  6.36 us (4%)
  matrix products  3.58 us (2%)
    all_to_all x2, starting transfers between devices, everyone(): return lax.all_to_all(copies, axis, split_axis=0, concat_axis=0, tiled=True)  18.2 us
    ppermute x4, starting transfers between devices, padded_2(): lax.ppermute(head, axis, [((i + 1) % count, i) for i in range(ends)])  17.6 us
    ppermute x4, starting transfers between devices, padded_2(): lax.ppermute(tail, axis, [(i, (i + 1) % count) for i in range(ends)])  15.9 us
    all_to_all x1, waiting for transfers between devices, shards(): lax.all_to_all(jnp.concatenate([packed, pht], axis=1), COL, split_axis=0,...  12.6 us
    pallas_call x1, Pallas kernels, spd_inverse(): pl.pallas_call(inverse_kernel, out_shape=jax.ShapeDtypeStruct((n, n), jnp...  12.1 us
    all_to_all x2, waiting for transfers between devices, everyone(): return lax.all_to_all(copies, axis, split_axis=0, concat_axis=0, tiled=True)  11.3 us
    all_to_all x1, starting transfers between devices, shards(): lax.all_to_all(jnp.concatenate([packed, pht], axis=1), COL, split_axis=0,...  9.38 us
    ppermute x1, starting transfers between devices, shards(): block = joined(block, lax.ppermute(block, 'co', SWAP), 0, core)  8.73 us
  transfers between devices with their start and end apart: 16, of which 7 were waited for; matrix products, arithmetic and copies ran while one was open for 5% of the time, Pallas kernels for 12%

profile of v5, /device:TPU:1, one launch (start us, length us, event | category | flops | bytes accessed | tf_op | source)
XLA Modules:
  0.0 165.2 jit_solution(2095343809395742921)
XLA Ops:
  0.0 1.1 copy.10
  1.1 5.4 %collective-permute-start.2 = (f32[128,512]{0,1:T(8,128)S(1)}, f32[128,512]{0,1:T(8,128)S(1)}, u32[]{:S(2)}, u32[]{:S(2)}) collective-permute-start(f32[128,512]{0,1:T(8,128)S(1)} %copy.10), channel_id=1, source_target_pairs={{0,16},{16,32},{32,48},{48,64},{64,80},{80,96},{96,112},{112,128},... | collective-permute-start | bytes 786440 | tf_op jit(solution)/shard_map/ppermute | solution.py:29
  6.5 11.9 %collective-permute-start.3 = (f32[128,512]{0,1:T(8,128)S(1)}, f32[128,512]{0,1:T(8,128)S(1)}, u32[]{:S(2)}, u32[]{:S(2)}) collective-permute-start(f32[128,512]{0,1:T(8,128)S(1)} %copy.10), channel_id=1, source_target_pairs={{16,0},{32,16},{48,32},{64,48},{80,64},{96,80},{112,96},{128,112},... | collective-permute-start | bytes 786440 | tf_op jit(solution)/shard_map/ppermute | solution.py:31
  19.1 8.0 %footprints.1 = (f32[256,512]{1,0:T(8,128)}, f32[256,512]{1,0:T(8,128)}) custom-call(s32[2]{0:T(128)} %and_select_fusion.start_ref, s32[1,256]{1,0:T(1,128)} %bitcast.115, f32[64,128]{1,0:T(8,128)} %bitcast.113, f32[64,128]{1,0:T(8,128)} %bitcast.112, s32[64,128]{1,0:T(8,128)} %bitcast.110, s32[64,128]{1,0:T(8,128)} %bitcast.109, f32[128,512]{1,0:T(8,128)} %cov_ref.1), custom_call_target="tpu_custom_call" | custom-call | flops 400000000 | bytes 1500000 | tf_op jit(solution)/shard_map/footprints/pallas_call | solution.py:161
  27.0 1.1 slice_select_fusion.3
  28.1 1.9 %collective-permute-start = (f32[128,512]{1,0:T(8,128)S(1)}, f32[128,512]{1,0:T(8,128)S(1)}, u32[]{:S(2)}, u32[]{:S(2)}) collective-permute-start(f32[128,512]{1,0:T(8,128)S(1)} %slice_select_fusion.3), channel_id=1, source_target_pairs={{0,16},{16,0},{1,17},{17,1},{2,18},{18,2},{3,19},{19,3},{4,20},{20... | collective-permute-start | bytes 786440 | tf_op jit(solution)/shard_map/ppermute | solution.py:271
  32.0 1.9 %collective-permute-start.4 = (f32[128,512]{0,1:T(8,128)S(1)}, f32[128,512]{0,1:T(8,128)S(1)}, u32[]{:S(2)}, u32[]{:S(2)}) collective-permute-start(f32[128,512]{0,1:T(8,128)S(1)} %fusion.22), channel_id=1, source_target_pairs={{0,16},{16,32},{32,48},{48,64},{64,80},{80,96},{96,112},{112,128},... | collective-permute-start | bytes 786440 | tf_op jit(solution)/shard_map/ppermute | solution.py:29
  33.9 2.4 %collective-permute-start.5 = (f32[128,512]{0,1:T(8,128)S(1)}, f32[128,512]{0,1:T(8,128)S(1)}, u32[]{:S(2)}, u32[]{:S(2)}) collective-permute-start(f32[128,512]{0,1:T(8,128)S(1)} %fusion.22), channel_id=1, source_target_pairs={{16,0},{32,16},{48,32},{64,48},{80,64},{96,80},{112,96},{128,112},... | collective-permute-start | bytes 786440 | tf_op jit(solution)/shard_map/ppermute | solution.py:31
  36.5 0.9 copy-done.1
  37.4 6.8 %collective-permute-start.1 = (f32[64,512]{1,0:T(8,128)S(1)}, f32[64,512]{1,0:T(8,128)S(1)}, u32[]{:S(2)}, u32[]{:S(2)}) collective-permute-start(f32[64,512]{1,0:T(8,128)S(1)} %slice_select_fusion.4), channel_id=1, source_target_pairs={{0,512},{512,0},{1,513},{513,1},{2,514},{514,2},{3,515},{515,3},{4... | collective-permute-start | bytes 393224 | tf_op jit(solution)/shard_map/ppermute | solution.py:272
  44.4 2.2 %collective-permute-done.1 = f32[64,512]{1,0:T(8,128)S(1)} collective-permute-done((f32[64,512]{1,0:T(8,128)S(1)}, f32[64,512]{1,0:T(8,128)S(1)}, u32[]{:S(2)}, u32[]{:S(2)}) %collective-permute-start.1) | collective-permute-done | bytes 131104 | tf_op jit(solution)/shard_map/ppermute | solution.py:272
  47.3 8.7 %all-to-all-start = ((f32[16,4,512]{2,1,0:T(4,128)}), f32[16,4,512]{2,1,0:T(4,128)S(1)}, u32[]{:S(2)}, u32[]{:S(2)}) async-start(f32[16,4,512]{2,1,0:T(4,128)} %reshape.157), calls=%async_computation | async-start | bytes 262144 | tf_op jit(solution)/shard_map/all_to_all | solution.py:182
  56.3 4.7 %collective-permute-start.6 = (f32[128,512]{0,1:T(8,128)S(1)}, f32[128,512]{0,1:T(8,128)S(1)}, u32[]{:S(2)}, u32[]{:S(2)}) collective-permute-start(f32[128,512]{0,1:T(8,128)S(1)} %fusion.26), channel_id=1, source_target_pairs={{0,16},{16,32},{32,48},{48,64},{64,80},{80,96},{96,112},{112,128},... | collective-permute-start | bytes 786440 | tf_op jit(solution)/shard_map/ppermute | solution.py:29
  60.9 1.9 %collective-permute-start.7 = (f32[128,512]{0,1:T(8,128)S(1)}, f32[128,512]{0,1:T(8,128)S(1)}, u32[]{:S(2)}, u32[]{:S(2)}) collective-permute-start(f32[128,512]{0,1:T(8,128)S(1)} %fusion.26), channel_id=1, source_target_pairs={{16,0},{32,16},{48,32},{64,48},{80,64},{96,80},{112,96},{128,112},... | collective-permute-start | bytes 786440 | tf_op jit(solution)/shard_map/ppermute | solution.py:31
  63.1 3.5 %collective-permute-done.6 = f32[128,512]{0,1:T(8,128)S(1)} collective-permute-done((f32[128,512]{0,1:T(8,128)S(1)}, f32[128,512]{0,1:T(8,128)S(1)}, u32[]{:S(2)}, u32[]{:S(2)}) %collective-permute-start.6) | collective-permute-done | bytes 262176 | tf_op jit(solution)/shard_map/ppermute | solution.py:29
  66.6 2.8 %collective-permute-done.7 = f32[128,512]{0,1:T(8,128)S(1)} collective-permute-done((f32[128,512]{0,1:T(8,128)S(1)}, f32[128,512]{0,1:T(8,128)S(1)}, u32[]{:S(2)}, u32[]{:S(2)}) %collective-permute-start.7) | collective-permute-done | bytes 262176 | tf_op jit(solution)/shard_map/ppermute | solution.py:31
  69.7 0.8 copy-done
  71.7 0.8 pad_maximum_fusion.4
  72.5 9.4 %all-to-all-start.1 = ((f32[16,40,128]{2,1,0:T(8,128)}), f32[16,40,128]{2,1,0:T(8,128)S(1)}, u32[]{:S(2)}, u32[]{:S(2)}) async-start(f32[16,40,128]{2,1,0:T(8,128)} %pad_maximum_fusion.4), calls=%async_computation.1 | async-start | bytes 655360 | tf_op jit(solution)/shard_map/all_to_all | solution.py:285
  81.9 12.6 %all-to-all-done.1 = f32[16,40,128]{2,1,0:T(8,128)S(1)} async-done(((f32[16,40,128]{2,1,0:T(8,128)}), f32[16,40,128]{2,1,0:T(8,128)S(1)}, u32[]{:S(2)}, u32[]{:S(2)}) %all-to-all-start.1) | async-done | bytes 327712 | tf_op jit(solution)/shard_map/all_to_all | solution.py:285
  95.4 1.3 collective-permute-start.9
  96.7 4.0 %collective-permute-start.8 = (f32[128,384]{0,1:T(8,128)S(1)}, f32[128,384]{0,1:T(8,128)S(1)}, u32[]{:S(2)}, u32[]{:S(2)}) collective-permute-start(f32[128,384]{0,1:T(8,128)S(1)} %get-tuple-element.33), channel_id=1, source_target_pairs={{0,1},{1,2},{2,3},{3,4},{4,5},{5,6},{6,7},{7,8},{8,9},{9,10},{10,1... | collective-permute-start | bytes 589832 | tf_op jit(solution)/shard_map/ppermute | solution.py:29
  101.5 9.4 %all-to-all-start.2 = ((f32[16,4,768]{2,1,0:T(4,128)}), f32[16,4,768]{2,1,0:T(4,128)S(1)}, u32[]{:S(2)}, u32[]{:S(2)}) async-start(f32[16,4,768]{2,1,0:T(4,128)} %broadcast_in_dim.150), calls=%async_computation.2 | async-start | bytes 393216 | tf_op jit(solution)/shard_map/all_to_all | solution.py:178
  111.1 0.8 fusion.4
  112.0 11.3 %all-to-all-done.2 = f32[16,4,768]{2,1,0:T(4,128)S(1)} async-done(((f32[16,4,768]{2,1,0:T(4,128)}), f32[16,4,768]{2,1,0:T(4,128)S(1)}, u32[]{:S(2)}, u32[]{:S(2)}) %all-to-all-start.2) | async-done | bytes 196640 | tf_op jit(solution)/shard_map/all_to_all | solution.py:178
  123.3 2.4 %collective-permute-start.10 = (f32[64,768]{1,0:T(8,128)S(1)}, f32[64,768]{1,0:T(8,128)S(1)}, u32[]{:S(2)}, u32[]{:S(2)}) collective-permute-start(f32[64,768]{1,0:T(8,128)S(1)} %reshape.167), channel_id=1, source_target_pairs={{0,512},{512,0},{1,513},{513,1},{2,514},{514,2},{3,515},{515,3},{4... | collective-permute-start | bytes 589832 | tf_op jit(solution)/shard_map/ppermute | solution.py:302
  125.7 4.0 %collective-permute-done.10 = f32[64,768]{1,0:T(8,128)S(1)} collective-permute-done((f32[64,768]{1,0:T(8,128)S(1)}, f32[64,768]{1,0:T(8,128)S(1)}, u32[]{:S(2)}, u32[]{:S(2)}) %collective-permute-start.10) | collective-permute-done | bytes 196640 | tf_op jit(solution)/shard_map/ppermute | solution.py:302
  129.8 8.7 %collective-permute-start.11 = (f32[128,768]{1,0:T(8,128)S(1)}, f32[128,768]{1,0:T(8,128)S(1)}, u32[]{:S(2)}, u32[]{:S(2)}) collective-permute-start(f32[128,768]{1,0:T(8,128)S(1)} %pad_maximum_fusion.3), channel_id=1, source_target_pairs={{0,16},{16,0},{1,17},{17,1},{2,18},{18,2},{3,19},{19,3},{4,20},{20... | collective-permute-start | bytes 1179656 | tf_op jit(solution)/shard_map/ppermute | solution.py:303
  141.3 8.8 %all-to-all-start.3 = ((f32[16,16,128]{2,1,0:T(8,128)}), f32[16,16,128]{2,1,0:T(8,128)S(1)}, u32[]{:S(2)}, u32[]{:S(2)}) async-start(f32[16,16,128]{2,1,0:T(8,128)} %broadcast_in_dim.151), calls=%async_computation.3 | async-start | bytes 262144 | tf_op jit(solution)/shard_map/all_to_all | solution.py:178
  150.6 12.1 %spd_inverse.1 = f32[256,256]{1,0:T(8,128)} custom-call(f32[256,256]{1,0:T(8,128)} %pad_maximum_fusion.5.s_ref, f32[1,256]{1,0:T(1,128)} %bitcast.114), custom_call_target="tpu_custom_call" | custom-call | flops 67108864 | bytes 524288 | tf_op jit(solution)/shard_map/spd_inverse/pallas_call | solution.py:89
  162.7 1.3 fusion.86
  164.0 1.2 convolution_subtract_fusion
  (99 shorter events, 10.6 us)
Async XLA Ops:
  1.1 30.6 %collective-permute-start.2 = (f32[128,512]{0,1:T(8,128)S(1)}, f32[128,512]{0,1:T(8,128)S(1)}, u32[]{:S(2)}, u32[]{:S(2)}) collective-permute-start(f32[128,512]{0,1:T(8,128)S(1)} %copy.10), channel_id=1, source_target_pairs={{0,16},{16,32},{32,48},{48,64},{64,80},{80,96},{96,112},{112,128},... | collective-permute-start | bytes 786440 | tf_op jit(solution)/shard_map/ppermute | solution.py:29
  6.5 25.3 %collective-permute-start.3 = (f32[128,512]{0,1:T(8,128)S(1)}, f32[128,512]{0,1:T(8,128)S(1)}, u32[]{:S(2)}, u32[]{:S(2)}) collective-permute-start(f32[128,512]{0,1:T(8,128)S(1)} %copy.10), channel_id=1, source_target_pairs={{16,0},{32,16},{48,32},{64,48},{80,64},{96,80},{112,96},{128,112},... | collective-permute-start | bytes 786440 | tf_op jit(solution)/shard_map/ppermute | solution.py:31
  27.0 3.0 %copy-start.4 = (f32[8192]{0:T(1024)S(1)}, f32[8192]{0:T(1024)}, u32[]{:S(2)}) copy-start(f32[8192]{0:T(1024)} %param.9) | copy-start | bytes 98308
  27.0 3.0 %copy-start.5 = (f32[8192]{0:T(1024)S(1)}, f32[8192]{0:T(1024)}, u32[]{:S(2)}) copy-start(f32[8192]{0:T(1024)} %param.8) | copy-start | bytes 98308
  28.1 8.3 %collective-permute-start = (f32[128,512]{1,0:T(8,128)S(1)}, f32[128,512]{1,0:T(8,128)S(1)}, u32[]{:S(2)}, u32[]{:S(2)}) collective-permute-start(f32[128,512]{1,0:T(8,128)S(1)} %slice_select_fusion.3), channel_id=1, source_target_pairs={{0,16},{16,0},{1,17},{17,1},{2,18},{18,2},{3,19},{19,3},{4,20},{20... | collective-permute-start | bytes 786440 | tf_op jit(solution)/shard_map/ppermute | solution.py:271
  30.1 0.8 copy-start.2
  30.1 0.8 copy-start.3
  32.0 24.1 %collective-permute-start.4 = (f32[128,512]{0,1:T(8,128)S(1)}, f32[128,512]{0,1:T(8,128)S(1)}, u32[]{:S(2)}, u32[]{:S(2)}) collective-permute-start(f32[128,512]{0,1:T(8,128)S(1)} %fusion.22), channel_id=1, source_target_pairs={{0,16},{16,32},{32,48},{48,64},{64,80},{80,96},{96,112},{112,128},... | collective-permute-start | bytes 786440 | tf_op jit(solution)/shard_map/ppermute | solution.py:29
  33.9 22.2 %collective-permute-start.5 = (f32[128,512]{0,1:T(8,128)S(1)}, f32[128,512]{0,1:T(8,128)S(1)}, u32[]{:S(2)}, u32[]{:S(2)}) collective-permute-start(f32[128,512]{0,1:T(8,128)S(1)} %fusion.22), channel_id=1, source_target_pairs={{16,0},{32,16},{48,32},{64,48},{80,64},{96,80},{112,96},{128,112},... | collective-permute-start | bytes 786440 | tf_op jit(solution)/shard_map/ppermute | solution.py:31
  36.3 1.0 copy-start.1
  37.4 9.2 %collective-permute-start.1 = (f32[64,512]{1,0:T(8,128)S(1)}, f32[64,512]{1,0:T(8,128)S(1)}, u32[]{:S(2)}, u32[]{:S(2)}) collective-permute-start(f32[64,512]{1,0:T(8,128)S(1)} %slice_select_fusion.4), channel_id=1, source_target_pairs={{0,512},{512,0},{1,513},{513,1},{2,514},{514,2},{3,515},{515,3},{4... | collective-permute-start | bytes 393224 | tf_op jit(solution)/shard_map/ppermute | solution.py:272
  47.3 23.7 %all-to-all-start = ((f32[16,4,512]{2,1,0:T(4,128)}), f32[16,4,512]{2,1,0:T(4,128)S(1)}, u32[]{:S(2)}, u32[]{:S(2)}) async-start(f32[16,4,512]{2,1,0:T(4,128)} %reshape.157), calls=%async_computation | async-start | bytes 262144 | tf_op jit(solution)/shard_map/all_to_all | solution.py:182
  56.3 10.3 %collective-permute-start.6 = (f32[128,512]{0,1:T(8,128)S(1)}, f32[128,512]{0,1:T(8,128)S(1)}, u32[]{:S(2)}, u32[]{:S(2)}) collective-permute-start(f32[128,512]{0,1:T(8,128)S(1)} %fusion.26), channel_id=1, source_target_pairs={{0,16},{16,32},{32,48},{48,64},{64,80},{80,96},{96,112},{112,128},... | collective-permute-start | bytes 786440 | tf_op jit(solution)/shard_map/ppermute | solution.py:29
  60.9 8.5 %collective-permute-start.7 = (f32[128,512]{0,1:T(8,128)S(1)}, f32[128,512]{0,1:T(8,128)S(1)}, u32[]{:S(2)}, u32[]{:S(2)}) collective-permute-start(f32[128,512]{0,1:T(8,128)S(1)} %fusion.26), channel_id=1, source_target_pairs={{16,0},{32,16},{48,32},{64,48},{80,64},{96,80},{112,96},{128,112},... | collective-permute-start | bytes 786440 | tf_op jit(solution)/shard_map/ppermute | solution.py:31
  69.4 1.0 copy-start
  72.5 22.1 %all-to-all-start.1 = ((f32[16,40,128]{2,1,0:T(8,128)}), f32[16,40,128]{2,1,0:T(8,128)S(1)}, u32[]{:S(2)}, u32[]{:S(2)}) async-start(f32[16,40,128]{2,1,0:T(8,128)} %pad_maximum_fusion.4), calls=%async_computation.1 | async-start | bytes 655360 | tf_op jit(solution)/shard_map/all_to_all | solution.py:285
  95.4 15.6 %collective-permute-start.9 = (f32[128,384]{0,1:T(8,128)S(1)}, f32[128,384]{0,1:T(8,128)S(1)}, u32[]{:S(2)}, u32[]{:S(2)}) collective-permute-start(f32[128,384]{0,1:T(8,128)S(1)} %get-tuple-element.34), channel_id=1, source_target_pairs={{1,0},{2,1},{3,2},{4,3},{5,4},{6,5},{7,6},{8,7},{9,8},{10,9},{11,1... | collective-permute-start | bytes 589832 | tf_op jit(solution)/shard_map/ppermute | solution.py:31
  96.7 14.3 %collective-permute-start.8 = (f32[128,384]{0,1:T(8,128)S(1)}, f32[128,384]{0,1:T(8,128)S(1)}, u32[]{:S(2)}, u32[]{:S(2)}) collective-permute-start(f32[128,384]{0,1:T(8,128)S(1)} %get-tuple-element.33), channel_id=1, source_target_pairs={{0,1},{1,2},{2,3},{3,4},{4,5},{5,6},{6,7},{7,8},{8,9},{9,10},{10,1... | collective-permute-start | bytes 589832 | tf_op jit(solution)/shard_map/ppermute | solution.py:29
  101.5 21.7 %all-to-all-start.2 = ((f32[16,4,768]{2,1,0:T(4,128)}), f32[16,4,768]{2,1,0:T(4,128)S(1)}, u32[]{:S(2)}, u32[]{:S(2)}) async-start(f32[16,4,768]{2,1,0:T(4,128)} %broadcast_in_dim.150), calls=%async_computation.2 | async-start | bytes 393216 | tf_op jit(solution)/shard_map/all_to_all | solution.py:178
  123.3 6.4 %collective-permute-start.10 = (f32[64,768]{1,0:T(8,128)S(1)}, f32[64,768]{1,0:T(8,128)S(1)}, u32[]{:S(2)}, u32[]{:S(2)}) collective-permute-start(f32[64,768]{1,0:T(8,128)S(1)} %reshape.167), channel_id=1, source_target_pairs={{0,512},{512,0},{1,513},{513,1},{2,514},{514,2},{3,515},{515,3},{4... | collective-permute-start | bytes 589832 | tf_op jit(solution)/shard_map/ppermute | solution.py:302
  129.8 10.1 %collective-permute-start.11 = (f32[128,768]{1,0:T(8,128)S(1)}, f32[128,768]{1,0:T(8,128)S(1)}, u32[]{:S(2)}, u32[]{:S(2)}) collective-permute-start(f32[128,768]{1,0:T(8,128)S(1)} %pad_maximum_fusion.3), channel_id=1, source_target_pairs={{0,16},{16,0},{1,17},{17,1},{2,18},{18,2},{3,19},{19,3},{4,20},{20... | collective-permute-start | bytes 1179656 | tf_op jit(solution)/shard_map/ppermute | solution.py:303
  141.3 21.4 %all-to-all-start.3 = ((f32[16,16,128]{2,1,0:T(8,128)}), f32[16,16,128]{2,1,0:T(8,128)S(1)}, u32[]{:S(2)}, u32[]{:S(2)}) async-start(f32[16,16,128]{2,1,0:T(8,128)} %broadcast_in_dim.151), calls=%async_computation.3 | async-start | bytes 262144 | tf_op jit(solution)/shard_map/all_to_all | solution.py:178

commit v6 on v5

--- a/solution.py
+++ b/solution.py
@@ -96,81 +96,89 @@
     )(s, var.reshape(1, n))
 
 
-def footprint_kernel(start_ref, site_ref, cu_ref, cv_ref, su_ref, sv_ref, cov_ref, spread_ref, rows_ref, coef_ref, near_ref, site_col_ref):
+def footprint(start_ref, site_ref, cu_ref, cv_ref, su_ref, sv_ref, out_ref, coef_ref, site_col_ref):
     nobs = site_ref.shape[1]
     bands = cu_ref.shape[0]
+    count = out_ref.shape[1] // MERIDIAN_TOTAL
+    total = count + 2 * STEPS
+    first = start_ref[0]
     chunk = 32
     lane = lax.broadcasted_iota(jnp.int32, (chunk, MERIDIAN_TOTAL), 1)
     site_col_ref[...] = jnp.broadcast_to(site_ref[...], (8, nobs)).T
-
-    def footprint(first, count, store):
-        total = count + 2 * STEPS
-        for t in range(total):
-            band = first + (t - STEPS)
-            inside = (band >= 0) & (band < bands)
-            at = pl.ds(jnp.clip(band, 0, bands - 1), 1)
-            cu = jnp.where(inside, cu_ref[at, :], 0.0)
-            cv = jnp.where(inside, cv_ref[at, :], 0.0)
-            west = jnp.where(su_ref[at, :] > 0, cu, 0.0)
-            south = jnp.where(sv_ref[at, :] > 0, cv, 0.0)
-            for k, line in enumerate((1.0 - cu - cv, west, cu - west, south, cv - south)):
-                coef_ref[5 * t + k : 5 * t + k + 1, :] = line
-
-        def coeff(t, k):
-            return coef_ref[5 * t + k : 5 * t + k + 1, :]
-
-        def body(i, carry):
-            at = pl.multiple_of(i * chunk, chunk)
-            site = site_col_ref[pl.ds(at, chunk), 0:1] - (first - STEPS) * MERIDIAN_TOTAL - lane
-            v = [(site == t * MERIDIAN_TOTAL).astype(jnp.float32) for t in range(total)]
-            for step in range(STEPS):
-                low, high = (step + 1, total - step - 1)
-                new = []
-                for t in range(low, high):
-                    w = coeff(t, 0) * v[t]
-                    w = w + pltpu.roll(coeff(t, 1) * v[t], MERIDIAN_TOTAL - 1, 1)
-                    w = w + pltpu.roll(coeff(t, 2) * v[t], 1, 1)
-                    w = w + coeff(t + 1, 3) * v[t + 1]
-                    w = w + coeff(t - 1, 4) * v[t - 1]
-                    new.append(w)
-                v = [None] * low + new + [None] * (total - high)
-            store(at, v[STEPS : STEPS + count])
-            return carry
-
-        lax.fori_loop(0, nobs // chunk, body, 0)
-
-    def store_near(at, v):
-        near_ref[pl.ds(at, chunk), :] = v[0]
-
-    def store_spread(at, v):
-        for b, w in enumerate(v):
-            spread_ref[pl.ds(at, chunk), b * MERIDIAN_TOTAL : (b + 1) * MERIDIAN_TOTAL] = w
-
-    footprint(start_ref[0], 1, store_near)
+    for t in range(total):
+        band = first + (t - STEPS)
+        inside = (band >= 0) & (band < bands)
+        at = pl.ds(jnp.clip(band, 0, bands - 1), 1)
+        cu = jnp.where(inside, cu_ref[at, :], 0.0)
+        cv = jnp.where(inside, cv_ref[at, :], 0.0)
+        west = jnp.where(su_ref[at, :] > 0, cu, 0.0)
+        south = jnp.where(sv_ref[at, :] > 0, cv, 0.0)
+        for k, line in enumerate((1.0 - cu - cv, west, cu - west, south, cv - south)):
+            coef_ref[5 * t + k : 5 * t + k + 1, :] = line
+
+    def coeff(t, k):
+        return coef_ref[5 * t + k : 5 * t + k + 1, :]
+
+    def body(i, carry):
+        at = pl.multiple_of(i * chunk, chunk)
+        site = site_col_ref[pl.ds(at, chunk), 0:1] - (first - STEPS) * MERIDIAN_TOTAL - lane
+        v = [(site == t * MERIDIAN_TOTAL).astype(jnp.float32) for t in range(total)]
+        for step in range(STEPS):
+            low, high = (step + 1, total - step - 1)
+            new = []
+            for t in range(low, high):
+                w = coeff(t, 0) * v[t]
+                w = w + pltpu.roll(coeff(t, 1) * v[t], MERIDIAN_TOTAL - 1, 1)
+                w = w + pltpu.roll(coeff(t, 2) * v[t], 1, 1)
+                w = w + coeff(t + 1, 3) * v[t + 1]
+                w = w + coeff(t - 1, 4) * v[t - 1]
+                new.append(w)
+            v = [None] * low + new + [None] * (total - high)
+        for b in range(count):
+            out_ref[pl.ds(at, chunk), b * MERIDIAN_TOTAL : (b + 1) * MERIDIAN_TOTAL] = v[STEPS + b]
+        return carry
+
+    lax.fori_loop(0, nobs // chunk, body, 0)
+
+
+def rows_kernel(start_ref, site_ref, cu_ref, cv_ref, su_ref, sv_ref, cov_ref, rows_ref, near_ref, coef_ref, site_col_ref):
+    footprint(start_ref, site_ref, cu_ref, cv_ref, su_ref, sv_ref, near_ref, coef_ref, site_col_ref)
     rows_ref[...] = jnp.dot(near_ref[...], cov_ref[...], precision=HIGHEST, preferred_element_type=jnp.float32)
-    footprint(start_ref[1], cov_ref.shape[1] // MERIDIAN_TOTAL, store_spread)
-
-
-def footprints(covariance, starts, site, *winds):
+
+
+def footprint_call(kernel, cells, nobs, width, scratch, operands):
+    vmem = pl.BlockSpec(memory_space=pltpu.VMEM)
+    total = cells // MERIDIAN_TOTAL + 2 * STEPS
+    return pl.pallas_call(
+        kernel,
+        out_shape=jax.ShapeDtypeStruct((nobs, width), jnp.float32),
+        in_specs=[pl.BlockSpec(memory_space=pltpu.SMEM)] + [vmem] * (len(operands) - 1),
+        out_specs=vmem,
+        scratch_shapes=[
+            *scratch,
+            pltpu.VMEM((5 * total + 6, MERIDIAN_TOTAL), jnp.float32),
+            pltpu.VMEM((nobs, 8), jnp.int32),
+        ],
+        cost_estimate=pl.CostEstimate(flops=200 * 1000 * 1000, bytes_accessed=900000, transcendentals=0),
+    )(*operands)
+
+
+def gridded(site, winds):
+    return [site.reshape(1, -1)] + [field.reshape(-1, MERIDIAN_TOTAL) for field in winds]
+
+
+def observed_rows(covariance, band, site, *winds):
     rows_dev, cols_dev = covariance.shape
     assert rows_dev == MERIDIAN_TOTAL
     nobs = site.shape[0]
-    bands = winds[0].shape[0] // MERIDIAN_TOTAL
-    total = cols_dev // MERIDIAN_TOTAL + 2 * STEPS
-    vmem = pl.BlockSpec(memory_space=pltpu.VMEM)
-    return pl.pallas_call(
-        footprint_kernel,
-        out_shape=[jax.ShapeDtypeStruct((nobs, cols_dev), jnp.float32)] * 2,
-        in_specs=[pl.BlockSpec(memory_space=pltpu.SMEM)] + [vmem] * 6,
-        out_specs=[vmem] * 2,
-        scratch_shapes=[
-            pltpu.VMEM((5 * total + 6, MERIDIAN_TOTAL), jnp.float32),
-            pltpu.VMEM((nobs, MERIDIAN_TOTAL), jnp.float32),
-            pltpu.VMEM((nobs, 8), jnp.int32),
-        ],
-        cost_estimate=pl.CostEstimate(flops=400 * 1000 * 1000, bytes_accessed=1500000, transcendentals=0),
-        name="footprints",
-    )(starts, site.reshape(1, nobs), *(field.reshape(bands, MERIDIAN_TOTAL) for field in winds), covariance)
+    operands = [band.reshape(1), *gridded(site, winds), covariance]
+    near = [pltpu.VMEM((nobs, rows_dev), jnp.float32)]
+    return footprint_call(rows_kernel, rows_dev, nobs, cols_dev, near, operands)
+
+
+def column_footprint(cols_dev, band, site, *winds):
+    operands = [band.reshape(1), *gridded(site, winds)]
+    return footprint_call(footprint, cols_dev, site.shape[0], cols_dev, [], operands)
 
 
 def everyone(chunk, axis):
@@ -264,12 +272,18 @@
         lax.dot_general, precision=HIGHEST, preferred_element_type=jnp.float32
     )
     winds = (lon_speed, lat_speed, lon_sign, lat_sign)
-    starts = jnp.stack([row_start, col_start]) // MERIDIAN_TOTAL
-    spread, hp = footprints(covariance, starts, measurement_site_position, *winds)
+    hp = observed_rows(
+        covariance, row_start // MERIDIAN_TOTAL, measurement_site_position, *winds
+    )
+    spread = column_footprint(
+        cols_dev, col_start // MERIDIAN_TOTAL, measurement_site_position, *winds
+    )
 
     own, other = halves(hp, 0, core)
-    own, other = halves(own + lax.ppermute(other, "co", SWAP), 0, lat_half)
-    hp = own + lax.ppermute(other, "yl", SWAP)
+    fellow = lax.ppermute(other, "co", SWAP)
+    own, other = halves(own + fellow, 0, lat_half)
+    fellow = lax.ppermute(other, "yl", SWAP)
+    hp = own + fellow
     deep = lax.axis_size("z")
     hp = scattered_sum(hp.reshape(deep, nobs // 4 // deep, cols_dev), "z")
 

time: 166 us -> 167 us (level)
  Pallas kernels: 20 us -> 21.8 us
    pallas_call x1 -> x2, Pallas kernels: 7.97 us -> 9.77 us  [footprint_call(): pl.pallas_call(kernel, out_shape=jax.ShapeDtypeStruct((nobs, width), jnp....]
  transfers between devices with their start and end apart: 16 -> 16, of which waited for: 7 -> 7; matrix products, arithmetic and copies ran while one was open for 5% -> 5% of each run, Pallas kernels for 12% -> 13%
where the time goes in v6:
time: 167 us; the launch traced here: 166 us
  starting transfers between devices  89.7 us (54%)
  waiting for transfers between devices  37 us (22%)
  Pallas kernels  21.8 us (13%)
  local copies, waits for them, and re-layouts  7.24 us (4%)
  other arithmetic  5.73 us (3%)
  matrix products  3.58 us (2%)
    all_to_all x2, starting transfers between devices, everyone(): return lax.all_to_all(copies, axis, split_axis=0, concat_axis=0, tiled=True)  18.2 us
    ppermute x4, starting transfers between devices, padded_2(): lax.ppermute(head, axis, [((i + 1) % count, i) for i in range(ends)])  17.6 us
    ppermute x4, starting transfers between devices, padded_2(): lax.ppermute(tail, axis, [(i, (i + 1) % count) for i in range(ends)])  15.9 us
    all_to_all x1, waiting for transfers between devices, shards(): lax.all_to_all(jnp.concatenate([packed, pht], axis=1), COL, split_axis=0,...  12.6 us
    pallas_call x1, Pallas kernels, spd_inverse(): pl.pallas_call(inverse_kernel, out_shape=jax.ShapeDtypeStruct((n, n), jnp...  12 us
    all_to_all x2, waiting for transfers between devices, everyone(): return lax.all_to_all(copies, axis, split_axis=0, concat_axis=0, tiled=True)  11.3 us
    pallas_call x2, Pallas kernels, footprint_call(): pl.pallas_call(kernel, out_shape=jax.ShapeDtypeStruct((nobs, width), jnp....  9.77 us
    all_to_all x1, starting transfers between devices, shards(): lax.all_to_all(jnp.concatenate([packed, pht], axis=1), COL, split_axis=0,...  9.38 us
  transfers between devices with their start and end apart: 16, of which 7 were waited for; matrix products, arithmetic and copies ran while one was open for 5% of the time, Pallas kernels for 13%

profile of v6, /device:TPU:1, one launch (start us, length us, event | category | flops | bytes accessed | tf_op | source)
XLA Modules:
  0.0 165.7 jit_solution(5813061995305637572)
XLA Ops:
  0.0 1.1 copy.10
  1.1 5.4 %collective-permute-start.2 = (f32[128,512]{0,1:T(8,128)S(1)}, f32[128,512]{0,1:T(8,128)S(1)}, u32[]{:S(2)}, u32[]{:S(2)}) collective-permute-start(f32[128,512]{0,1:T(8,128)S(1)} %copy.10), channel_id=1, source_target_pairs={{0,16},{16,32},{32,48},{48,64},{64,80},{80,96},{96,112},{112,128},... | collective-permute-start | bytes 786440 | tf_op jit(solution)/shard_map/ppermute | solution.py:29
  6.5 11.9 %collective-permute-start.3 = (f32[128,512]{0,1:T(8,128)S(1)}, f32[128,512]{0,1:T(8,128)S(1)}, u32[]{:S(2)}, u32[]{:S(2)}) collective-permute-start(f32[128,512]{0,1:T(8,128)S(1)} %copy.10), channel_id=1, source_target_pairs={{16,0},{32,16},{48,32},{64,48},{80,64},{96,80},{112,96},{128,112},... | collective-permute-start | bytes 786440 | tf_op jit(solution)/shard_map/ppermute | solution.py:31
  18.4 5.0 %shard_map.73 = f32[256,512]{1,0:T(8,128)} custom-call(s32[1]{0:T(128)} %bitcast.start_ref, s32[1,256]{1,0:T(1,128)} %bitcast.119, f32[64,128]{1,0:T(8,128)} %bitcast.115, f32[64,128]{1,0:T(8,128)} %bitcast.113, s32[64,128]{1,0:T(8,128)} %bitcast.111, s32[64,128]{1,0:T(8,128)} %bitcast.109, f32[128,512]{1,0:T(8,128)} %cov_ref.1), custom_call_target="tpu_custom_call" | custom-call | flops 200000000 | bytes 900000 | tf_op jit(solution)/shard_map/pallas_call | solution.py:152
  23.5 1.1 slice_select_fusion.3
  24.6 1.9 %collective-permute-start = (f32[128,512]{1,0:T(8,128)S(1)}, f32[128,512]{1,0:T(8,128)S(1)}, u32[]{:S(2)}, u32[]{:S(2)}) collective-permute-start(f32[128,512]{1,0:T(8,128)S(1)} %slice_select_fusion.3), channel_id=1, source_target_pairs={{0,16},{16,0},{1,17},{17,1},{2,18},{18,2},{3,19},{19,3},{4,20},{20... | collective-permute-start | bytes 786440 | tf_op jit(solution)/shard_map/ppermute | solution.py:283
  27.3 4.7 %shard_map.74 = f32[256,512]{1,0:T(8,128)} custom-call(s32[1]{0:T(128)} %bitcast.6.start_ref, s32[1,256]{1,0:T(1,128)} %bitcast.120, f32[64,128]{1,0:T(8,128)} %bitcast.116, f32[64,128]{1,0:T(8,128)} %bitcast.114, s32[64,128]{1,0:T(8,128)} %bitcast.112, s32[64,128]{1,0:T(8,128)} %bitcast.110), custom_call_target="tpu_custom_call" | custom-call | flops 200000000 | bytes 900000 | tf_op jit(solution)/shard_map/pallas_call | solution.py:152
  32.5 1.9 %collective-permute-start.4 = (f32[128,512]{0,1:T(8,128)S(1)}, f32[128,512]{0,1:T(8,128)S(1)}, u32[]{:S(2)}, u32[]{:S(2)}) collective-permute-start(f32[128,512]{0,1:T(8,128)S(1)} %fusion.22), channel_id=1, source_target_pairs={{0,16},{16,32},{32,48},{48,64},{64,80},{80,96},{96,112},{112,128},... | collective-permute-start | bytes 786440 | tf_op jit(solution)/shard_map/ppermute | solution.py:29
  34.4 2.4 %collective-permute-start.5 = (f32[128,512]{0,1:T(8,128)S(1)}, f32[128,512]{0,1:T(8,128)S(1)}, u32[]{:S(2)}, u32[]{:S(2)}) collective-permute-start(f32[128,512]{0,1:T(8,128)S(1)} %fusion.22), channel_id=1, source_target_pairs={{16,0},{32,16},{48,32},{64,48},{80,64},{96,80},{112,96},{128,112},... | collective-permute-start | bytes 786440 | tf_op jit(solution)/shard_map/ppermute | solution.py:31
  37.0 0.9 copy-done
  38.0 6.8 %collective-permute-start.1 = (f32[64,512]{1,0:T(8,128)S(1)}, f32[64,512]{1,0:T(8,128)S(1)}, u32[]{:S(2)}, u32[]{:S(2)}) collective-permute-start(f32[64,512]{1,0:T(8,128)S(1)} %slice_select_fusion.4), channel_id=1, source_target_pairs={{0,512},{512,0},{1,513},{513,1},{2,514},{514,2},{3,515},{515,3},{4... | collective-permute-start | bytes 393224 | tf_op jit(solution)/shard_map/ppermute | solution.py:285
  44.9 2.2 %collective-permute-done.1 = f32[64,512]{1,0:T(8,128)S(1)} collective-permute-done((f32[64,512]{1,0:T(8,128)S(1)}, f32[64,512]{1,0:T(8,128)S(1)}, u32[]{:S(2)}, u32[]{:S(2)}) %collective-permute-start.1) | collective-permute-done | bytes 131104 | tf_op jit(solution)/shard_map/ppermute | solution.py:285
  47.8 8.7 %all-to-all-start = ((f32[16,4,512]{2,1,0:T(4,128)}), f32[16,4,512]{2,1,0:T(4,128)S(1)}, u32[]{:S(2)}, u32[]{:S(2)}) async-start(f32[16,4,512]{2,1,0:T(4,128)} %reshape.169), calls=%async_computation | async-start | bytes 262144 | tf_op jit(solution)/shard_map/all_to_all | solution.py:190
  56.8 4.7 %collective-permute-start.6 = (f32[128,512]{0,1:T(8,128)S(1)}, f32[128,512]{0,1:T(8,128)S(1)}, u32[]{:S(2)}, u32[]{:S(2)}) collective-permute-start(f32[128,512]{0,1:T(8,128)S(1)} %fusion.26), channel_id=1, source_target_pairs={{0,16},{16,32},{32,48},{48,64},{64,80},{80,96},{96,112},{112,128},... | collective-permute-start | bytes 786440 | tf_op jit(solution)/shard_map/ppermute | solution.py:29
  61.4 1.9 %collective-permute-start.7 = (f32[128,512]{0,1:T(8,128)S(1)}, f32[128,512]{0,1:T(8,128)S(1)}, u32[]{:S(2)}, u32[]{:S(2)}) collective-permute-start(f32[128,512]{0,1:T(8,128)S(1)} %fusion.26), channel_id=1, source_target_pairs={{16,0},{32,16},{48,32},{64,48},{80,64},{96,80},{112,96},{128,112},... | collective-permute-start | bytes 786440 | tf_op jit(solution)/shard_map/ppermute | solution.py:31
  63.6 3.5 %collective-permute-done.6 = f32[128,512]{0,1:T(8,128)S(1)} collective-permute-done((f32[128,512]{0,1:T(8,128)S(1)}, f32[128,512]{0,1:T(8,128)S(1)}, u32[]{:S(2)}, u32[]{:S(2)}) %collective-permute-start.6) | collective-permute-done | bytes 262176 | tf_op jit(solution)/shard_map/ppermute | solution.py:29
  67.1 2.8 %collective-permute-done.7 = f32[128,512]{0,1:T(8,128)S(1)} collective-permute-done((f32[128,512]{0,1:T(8,128)S(1)}, f32[128,512]{0,1:T(8,128)S(1)}, u32[]{:S(2)}, u32[]{:S(2)}) %collective-permute-start.7) | collective-permute-done | bytes 262176 | tf_op jit(solution)/shard_map/ppermute | solution.py:31
  70.2 0.8 copy-done.1
  73.0 9.4 %all-to-all-start.1 = ((f32[16,40,128]{2,1,0:T(8,128)}), f32[16,40,128]{2,1,0:T(8,128)S(1)}, u32[]{:S(2)}, u32[]{:S(2)}) async-start(f32[16,40,128]{2,1,0:T(8,128)} %pad_maximum_fusion.4), calls=%async_computation.1 | async-start | bytes 655360 | tf_op jit(solution)/shard_map/all_to_all | solution.py:299
  82.4 12.6 %all-to-all-done.1 = f32[16,40,128]{2,1,0:T(8,128)S(1)} async-done(((f32[16,40,128]{2,1,0:T(8,128)}), f32[16,40,128]{2,1,0:T(8,128)S(1)}, u32[]{:S(2)}, u32[]{:S(2)}) %all-to-all-start.1) | async-done | bytes 327712 | tf_op jit(solution)/shard_map/all_to_all | solution.py:299
  95.9 1.3 collective-permute-start.9
  97.2 4.0 %collective-permute-start.8 = (f32[128,384]{0,1:T(8,128)S(1)}, f32[128,384]{0,1:T(8,128)S(1)}, u32[]{:S(2)}, u32[]{:S(2)}) collective-permute-start(f32[128,384]{0,1:T(8,128)S(1)} %get-tuple-element.29), channel_id=1, source_target_pairs={{0,1},{1,2},{2,3},{3,4},{4,5},{5,6},{6,7},{7,8},{8,9},{9,10},{10,1... | collective-permute-start | bytes 589832 | tf_op jit(solution)/shard_map/ppermute | solution.py:29
  102.0 9.4 %all-to-all-start.2 = ((f32[16,4,768]{2,1,0:T(4,128)}), f32[16,4,768]{2,1,0:T(4,128)S(1)}, u32[]{:S(2)}, u32[]{:S(2)}) async-start(f32[16,4,768]{2,1,0:T(4,128)} %broadcast_in_dim.150), calls=%async_computation.2 | async-start | bytes 393216 | tf_op jit(solution)/shard_map/all_to_all | solution.py:186
  111.6 0.8 fusion.4
  112.5 11.3 %all-to-all-done.2 = f32[16,4,768]{2,1,0:T(4,128)S(1)} async-done(((f32[16,4,768]{2,1,0:T(4,128)}), f32[16,4,768]{2,1,0:T(4,128)S(1)}, u32[]{:S(2)}, u32[]{:S(2)}) %all-to-all-start.2) | async-done | bytes 196640 | tf_op jit(solution)/shard_map/all_to_all | solution.py:186
  123.8 2.4 %collective-permute-start.10 = (f32[64,768]{1,0:T(8,128)S(1)}, f32[64,768]{1,0:T(8,128)S(1)}, u32[]{:S(2)}, u32[]{:S(2)}) collective-permute-start(f32[64,768]{1,0:T(8,128)S(1)} %reshape.180), channel_id=1, source_target_pairs={{0,512},{512,0},{1,513},{513,1},{2,514},{514,2},{3,515},{515,3},{4... | collective-permute-start | bytes 589832 | tf_op jit(solution)/shard_map/ppermute | solution.py:316
  126.2 4.0 %collective-permute-done.10 = f32[64,768]{1,0:T(8,128)S(1)} collective-permute-done((f32[64,768]{1,0:T(8,128)S(1)}, f32[64,768]{1,0:T(8,128)S(1)}, u32[]{:S(2)}, u32[]{:S(2)}) %collective-permute-start.10) | collective-permute-done | bytes 196640 | tf_op jit(solution)/shard_map/ppermute | solution.py:316
  130.3 8.7 %collective-permute-start.11 = (f32[128,768]{1,0:T(8,128)S(1)}, f32[128,768]{1,0:T(8,128)S(1)}, u32[]{:S(2)}, u32[]{:S(2)}) collective-permute-start(f32[128,768]{1,0:T(8,128)S(1)} %pad_maximum_fusion.3), channel_id=1, source_target_pairs={{0,16},{16,0},{1,17},{17,1},{2,18},{18,2},{3,19},{19,3},{4,20},{20... | collective-permute-start | bytes 1179656 | tf_op jit(solution)/shard_map/ppermute | solution.py:317
  141.8 8.8 %all-to-all-start.3 = ((f32[16,16,128]{2,1,0:T(8,128)}), f32[16,16,128]{2,1,0:T(8,128)S(1)}, u32[]{:S(2)}, u32[]{:S(2)}) async-start(f32[16,16,128]{2,1,0:T(8,128)} %broadcast_in_dim.151), calls=%async_computation.3 | async-start | bytes 262144 | tf_op jit(solution)/shard_map/all_to_all | solution.py:186
  151.1 12.0 %spd_inverse.1 = f32[256,256]{1,0:T(8,128)} custom-call(f32[256,256]{1,0:T(8,128)} %pad_maximum_fusion.5.s_ref, f32[1,256]{1,0:T(1,128)} %bitcast.118), custom_call_target="tpu_custom_call" | custom-call | flops 67108864 | bytes 524288 | tf_op jit(solution)/shard_map/spd_inverse/pallas_call | solution.py:89
  163.2 1.3 fusion.86
  164.5 1.2 convolution_subtract_fusion
  (99 shorter events, 10.1 us)
Async XLA Ops:
  1.1 31.1 %collective-permute-start.2 = (f32[128,512]{0,1:T(8,128)S(1)}, f32[128,512]{0,1:T(8,128)S(1)}, u32[]{:S(2)}, u32[]{:S(2)}) collective-permute-start(f32[128,512]{0,1:T(8,128)S(1)} %copy.10), channel_id=1, source_target_pairs={{0,16},{16,32},{32,48},{48,64},{64,80},{80,96},{96,112},{112,128},... | collective-permute-start | bytes 786440 | tf_op jit(solution)/shard_map/ppermute | solution.py:29
  6.5 25.8 %collective-permute-start.3 = (f32[128,512]{0,1:T(8,128)S(1)}, f32[128,512]{0,1:T(8,128)S(1)}, u32[]{:S(2)}, u32[]{:S(2)}) collective-permute-start(f32[128,512]{0,1:T(8,128)S(1)} %copy.10), channel_id=1, source_target_pairs={{16,0},{32,16},{48,32},{64,48},{80,64},{96,80},{112,96},{128,112},... | collective-permute-start | bytes 786440 | tf_op jit(solution)/shard_map/ppermute | solution.py:31
  23.5 3.1 %copy-start.4 = (f32[8192]{0:T(1024)S(1)}, f32[8192]{0:T(1024)}, u32[]{:S(2)}) copy-start(f32[8192]{0:T(1024)} %param.9) | copy-start | bytes 98308
  23.5 3.1 %copy-start.5 = (f32[8192]{0:T(1024)S(1)}, f32[8192]{0:T(1024)}, u32[]{:S(2)}) copy-start(f32[8192]{0:T(1024)} %param.8) | copy-start | bytes 98308
  23.5 3.2 %copy-start.3 = (s32[8192]{0:T(1024)S(1)}, s32[8192]{0:T(1024)}, u32[]{:S(2)}) copy-start(s32[8192]{0:T(1024)} %param.10) | copy-start | bytes 98308
  24.6 2.1 %copy-start.2 = (s32[8192]{0:T(1024)S(1)}, s32[8192]{0:T(1024)}, u32[]{:S(2)}) copy-start(s32[8192]{0:T(1024)} %param.11) | copy-start | bytes 98308
  24.6 12.4 %collective-permute-start = (f32[128,512]{1,0:T(8,128)S(1)}, f32[128,512]{1,0:T(8,128)S(1)}, u32[]{:S(2)}, u32[]{:S(2)}) collective-permute-start(f32[128,512]{1,0:T(8,128)S(1)} %slice_select_fusion.3), channel_id=1, source_target_pairs={{0,16},{16,0},{1,17},{17,1},{2,18},{18,2},{3,19},{19,3},{4,20},{20... | collective-permute-start | bytes 786440 | tf_op jit(solution)/shard_map/ppermute | solution.py:283
  32.5 24.1 %collective-permute-start.4 = (f32[128,512]{0,1:T(8,128)S(1)}, f32[128,512]{0,1:T(8,128)S(1)}, u32[]{:S(2)}, u32[]{:S(2)}) collective-permute-start(f32[128,512]{0,1:T(8,128)S(1)} %fusion.22), channel_id=1, source_target_pairs={{0,16},{16,32},{32,48},{48,64},{64,80},{80,96},{96,112},{112,128},... | collective-permute-start | bytes 786440 | tf_op jit(solution)/shard_map/ppermute | solution.py:29
  34.4 22.2 %collective-permute-start.5 = (f32[128,512]{0,1:T(8,128)S(1)}, f32[128,512]{0,1:T(8,128)S(1)}, u32[]{:S(2)}, u32[]{:S(2)}) collective-permute-start(f32[128,512]{0,1:T(8,128)S(1)} %fusion.22), channel_id=1, source_target_pairs={{16,0},{32,16},{48,32},{64,48},{80,64},{96,80},{112,96},{128,112},... | collective-permute-start | bytes 786440 | tf_op jit(solution)/shard_map/ppermute | solution.py:31
  36.8 1.0 copy-start
  38.0 9.2 %collective-permute-start.1 = (f32[64,512]{1,0:T(8,128)S(1)}, f32[64,512]{1,0:T(8,128)S(1)}, u32[]{:S(2)}, u32[]{:S(2)}) collective-permute-start(f32[64,512]{1,0:T(8,128)S(1)} %slice_select_fusion.4), channel_id=1, source_target_pairs={{0,512},{512,0},{1,513},{513,1},{2,514},{514,2},{3,515},{515,3},{4... | collective-permute-start | bytes 393224 | tf_op jit(solution)/shard_map/ppermute | solution.py:285
  47.8 23.7 %all-to-all-start = ((f32[16,4,512]{2,1,0:T(4,128)}), f32[16,4,512]{2,1,0:T(4,128)S(1)}, u32[]{:S(2)}, u32[]{:S(2)}) async-start(f32[16,4,512]{2,1,0:T(4,128)} %reshape.169), calls=%async_computation | async-start | bytes 262144 | tf_op jit(solution)/shard_map/all_to_all | solution.py:190
  56.8 10.3 %collective-permute-start.6 = (f32[128,512]{0,1:T(8,128)S(1)}, f32[128,512]{0,1:T(8,128)S(1)}, u32[]{:S(2)}, u32[]{:S(2)}) collective-permute-start(f32[128,512]{0,1:T(8,128)S(1)} %fusion.26), channel_id=1, source_target_pairs={{0,16},{16,32},{32,48},{48,64},{64,80},{80,96},{96,112},{112,128},... | collective-permute-start | bytes 786440 | tf_op jit(solution)/shard_map/ppermute | solution.py:29
  61.4 8.5 %collective-permute-start.7 = (f32[128,512]{0,1:T(8,128)S(1)}, f32[128,512]{0,1:T(8,128)S(1)}, u32[]{:S(2)}, u32[]{:S(2)}) collective-permute-start(f32[128,512]{0,1:T(8,128)S(1)} %fusion.26), channel_id=1, source_target_pairs={{16,0},{32,16},{48,32},{64,48},{80,64},{96,80},{112,96},{128,112},... | collective-permute-start | bytes 786440 | tf_op jit(solution)/shard_map/ppermute | solution.py:31
  69.9 1.0 copy-start.1
  73.0 22.1 %all-to-all-start.1 = ((f32[16,40,128]{2,1,0:T(8,128)}), f32[16,40,128]{2,1,0:T(8,128)S(1)}, u32[]{:S(2)}, u32[]{:S(2)}) async-start(f32[16,40,128]{2,1,0:T(8,128)} %pad_maximum_fusion.4), calls=%async_computation.1 | async-start | bytes 655360 | tf_op jit(solution)/shard_map/all_to_all | solution.py:299
  95.9 15.5 %collective-permute-start.9 = (f32[128,384]{0,1:T(8,128)S(1)}, f32[128,384]{0,1:T(8,128)S(1)}, u32[]{:S(2)}, u32[]{:S(2)}) collective-permute-start(f32[128,384]{0,1:T(8,128)S(1)} %get-tuple-element.30), channel_id=1, source_target_pairs={{1,0},{2,1},{3,2},{4,3},{5,4},{6,5},{7,6},{8,7},{9,8},{10,9},{11,1... | collective-permute-start | bytes 589832 | tf_op jit(solution)/shard_map/ppermute | solution.py:31
  97.2 14.3 %collective-permute-start.8 = (f32[128,384]{0,1:T(8,128)S(1)}, f32[128,384]{0,1:T(8,128)S(1)}, u32[]{:S(2)}, u32[]{:S(2)}) collective-permute-start(f32[128,384]{0,1:T(8,128)S(1)} %get-tuple-element.29), channel_id=1, source_target_pairs={{0,1},{1,2},{2,3},{3,4},{4,5},{5,6},{6,7},{7,8},{8,9},{9,10},{10,1... | collective-permute-start | bytes 589832 | tf_op jit(solution)/shard_map/ppermute | solution.py:29
  102.0 21.7 %all-to-all-start.2 = ((f32[16,4,768]{2,1,0:T(4,128)}), f32[16,4,768]{2,1,0:T(4,128)S(1)}, u32[]{:S(2)}, u32[]{:S(2)}) async-start(f32[16,4,768]{2,1,0:T(4,128)} %broadcast_in_dim.150), calls=%async_computation.2 | async-start | bytes 393216 | tf_op jit(solution)/shard_map/all_to_all | solution.py:186
  123.8 6.4 %collective-permute-start.10 = (f32[64,768]{1,0:T(8,128)S(1)}, f32[64,768]{1,0:T(8,128)S(1)}, u32[]{:S(2)}, u32[]{:S(2)}) collective-permute-start(f32[64,768]{1,0:T(8,128)S(1)} %reshape.180), channel_id=1, source_target_pairs={{0,512},{512,0},{1,513},{513,1},{2,514},{514,2},{3,515},{515,3},{4... | collective-permute-start | bytes 589832 | tf_op jit(solution)/shard_map/ppermute | solution.py:316
  130.3 10.1 %collective-permute-start.11 = (f32[128,768]{1,0:T(8,128)S(1)}, f32[128,768]{1,0:T(8,128)S(1)}, u32[]{:S(2)}, u32[]{:S(2)}) collective-permute-start(f32[128,768]{1,0:T(8,128)S(1)} %pad_maximum_fusion.3), channel_id=1, source_target_pairs={{0,16},{16,0},{1,17},{17,1},{2,18},{18,2},{3,19},{19,3},{4,20},{20... | collective-permute-start | bytes 1179656 | tf_op jit(solution)/shard_map/ppermute | solution.py:317
  141.8 21.4 %all-to-all-start.3 = ((f32[16,16,128]{2,1,0:T(8,128)}), f32[16,16,128]{2,1,0:T(8,128)S(1)}, u32[]{:S(2)}, u32[]{:S(2)}) async-start(f32[16,16,128]{2,1,0:T(8,128)} %broadcast_in_dim.151), calls=%async_computation.3 | async-start | bytes 262144 | tf_op jit(solution)/shard_map/all_to_all | solution.py:186

commit v7 on v6

--- a/solution.py
+++ b/solution.py
@@ -206,6 +206,11 @@
     )
 
 
+def doubled(part, axis, reach):
+    fellow = lax.ppermute(part, axis, [(i, i ^ reach) for i in range(lax.axis_size(axis))])
+    return joined(part, fellow, 0, (lax.axis_index(axis) >> (reach.bit_length() - 1)) & 1)
+
+
 def row_transported(cells, lon_speed, lat_speed, lon_sign, lat_sign, row_start):
     rows_dev, width = cells.shape
     row_bands = rows_dev // MERIDIAN_TOTAL
@@ -313,12 +318,14 @@
     block = everyone(block, "z").reshape(nobs // 4, cols_dev + nobs)
     forecast = padded_2(forecast, ((COL, 1),), margin)
     forecast = col_transported(forecast, fields)
-    block = joined(block, lax.ppermute(block, "yl", SWAP), 0, lat_half)
-    block = joined(block, lax.ppermute(block, "co", SWAP), 0, core)
+    fellow = lax.ppermute(block, "yl", SWAP)
+    block = joined(block, fellow, 0, lat_half)
+    fellow = lax.ppermute(block, "co", SWAP)
+    block = joined(block, fellow, 0, core)
     hp, hpht = block[:, :cols_dev], block[:, cols_dev:]
 
-    pht, hpht = lax.optimization_barrier((pht, hpht))
-    pht = everyone(pht, COL).reshape(nobs, rows_dev)
+    for axis, reach in (("x", 1), ("x", 2), ("yh", 1), ("yh", 2)):
+        pht = doubled(pht, axis, reach)
     inverse = spd_inverse(hpht, obs_var)
     gain = dot(inverse, pht, (((1,), (0,)), ((), ())))
     return forecast - dot(gain, hp, (((0,), (0,)), ((), ())))

time: 167 us -> 179 us (1.072)
  starting transfers between devices: 89.7 us -> 97.4 us
  waiting for transfers between devices: 37 us -> 40.5 us
    ppermute x2 -> x6, starting transfers between devices: 11.1 us -> 27.6 us  [the longest x4 16.8 us: doubled(): lax.ppermute(part, axis, [(i, i ^ reach) for i in range(lax.axis_size(axi...]
    all_to_all x2 -> x1, starting transfers between devices: 18.2 us -> 9.51 us  [everyone(): return lax.all_to_all(copies, axis, split_axis=0, concat_axis=0, tiled=True)]
    ppermute x2 -> x6, waiting for transfers between devices: 4.64 us -> 8.79 us  [the longest x1 4.44 us: shards(): fellow = lax.ppermute(block, 'yl', SWAP)]
    all_to_all x2 -> x1, waiting for transfers between devices: 11.3 us -> 10.6 us  [everyone(): return lax.all_to_all(copies, axis, split_axis=0, concat_axis=0, tiled=True)]
  transfers between devices with their start and end apart: 16 -> 19, of which waited for: 7 -> 9; matrix products, arithmetic and copies ran while one was open for 5% -> 4% of each run, Pallas kernels for 13% -> 6%
where the time goes in v7:
time: 179 us; the launch traced here: 176 us
  starting transfers between devices  97.4 us (54%)
  waiting for transfers between devices  40.5 us (23%)
  Pallas kernels  21.8 us (12%)
  local copies, waits for them, and re-layouts  6.57 us (4%)
  other arithmetic  5.76 us (3%)
  matrix products  3.57 us (2%)
    ppermute x4, starting transfers between devices, padded_2(): lax.ppermute(head, axis, [((i + 1) % count, i) for i in range(ends)])  17.6 us
    ppermute x4, starting transfers between devices, doubled(): lax.ppermute(part, axis, [(i, i ^ reach) for i in range(lax.axis_size(axi...  16.8 us
    ppermute x4, starting transfers between devices, padded_2(): lax.ppermute(tail, axis, [(i, (i + 1) % count) for i in range(ends)])  15.9 us
    all_to_all x1, waiting for transfers between devices, shards(): lax.all_to_all(jnp.concatenate([packed, pht], axis=1), COL, split_axis=0,...  12.6 us
    pallas_call x1, Pallas kernels, spd_inverse(): pl.pallas_call(inverse_kernel, out_shape=jax.ShapeDtypeStruct((n, n), jnp...  12.1 us
    all_to_all x1, waiting for transfers between devices, everyone(): return lax.all_to_all(copies, axis, split_axis=0, concat_axis=0, tiled=True)  10.6 us
    pallas_call x2, Pallas kernels, footprint_call(): pl.pallas_call(kernel, out_shape=jax.ShapeDtypeStruct((nobs, width), jnp....  9.77 us
    all_to_all x1, starting transfers between devices, everyone(): return lax.all_to_all(copies, axis, split_axis=0, concat_axis=0, tiled=True)  9.51 us
  transfers between devices with their start and end apart: 19, of which 9 were waited for; matrix products, arithmetic and copies ran while one was open for 4% of the time, Pallas kernels for 6%

profile of v7, /device:TPU:1, one launch (start us, length us, event | category | flops | bytes accessed | tf_op | source)
XLA Modules:
  0.0 176.4 jit_solution(8239737952948481362)
XLA Ops:
  1.1 5.4 %collective-permute-start.2 = (f32[128,512]{0,1:T(8,128)S(1)}, f32[128,512]{0,1:T(8,128)S(1)}, u32[]{:S(2)}, u32[]{:S(2)}) collective-permute-start(f32[128,512]{0,1:T(8,128)S(1)} %copy.10), channel_id=1, source_target_pairs={{0,16},{16,32},{32,48},{48,64},{64,80},{80,96},{96,112},{112,128},... | collective-permute-start | bytes 786440 | tf_op jit(solution)/shard_map/ppermute | solution.py:29
  6.5 11.9 %collective-permute-start.3 = (f32[128,512]{0,1:T(8,128)S(1)}, f32[128,512]{0,1:T(8,128)S(1)}, u32[]{:S(2)}, u32[]{:S(2)}) collective-permute-start(f32[128,512]{0,1:T(8,128)S(1)} %copy.10), channel_id=1, source_target_pairs={{16,0},{32,16},{48,32},{64,48},{80,64},{96,80},{112,96},{128,112},... | collective-permute-start | bytes 786440 | tf_op jit(solution)/shard_map/ppermute | solution.py:31
  18.4 5.0 %shard_map.73 = f32[256,512]{1,0:T(8,128)} custom-call(s32[1]{0:T(128)} %bitcast.start_ref, s32[1,256]{1,0:T(1,128)} %bitcast.116, f32[64,128]{1,0:T(8,128)} %bitcast.112, f32[64,128]{1,0:T(8,128)} %bitcast.110, s32[64,128]{1,0:T(8,128)} %bitcast.108, s32[64,128]{1,0:T(8,128)} %bitcast.106, f32[128,512]{1,0:T(8,128)} %cov_ref.1), custom_call_target="tpu_custom_call" | custom-call | flops 200000000 | bytes 900000 | tf_op jit(solution)/shard_map/pallas_call | solution.py:152
  24.6 1.9 %collective-permute-start = (f32[128,512]{1,0:T(8,128)S(1)}, f32[128,512]{1,0:T(8,128)S(1)}, u32[]{:S(2)}, u32[]{:S(2)}) collective-permute-start(f32[128,512]{1,0:T(8,128)S(1)} %slice_select_fusion.3), channel_id=1, source_target_pairs={{0,16},{16,0},{1,17},{17,1},{2,18},{18,2},{3,19},{19,3},{4,20},{20... | collective-permute-start | bytes 786440 | tf_op jit(solution)/shard_map/ppermute | solution.py:288
  27.4 4.8 %shard_map.74 = f32[256,512]{1,0:T(8,128)} custom-call(s32[1]{0:T(128)} %bitcast.6.start_ref, s32[1,256]{1,0:T(1,128)} %bitcast.117, f32[64,128]{1,0:T(8,128)} %bitcast.113, f32[64,128]{1,0:T(8,128)} %bitcast.111, s32[64,128]{1,0:T(8,128)} %bitcast.109, s32[64,128]{1,0:T(8,128)} %bitcast.107), custom_call_target="tpu_custom_call" | custom-call | flops 200000000 | bytes 900000 | tf_op jit(solution)/shard_map/pallas_call | solution.py:152
  32.5 1.9 %collective-permute-start.4 = (f32[128,512]{0,1:T(8,128)S(1)}, f32[128,512]{0,1:T(8,128)S(1)}, u32[]{:S(2)}, u32[]{:S(2)}) collective-permute-start(f32[128,512]{0,1:T(8,128)S(1)} %fusion.22), channel_id=1, source_target_pairs={{0,16},{16,32},{32,48},{48,64},{64,80},{80,96},{96,112},{112,128},... | collective-permute-start | bytes 786440 | tf_op jit(solution)/shard_map/ppermute | solution.py:29
  34.4 2.4 %collective-permute-start.5 = (f32[128,512]{0,1:T(8,128)S(1)}, f32[128,512]{0,1:T(8,128)S(1)}, u32[]{:S(2)}, u32[]{:S(2)}) collective-permute-start(f32[128,512]{0,1:T(8,128)S(1)} %fusion.22), channel_id=1, source_target_pairs={{16,0},{32,16},{48,32},{64,48},{80,64},{96,80},{112,96},{128,112},... | collective-permute-start | bytes 786440 | tf_op jit(solution)/shard_map/ppermute | solution.py:31
  38.0 6.8 %collective-permute-start.1 = (f32[64,512]{1,0:T(8,128)S(1)}, f32[64,512]{1,0:T(8,128)S(1)}, u32[]{:S(2)}, u32[]{:S(2)}) collective-permute-start(f32[64,512]{1,0:T(8,128)S(1)} %slice_select_fusion.4), channel_id=1, source_target_pairs={{0,512},{512,0},{1,513},{513,1},{2,514},{514,2},{3,515},{515,3},{4... | collective-permute-start | bytes 393224 | tf_op jit(solution)/shard_map/ppermute | solution.py:290
  44.9 2.2 %collective-permute-done.1 = f32[64,512]{1,0:T(8,128)S(1)} collective-permute-done((f32[64,512]{1,0:T(8,128)S(1)}, f32[64,512]{1,0:T(8,128)S(1)}, u32[]{:S(2)}, u32[]{:S(2)}) %collective-permute-start.1) | collective-permute-done | bytes 131104 | tf_op jit(solution)/shard_map/ppermute | solution.py:290
  47.9 8.7 %all-to-all-start = ((f32[16,4,512]{2,1,0:T(4,128)}), f32[16,4,512]{2,1,0:T(4,128)S(1)}, u32[]{:S(2)}, u32[]{:S(2)}) async-start(f32[16,4,512]{2,1,0:T(4,128)} %reshape.166), calls=%async_computation | async-start | bytes 262144 | tf_op jit(solution)/shard_map/all_to_all | solution.py:190
  56.8 4.7 %collective-permute-start.6 = (f32[128,512]{0,1:T(8,128)S(1)}, f32[128,512]{0,1:T(8,128)S(1)}, u32[]{:S(2)}, u32[]{:S(2)}) collective-permute-start(f32[128,512]{0,1:T(8,128)S(1)} %fusion.26), channel_id=1, source_target_pairs={{0,16},{16,32},{32,48},{48,64},{64,80},{80,96},{96,112},{112,128},... | collective-permute-start | bytes 786440 | tf_op jit(solution)/shard_map/ppermute | solution.py:29
  61.5 1.9 %collective-permute-start.7 = (f32[128,512]{0,1:T(8,128)S(1)}, f32[128,512]{0,1:T(8,128)S(1)}, u32[]{:S(2)}, u32[]{:S(2)}) collective-permute-start(f32[128,512]{0,1:T(8,128)S(1)} %fusion.26), channel_id=1, source_target_pairs={{16,0},{32,16},{48,32},{64,48},{80,64},{96,80},{112,96},{128,112},... | collective-permute-start | bytes 786440 | tf_op jit(solution)/shard_map/ppermute | solution.py:31
  63.7 3.5 %collective-permute-done.6 = f32[128,512]{0,1:T(8,128)S(1)} collective-permute-done((f32[128,512]{0,1:T(8,128)S(1)}, f32[128,512]{0,1:T(8,128)S(1)}, u32[]{:S(2)}, u32[]{:S(2)}) %collective-permute-start.6) | collective-permute-done | bytes 262176 | tf_op jit(solution)/shard_map/ppermute | solution.py:29
  67.1 2.8 %collective-permute-done.7 = f32[128,512]{0,1:T(8,128)S(1)} collective-permute-done((f32[128,512]{0,1:T(8,128)S(1)}, f32[128,512]{0,1:T(8,128)S(1)}, u32[]{:S(2)}, u32[]{:S(2)}) %collective-permute-start.7) | collective-permute-done | bytes 262176 | tf_op jit(solution)/shard_map/ppermute | solution.py:31
  73.0 9.4 %all-to-all-start.1 = ((f32[16,40,128]{2,1,0:T(8,128)}), f32[16,40,128]{2,1,0:T(8,128)S(1)}, u32[]{:S(2)}, u32[]{:S(2)}) async-start(f32[16,40,128]{2,1,0:T(8,128)} %pad_maximum_fusion.4), calls=%async_computation.1 | async-start | bytes 655360 | tf_op jit(solution)/shard_map/all_to_all | solution.py:304
  82.4 12.6 %all-to-all-done.1 = f32[16,40,128]{2,1,0:T(8,128)S(1)} async-done(((f32[16,40,128]{2,1,0:T(8,128)}), f32[16,40,128]{2,1,0:T(8,128)S(1)}, u32[]{:S(2)}, u32[]{:S(2)}) %all-to-all-start.1) | async-done | bytes 327712 | tf_op jit(solution)/shard_map/all_to_all | solution.py:304
  95.8 2.4 %collective-permute-start.12 = (f32[16,128]{1,0:T(8,128)S(1)}, f32[16,128]{1,0:T(8,128)S(1)}, u32[]{:S(2)}, u32[]{:S(2)}) collective-permute-start(f32[16,128]{1,0:T(8,128)S(1)} %slice_reduce_fusion), channel_id=1, source_target_pairs={{0,1},{1,0},{2,3},{3,2},{4,5},{5,4},{6,7},{7,6},{8,9},{9,8},{10,11... | collective-permute-start | bytes 24584 | tf_op jit(solution)/shard_map/ppermute | solution.py:210
  98.3 1.9 %collective-permute-done.12 = f32[16,128]{1,0:T(8,128)S(1)} collective-permute-done((f32[16,128]{1,0:T(8,128)S(1)}, f32[16,128]{1,0:T(8,128)S(1)}, u32[]{:S(2)}, u32[]{:S(2)}) %collective-permute-start.12) | collective-permute-done | bytes 8224 | tf_op jit(solution)/shard_map/ppermute | solution.py:210
  100.2 2.7 %collective-permute-start.13 = (f32[32,128]{1,0:T(8,128)S(1)}, f32[32,128]{1,0:T(8,128)S(1)}, u32[]{:S(2)}, u32[]{:S(2)}) collective-permute-start(f32[32,128]{1,0:T(8,128)S(1)} %pad_maximum_fusion.9), channel_id=1, source_target_pairs={{0,2},{1,3},{2,0},{3,1},{4,6},{5,7},{6,4},{7,5},{8,10},{9,11},{10,... | collective-permute-start | bytes 49160 | tf_op jit(solution)/shard_map/ppermute | solution.py:210
  103.0 1.3 collective-permute-start.9
  104.3 4.0 %collective-permute-start.8 = (f32[128,384]{0,1:T(8,128)S(1)}, f32[128,384]{0,1:T(8,128)S(1)}, u32[]{:S(2)}, u32[]{:S(2)}) collective-permute-start(f32[128,384]{0,1:T(8,128)S(1)} %get-tuple-element.25), channel_id=1, source_target_pairs={{0,1},{1,2},{2,3},{3,4},{4,5},{5,6},{6,7},{7,8},{8,9},{9,10},{10,1... | collective-permute-start | bytes 589832 | tf_op jit(solution)/shard_map/ppermute | solution.py:29
  108.3 5.6 %collective-permute-start.14 = (f32[64,128]{1,0:T(8,128)S(1)}, f32[64,128]{1,0:T(8,128)S(1)}, u32[]{:S(2)}, u32[]{:S(2)}) collective-permute-start(f32[64,128]{1,0:T(8,128)S(1)} %pad_maximum_fusion.7), channel_id=1, source_target_pairs={{0,4},{4,0},{8,12},{12,8},{1,5},{5,1},{9,13},{13,9},{2,6},{6,2},{1... | collective-permute-start | bytes 98312 | tf_op jit(solution)/shard_map/ppermute | solution.py:210
  114.0 1.8 %collective-permute-done.14 = f32[64,128]{1,0:T(8,128)S(1)} collective-permute-done((f32[64,128]{1,0:T(8,128)S(1)}, f32[64,128]{1,0:T(8,128)S(1)}, u32[]{:S(2)}, u32[]{:S(2)}) %collective-permute-start.14) | collective-permute-done | bytes 32800 | tf_op jit(solution)/shard_map/ppermute | solution.py:210
  115.9 6.1 %collective-permute-start.15 = (f32[128,128]{1,0:T(8,128)S(1)}, f32[128,128]{1,0:T(8,128)S(1)}, u32[]{:S(2)}, u32[]{:S(2)}) collective-permute-start(f32[128,128]{1,0:T(8,128)S(1)} %pad_maximum_fusion.6), channel_id=1, source_target_pairs={{0,8},{4,12},{8,0},{12,4},{1,9},{5,13},{9,1},{13,5},{2,10},{6,14},... | collective-permute-start | bytes 196616 | tf_op jit(solution)/shard_map/ppermute | solution.py:210
  122.7 9.5 %all-to-all-start.2 = ((f32[16,4,768]{2,1,0:T(4,128)}), f32[16,4,768]{2,1,0:T(4,128)S(1)}, u32[]{:S(2)}, u32[]{:S(2)}) async-start(f32[16,4,768]{2,1,0:T(4,128)} %broadcast_in_dim.147), calls=%async_computation.2 | async-start | bytes 393216 | tf_op jit(solution)/shard_map/all_to_all | solution.py:186
  133.9 10.6 %all-to-all-done.2 = f32[16,4,768]{2,1,0:T(4,128)S(1)} async-done(((f32[16,4,768]{2,1,0:T(4,128)}), f32[16,4,768]{2,1,0:T(4,128)S(1)}, u32[]{:S(2)}, u32[]{:S(2)}) %all-to-all-start.2) | async-done | bytes 196640 | tf_op jit(solution)/shard_map/all_to_all | solution.py:186
  144.5 1.9 %collective-permute-start.10 = (f32[64,768]{1,0:T(8,128)S(1)}, f32[64,768]{1,0:T(8,128)S(1)}, u32[]{:S(2)}, u32[]{:S(2)}) collective-permute-start(f32[64,768]{1,0:T(8,128)S(1)} %reshape.177), channel_id=1, source_target_pairs={{0,512},{512,0},{1,513},{513,1},{2,514},{514,2},{3,515},{515,3},{4... | collective-permute-start | bytes 589832 | tf_op jit(solution)/shard_map/ppermute | solution.py:321
  146.5 4.4 %collective-permute-done.10 = f32[64,768]{1,0:T(8,128)S(1)} collective-permute-done((f32[64,768]{1,0:T(8,128)S(1)}, f32[64,768]{1,0:T(8,128)S(1)}, u32[]{:S(2)}, u32[]{:S(2)}) %collective-permute-start.10) | collective-permute-done | bytes 196640 | tf_op jit(solution)/shard_map/ppermute | solution.py:321
  151.0 8.9 %collective-permute-start.11 = (f32[128,768]{1,0:T(8,128)S(1)}, f32[128,768]{1,0:T(8,128)S(1)}, u32[]{:S(2)}, u32[]{:S(2)}) collective-permute-start(f32[128,768]{1,0:T(8,128)S(1)} %pad_maximum_fusion.3), channel_id=1, source_target_pairs={{0,16},{16,0},{1,17},{17,1},{2,18},{18,2},{3,19},{19,3},{4,20},{20... | collective-permute-start | bytes 1179656 | tf_op jit(solution)/shard_map/ppermute | solution.py:323
  161.8 12.1 %spd_inverse.1 = f32[256,256]{1,0:T(8,128)} custom-call(f32[256,256]{1,0:T(8,128)} %pad_maximum_fusion.5.s_ref, f32[1,256]{1,0:T(1,128)} %bitcast.115), custom_call_target="tpu_custom_call" | custom-call | flops 67108864 | bytes 524288 | tf_op jit(solution)/shard_map/spd_inverse/pallas_call | solution.py:89
  173.9 1.3 fusion.36
  175.2 1.2 convolution_subtract_fusion
  (111 shorter events, 14.1 us)
Async XLA Ops:
  1.1 31.2 %collective-permute-start.2 = (f32[128,512]{0,1:T(8,128)S(1)}, f32[128,512]{0,1:T(8,128)S(1)}, u32[]{:S(2)}, u32[]{:S(2)}) collective-permute-start(f32[128,512]{0,1:T(8,128)S(1)} %copy.10), channel_id=1, source_target_pairs={{0,16},{16,32},{32,48},{48,64},{64,80},{80,96},{96,112},{112,128},... | collective-permute-start | bytes 786440 | tf_op jit(solution)/shard_map/ppermute | solution.py:29
  6.5 25.8 %collective-permute-start.3 = (f32[128,512]{0,1:T(8,128)S(1)}, f32[128,512]{0,1:T(8,128)S(1)}, u32[]{:S(2)}, u32[]{:S(2)}) collective-permute-start(f32[128,512]{0,1:T(8,128)S(1)} %copy.10), channel_id=1, source_target_pairs={{16,0},{32,16},{48,32},{64,48},{80,64},{96,80},{112,96},{128,112},... | collective-permute-start | bytes 786440 | tf_op jit(solution)/shard_map/ppermute | solution.py:31
  23.5 3.1 %copy-start.4 = (f32[8192]{0:T(1024)S(1)}, f32[8192]{0:T(1024)}, u32[]{:S(2)}) copy-start(f32[8192]{0:T(1024)} %param.9) | copy-start | bytes 98308
  23.5 3.1 %copy-start.5 = (f32[8192]{0:T(1024)S(1)}, f32[8192]{0:T(1024)}, u32[]{:S(2)}) copy-start(f32[8192]{0:T(1024)} %param.8) | copy-start | bytes 98308
  23.5 3.2 %copy-start.3 = (s32[8192]{0:T(1024)S(1)}, s32[8192]{0:T(1024)}, u32[]{:S(2)}) copy-start(s32[8192]{0:T(1024)} %param.10) | copy-start | bytes 98308
  24.6 2.1 %copy-start.2 = (s32[8192]{0:T(1024)S(1)}, s32[8192]{0:T(1024)}, u32[]{:S(2)}) copy-start(s32[8192]{0:T(1024)} %param.11) | copy-start | bytes 98308
  24.6 12.4 %collective-permute-start = (f32[128,512]{1,0:T(8,128)S(1)}, f32[128,512]{1,0:T(8,128)S(1)}, u32[]{:S(2)}, u32[]{:S(2)}) collective-permute-start(f32[128,512]{1,0:T(8,128)S(1)} %slice_select_fusion.3), channel_id=1, source_target_pairs={{0,16},{16,0},{1,17},{17,1},{2,18},{18,2},{3,19},{19,3},{4,20},{20... | collective-permute-start | bytes 786440 | tf_op jit(solution)/shard_map/ppermute | solution.py:288
  32.5 24.1 %collective-permute-start.4 = (f32[128,512]{0,1:T(8,128)S(1)}, f32[128,512]{0,1:T(8,128)S(1)}, u32[]{:S(2)}, u32[]{:S(2)}) collective-permute-start(f32[128,512]{0,1:T(8,128)S(1)} %fusion.22), channel_id=1, source_target_pairs={{0,16},{16,32},{32,48},{48,64},{64,80},{80,96},{96,112},{112,128},... | collective-permute-start | bytes 786440 | tf_op jit(solution)/shard_map/ppermute | solution.py:29
  34.4 22.2 %collective-permute-start.5 = (f32[128,512]{0,1:T(8,128)S(1)}, f32[128,512]{0,1:T(8,128)S(1)}, u32[]{:S(2)}, u32[]{:S(2)}) collective-permute-start(f32[128,512]{0,1:T(8,128)S(1)} %fusion.22), channel_id=1, source_target_pairs={{16,0},{32,16},{48,32},{64,48},{80,64},{96,80},{112,96},{128,112},... | collective-permute-start | bytes 786440 | tf_op jit(solution)/shard_map/ppermute | solution.py:31
  36.8 1.0 copy-start
  38.0 9.2 %collective-permute-start.1 = (f32[64,512]{1,0:T(8,128)S(1)}, f32[64,512]{1,0:T(8,128)S(1)}, u32[]{:S(2)}, u32[]{:S(2)}) collective-permute-start(f32[64,512]{1,0:T(8,128)S(1)} %slice_select_fusion.4), channel_id=1, source_target_pairs={{0,512},{512,0},{1,513},{513,1},{2,514},{514,2},{3,515},{515,3},{4... | collective-permute-start | bytes 393224 | tf_op jit(solution)/shard_map/ppermute | solution.py:290
  47.9 23.7 %all-to-all-start = ((f32[16,4,512]{2,1,0:T(4,128)}), f32[16,4,512]{2,1,0:T(4,128)S(1)}, u32[]{:S(2)}, u32[]{:S(2)}) async-start(f32[16,4,512]{2,1,0:T(4,128)} %reshape.166), calls=%async_computation | async-start | bytes 262144 | tf_op jit(solution)/shard_map/all_to_all | solution.py:190
  56.8 10.3 %collective-permute-start.6 = (f32[128,512]{0,1:T(8,128)S(1)}, f32[128,512]{0,1:T(8,128)S(1)}, u32[]{:S(2)}, u32[]{:S(2)}) collective-permute-start(f32[128,512]{0,1:T(8,128)S(1)} %fusion.26), channel_id=1, source_target_pairs={{0,16},{16,32},{32,48},{48,64},{64,80},{80,96},{96,112},{112,128},... | collective-permute-start | bytes 786440 | tf_op jit(solution)/shard_map/ppermute | solution.py:29
  61.5 8.5 %collective-permute-start.7 = (f32[128,512]{0,1:T(8,128)S(1)}, f32[128,512]{0,1:T(8,128)S(1)}, u32[]{:S(2)}, u32[]{:S(2)}) collective-permute-start(f32[128,512]{0,1:T(8,128)S(1)} %fusion.26), channel_id=1, source_target_pairs={{16,0},{32,16},{48,32},{64,48},{80,64},{96,80},{112,96},{128,112},... | collective-permute-start | bytes 786440 | tf_op jit(solution)/shard_map/ppermute | solution.py:31
  70.0 1.0 copy-start.1
  73.0 22.1 %all-to-all-start.1 = ((f32[16,40,128]{2,1,0:T(8,128)}), f32[16,40,128]{2,1,0:T(8,128)S(1)}, u32[]{:S(2)}, u32[]{:S(2)}) async-start(f32[16,40,128]{2,1,0:T(8,128)} %pad_maximum_fusion.4), calls=%async_computation.1 | async-start | bytes 655360 | tf_op jit(solution)/shard_map/all_to_all | solution.py:304
  95.8 4.4 %collective-permute-start.12 = (f32[16,128]{1,0:T(8,128)S(1)}, f32[16,128]{1,0:T(8,128)S(1)}, u32[]{:S(2)}, u32[]{:S(2)}) collective-permute-start(f32[16,128]{1,0:T(8,128)S(1)} %slice_reduce_fusion), channel_id=1, source_target_pairs={{0,1},{1,0},{2,3},{3,2},{4,5},{5,4},{6,7},{7,6},{8,9},{9,8},{10,11... | collective-permute-start | bytes 24584 | tf_op jit(solution)/shard_map/ppermute | solution.py:210
  100.2 8.0 %collective-permute-start.13 = (f32[32,128]{1,0:T(8,128)S(1)}, f32[32,128]{1,0:T(8,128)S(1)}, u32[]{:S(2)}, u32[]{:S(2)}) collective-permute-start(f32[32,128]{1,0:T(8,128)S(1)} %pad_maximum_fusion.9), channel_id=1, source_target_pairs={{0,2},{1,3},{2,0},{3,1},{4,6},{5,7},{6,4},{7,5},{8,10},{9,11},{10,... | collective-permute-start | bytes 49160 | tf_op jit(solution)/shard_map/ppermute | solution.py:210
  103.0 29.2 %collective-permute-start.9 = (f32[128,384]{0,1:T(8,128)S(1)}, f32[128,384]{0,1:T(8,128)S(1)}, u32[]{:S(2)}, u32[]{:S(2)}) collective-permute-start(f32[128,384]{0,1:T(8,128)S(1)} %get-tuple-element.26), channel_id=1, source_target_pairs={{1,0},{2,1},{3,2},{4,3},{5,4},{6,5},{7,6},{8,7},{9,8},{10,9},{11,1... | collective-permute-start | bytes 589832 | tf_op jit(solution)/shard_map/ppermute | solution.py:31
  104.3 28.0 %collective-permute-start.8 = (f32[128,384]{0,1:T(8,128)S(1)}, f32[128,384]{0,1:T(8,128)S(1)}, u32[]{:S(2)}, u32[]{:S(2)}) collective-permute-start(f32[128,384]{0,1:T(8,128)S(1)} %get-tuple-element.25), channel_id=1, source_target_pairs={{0,1},{1,2},{2,3},{3,4},{4,5},{5,6},{6,7},{7,8},{8,9},{9,10},{10,1... | collective-permute-start | bytes 589832 | tf_op jit(solution)/shard_map/ppermute | solution.py:29
  108.3 7.5 %collective-permute-start.14 = (f32[64,128]{1,0:T(8,128)S(1)}, f32[64,128]{1,0:T(8,128)S(1)}, u32[]{:S(2)}, u32[]{:S(2)}) collective-permute-start(f32[64,128]{1,0:T(8,128)S(1)} %pad_maximum_fusion.7), channel_id=1, source_target_pairs={{0,4},{4,0},{8,12},{12,8},{1,5},{5,1},{9,13},{13,9},{2,6},{6,2},{1... | collective-permute-start | bytes 98312 | tf_op jit(solution)/shard_map/ppermute | solution.py:210
  115.9 16.3 %collective-permute-start.15 = (f32[128,128]{1,0:T(8,128)S(1)}, f32[128,128]{1,0:T(8,128)S(1)}, u32[]{:S(2)}, u32[]{:S(2)}) collective-permute-start(f32[128,128]{1,0:T(8,128)S(1)} %pad_maximum_fusion.6), channel_id=1, source_target_pairs={{0,8},{4,12},{8,0},{12,4},{1,9},{5,13},{9,1},{13,5},{2,10},{6,14},... | collective-permute-start | bytes 196616 | tf_op jit(solution)/shard_map/ppermute | solution.py:210
  122.7 21.8 %all-to-all-start.2 = ((f32[16,4,768]{2,1,0:T(4,128)}), f32[16,4,768]{2,1,0:T(4,128)S(1)}, u32[]{:S(2)}, u32[]{:S(2)}) async-start(f32[16,4,768]{2,1,0:T(4,128)} %broadcast_in_dim.147), calls=%async_computation.2 | async-start | bytes 393216 | tf_op jit(solution)/shard_map/all_to_all | solution.py:186
  144.5 6.4 %collective-permute-start.10 = (f32[64,768]{1,0:T(8,128)S(1)}, f32[64,768]{1,0:T(8,128)S(1)}, u32[]{:S(2)}, u32[]{:S(2)}) collective-permute-start(f32[64,768]{1,0:T(8,128)S(1)} %reshape.177), channel_id=1, source_target_pairs={{0,512},{512,0},{1,513},{513,1},{2,514},{514,2},{3,515},{515,3},{4... | collective-permute-start | bytes 589832 | tf_op jit(solution)/shard_map/ppermute | solution.py:321
  151.0 10.0 %collective-permute-start.11 = (f32[128,768]{1,0:T(8,128)S(1)}, f32[128,768]{1,0:T(8,128)S(1)}, u32[]{:S(2)}, u32[]{:S(2)}) collective-permute-start(f32[128,768]{1,0:T(8,128)S(1)} %pad_maximum_fusion.3), channel_id=1, source_target_pairs={{0,16},{16,0},{1,17},{17,1},{2,18},{18,2},{3,19},{19,3},{4,20},{20... | collective-permute-start | bytes 1179656 | tf_op jit(solution)/shard_map/ppermute | solution.py:323
